TPU v7x, 512 devices: a whole 4x4x16 slice. The times are simulated.
512 devices in a mesh: src: 32 (over y_lo, z), dst: 16 (over x, y_hi, core).
Axes of the slice: x: 4, y: 4 (y_hi: 2, y_lo: 2; y = y_hi * 2 + y_lo), z: 16, core: 2. Of those that a mesh axis runs over, the one named last changes fastest.
Arguments:
- features: bfloat16 [65536, 128], P(('src', 'dst')), may hold values from -6 to 6
- weight: bfloat16 [128, 256], replicated, may hold values from -0.5 to 0.5
- bias: float32 [256], replicated, may hold values from -3 to 3
- tile_index: int32 [32, 16, 128], P('src', 'dst'), may hold values from 0 to 511, as said below
- edge_count: int32 [32, 16, 128], P('src', 'dst'), may hold values from 0 to 64, as said below
- edge_pos: int32 [32, 16, 128, 64], P('src', 'dst'), may hold values from 0 to 16383
- edge_weight: bfloat16 [32, 16, 128, 64], P('src', 'dst'), may hold values from 0.099609375 to 0.3984375
- grad_out: bfloat16 [65536, 256], P(('src', 'dst')), may hold values from -15 to 15
Outputs:
- hidden: bfloat16 [65536, 256], P(('src', 'dst'))
- input_grad: bfloat16 [65536, 128], P(('src', 'dst'))
- weight_grad: float32 [128, 256], replicated
- bias_grad: float32 [256], replicated
Inputs may be any that keep to these rules, and one draw needn't show every extreme that they name: `tile_index`: the 128 entries of one device are distinct; id c names tile row c // 16 and tile column c % 16 of the device's block of 4096 target rows and 2048 source columns. `edge_count`: on each device the live slots (count 1 or more) come first and all later slots have count 0; slot 0 is always live; some device has all 128 slots live; every device has a slot with 64 edges. `edge_pos`: row * 128 + column inside the tile; positions may repeat within a tile.
All inputs are finite; a program needn't handle non-finite values.
Results may differ from a plain program's by a relative error of at most 0.0065.
Values may be sent and summed in bfloat16 or wider, within the bound.
No kernel may reach another device: no remote copies, remote signals or barrier semaphores. Data moves between devices by JAX's collectives and lax.ppermute only.
A program may use at most 64 MiB of HBM per device.

v0:
```python
import math

import jax
import jax.numpy as jnp
from jax import lax
from jax.sharding import PartitionSpec as P

F_IN = 128
TILE = 128


def build_tiles(positions, weights, counts):
    slot_ids = lax.broadcasted_iota(jnp.int32, positions.shape, 1)
    live_mask = slot_ids < counts[:, None]
    lane_ids = lax.broadcasted_iota(jnp.int32, (1, 1, TILE), 2)
    row_hot = jnp.where(
        ((positions // TILE)[:, :, None] == lane_ids) & live_mask[:, :, None],
        weights[:, :, None],
        jnp.zeros((), jnp.bfloat16),
    )
    col_hot = jnp.where(
        (positions % TILE)[:, :, None] == lane_ids,
        jnp.ones((), jnp.bfloat16),
        jnp.zeros((), jnp.bfloat16),
    )
    summed = jnp.einsum("bei,bej->bij", row_hot, col_hot, preferred_element_type=jnp.float32)
    return summed.astype(jnp.bfloat16)


def body(features, weight, bias, tile_index, edge_count, edge_pos, edge_weight, grad_out):
    own_rows = features.shape[0]
    tile_ids = tile_index.reshape(-1)
    counts = edge_count.reshape(-1)
    slot_total = counts.shape[0]
    positions = edge_pos.reshape(slot_total, -1)
    weights = edge_weight.reshape(slot_total, -1)
    tile_block = math.gcd(slot_total, 16)
    source_rows = lax.all_gather(features, "dst", axis=0, tiled=True)
    source_tiles = source_rows.reshape(-1, TILE, F_IN)
    src_tile_total = source_tiles.shape[0]
    target_rows = own_rows * lax.axis_size("src")
    target_tile_total = target_rows // TILE
    loop_turns = slot_total // tile_block

    def block_tiles(block_index):
        block_start = block_index * tile_block
        tile_slots = lax.dynamic_slice_in_dim(tile_ids, block_start, tile_block)
        dense_tiles = build_tiles(
            lax.dynamic_slice_in_dim(positions, block_start, tile_block),
            lax.dynamic_slice_in_dim(weights, block_start, tile_block),
            lax.dynamic_slice_in_dim(counts, block_start, tile_block),
        )
        return (tile_slots // src_tile_total, tile_slots % src_tile_total, dense_tiles)

    def forward_block(block_index, running):
        target_ids, source_ids, dense_tiles = block_tiles(block_index)
        inputs = jnp.take(source_tiles, source_ids, axis=0)
        contrib = jnp.einsum(
            "bij,bjf->bif", dense_tiles, inputs, preferred_element_type=jnp.float32
        )
        return running.at[target_ids].add(contrib)

    partial_sums = lax.fori_loop(
        0, loop_turns, forward_block, jnp.zeros((target_tile_total, TILE, F_IN), jnp.float32)
    )
    aggregated = lax.psum_scatter(
        partial_sums.reshape(target_rows, F_IN), "src", scatter_dimension=0, tiled=True
    ).astype(jnp.bfloat16)
    preact = jnp.dot(aggregated, weight, preferred_element_type=jnp.float32) + bias
    hidden = jax.nn.silu(preact).astype(jnp.bfloat16)
    sigmoid_pre = jax.nn.sigmoid(preact)
    grad_pre = (
        grad_out.astype(jnp.float32) * sigmoid_pre * (1.0 + preact * (1.0 - sigmoid_pre))
    ).astype(jnp.bfloat16)
    node_total = own_rows * lax.axis_size("src") * lax.axis_size("dst")
    node_scale = 1.0 / math.sqrt(node_total)
    weight_sum, bias_sum = lax.psum(
        (
            jnp.einsum("nf,nh->fh", aggregated, grad_pre, preferred_element_type=jnp.float32),
            jnp.sum(grad_pre.astype(jnp.float32), axis=0),
        ),
        ("src", "dst"),
    )
    target_grad = lax.all_gather(grad_pre, "src", axis=0, tiled=True)
    target_back = jnp.einsum(
        "nh,fh->nf", target_grad, weight, preferred_element_type=jnp.float32
    ).astype(jnp.bfloat16)
    back_tiles = target_back.reshape(target_tile_total, TILE, F_IN)

    def backward_block(block_index, running):
        target_ids, source_ids, dense_tiles = block_tiles(block_index)
        grad_tiles = jnp.take(back_tiles, target_ids, axis=0)
        contrib = jnp.einsum(
            "bij,bif->bjf", dense_tiles, grad_tiles, preferred_element_type=jnp.float32
        )
        return running.at[source_ids].add(contrib)

    back_sums = lax.fori_loop(
        0, loop_turns, backward_block, jnp.zeros((src_tile_total, TILE, F_IN), jnp.float32)
    )
    input_grad = lax.psum_scatter(
        back_sums.reshape(-1, F_IN), "dst", scatter_dimension=0, tiled=True
    ).astype(jnp.bfloat16)
    return (hidden, input_grad, weight_sum * node_scale, bias_sum * node_scale)


def solution(mesh):
    placed = (
        P(("src", "dst"), None),
        P(),
        P(),
        P("src", "dst", None),
        P("src", "dst", None),
        P("src", "dst", None, None),
        P("src", "dst", None, None),
        P(("src", "dst"), None),
    )
    return jax.shard_map(
        body,
        mesh=mesh,
        in_specs=placed,
        out_specs=(P(("src", "dst"), None), P(("src", "dst"), None), P(), P()),
        check_vma=False,
    )
```

profile of v0, /device:TPU:1, one launch (start us, length us, event | category | flops | bytes accessed | tf_op | source)
XLA Modules:
  0.0 897.0 jit_solution(7901479414969198087)
XLA Ops:
  8.9 28.9 %all_gather.6 = bf16[2048,128]{1,0:T(8,128)(2,1)} all-gather(bf16[128,128]{1,0:T(8,128)(2,1)} %param.12), channel_id=1, replica_groups=mesh['src'=32,'dst'=16] {'dst'}, dimensions={0}, use_global_device_ids=true | all-gather | bytes 557056 | tf_op jit(solution)/shard_map/all_gather | solution.py:38
  38.1 53.7 %while.32 = (s32[]{:T(128)}, f32[32,128,128]{2,1,0:T(8,128)S(1)}, s32[128]{0:T(128)S(1)}, s32[128,64]{1,0:T(8,128)S(1)}, s32[128]{0:T(128)S(1)}, /*index=5*/bf16...) while((s32[]{:T(128)}, f32[32,128,128]{2,1,0:T(8,128)S(1)}, ...), condition=%wide.region_2.3_spmd, body=%wide.region_0.2_spmd.sunk | while | flops 102133256 | bytes 5807059 | solution.py:63
  38.2 2.4 gather_fusion
  40.8 2.2 fusion.76
  43.2 1.6 scatter_fusion
  45.0 2.4 gather_fusion
  47.6 2.2 fusion.76
  49.9 1.6 scatter_fusion
  51.7 2.4 gather_fusion
  54.3 2.2 fusion.76
  56.6 1.6 scatter_fusion
  58.4 2.4 gather_fusion
  61.0 2.2 fusion.76
  65.1 2.4 gather_fusion
  67.7 2.2 fusion.76
  71.8 2.4 gather_fusion
  74.4 2.2 fusion.76
  76.8 1.6 scatter_fusion
  78.6 2.4 gather_fusion
  81.2 2.2 fusion.76
  85.3 2.4 gather_fusion
  87.9 2.2 fusion.76
  90.2 1.6 scatter_fusion
  93.2 114.9 %reduce-scatter.3.cloned.1.call-done = f32[128,128]{1,0:T(8,128)} async-done(((f32[4096,128]{1,0:T(8,128)}), f32[128,128]{1,0:T(8,128)}) %reduce-scatter.3.cloned.1.call-update) | async-done | bytes 65552 | tf_op jit(solution)/shard_map/reduce_scatter | solution.py:66
  208.2 1.7 convert_reduce_fusion
  210.0 1.7 fusion.58
  211.8 125.2 %all-gather.2.cloned.1.call-done = bf16[4096,256]{1,0:T(8,128)(2,1)} async-done(((bf16[128,256]{1,0:T(8,128)(2,1)}), bf16[4096,256]{1,0:T(8,128)(2,1)}) %all-gather.2.cloned.1.call-update) | async-done | bytes 2097168 | tf_op jit(solution)/shard_map/all_gather | solution.py:84
  337.0 2.3 convolution_convert_fusion.2
  339.4 45.0 %while.33 = (s32[]{:T(128)}, f32[16,128,128]{2,1,0:T(8,128)S(1)}, s32[128]{0:T(128)S(1)}, s32[128,64]{1,0:T(8,128)S(1)}, s32[128]{0:T(128)S(1)}, /*index=5*/bf16...) while((s32[]{:T(128)}, f32[16,128,128]{2,1,0:T(8,128)S(1)}, ...), condition=%wide.region_6.7_spmd, body=%wide.region_4.6_spmd.sunk | while | flops 102133208 | bytes 5806991 | solution.py:98
  341.1 2.3 fusion.80
  343.4 1.6 scatter_fusion.1
  346.7 2.3 fusion.80
  349.0 1.6 scatter_fusion.1
  352.4 2.3 fusion.80
  354.6 1.6 scatter_fusion.1
  358.0 2.3 fusion.80
  360.3 1.6 scatter_fusion.1
  363.6 2.3 fusion.80
  365.9 1.6 scatter_fusion.1
  369.2 2.3 fusion.80
  371.5 1.6 scatter_fusion.1
  374.9 2.3 fusion.80
  377.1 1.6 scatter_fusion.1
  380.5 2.3 fusion.80
  382.8 1.6 scatter_fusion.1
  385.4 122.0 %psum.15 = f32[256]{0:T(256)S(1)} all-reduce(f32[256]{0:T(256)S(1)} %get-tuple-element.472), channel_id=1, replica_groups=mesh['src'=32,'dst'=16] {'src','dst'}, use_global_device_ids=true, to_apply=%region_10.11 | all-reduce | flops 256 | bytes 2048 | tf_op jit(solution)/shard_map/psum | solution.py:77
  508.0 298.5 %all-reduce.2.cloned.1.call-done = f32[128,256]{1,0:T(8,128)} async-done(((f32[128,256]{1,0:T(8,128)}), f32[128,256]{1,0:T(8,128)}) %all-reduce.2.cloned.1.call-update) | async-done | bytes 131088 | tf_op jit(solution)/shard_map/psum | solution.py:77
  808.1 81.0 %reduce-scatter.5.cloned.1.call-done = f32[128,128]{1,0:T(8,128)} async-done(((f32[2048,128]{1,0:T(8,128)}), f32[128,128]{1,0:T(8,128)}) %reduce-scatter.5.cloned.1.call-update) | async-done | bytes 65552 | tf_op jit(solution)/shard_map/reduce_scatter | solution.py:101
  (168 shorter events, 29.4 us)
Async XLA Ops:
  7.2 201.0 %copy-start = (bf16[128,256]{1,0:T(8,128)(2,1)S(1)}, bf16[128,256]{1,0:T(8,128)(2,1)}, u32[]{:S(2)}) copy-start(bf16[128,256]{1,0:T(8,128)(2,1)} %param.13) | copy-start | bytes 196612
  7.2 30.9 %copy-start.3 = (s32[1,1,128]{2,1,0:T(1,128)S(1)}, s32[1,1,128]{2,1,0:T(1,128)}, u32[]{:S(2)}) copy-start(s32[1,1,128]{2,1,0:T(1,128)} %param.15) | copy-start | bytes 1540
  7.2 30.9 %copy-start.6 = (s32[1,1,128]{2,1,0:T(1,128)S(1)}, s32[1,1,128]{2,1,0:T(1,128)}, u32[]{:S(2)}) copy-start(s32[1,1,128]{2,1,0:T(1,128)} %param.16) | copy-start | bytes 1540
  7.2 201.0 %reduce-scatter.3.cloned.1.call-start = ((), (), s32[]{:S(2)}) async-start(), calls=%async_computation.2 | async-start | bytes 2162688 | tf_op jit(solution)/shard_map/reduce_scatter | solution.py:66
  91.8 1.3 copy-start.2
  91.8 116.4 %copy-start.4 = (bf16[128,256]{1,0:T(8,128)(2,1)S(1)}, bf16[128,256]{1,0:T(8,128)(2,1)}, u32[]{:S(2)}) copy-start(bf16[128,256]{1,0:T(8,128)(2,1)} %param.19) | copy-start | bytes 196612
  91.8 116.3 %copy-start.5 = (f32[256]{0:T(256)S(1)}, f32[256]{0:T(256)}, u32[]{:S(2)}) copy-start(f32[256]{0:T(256)} %param.14) | copy-start | bytes 3076
  93.2 243.8 %all-gather.2.cloned.1.call-start = ((), (), s32[]{:S(2)}) async-start(), calls=%async_computation.3 | async-start | bytes 2162688 | tf_op jit(solution)/shard_map/all_gather | solution.py:84
  209.9 596.6 %all-reduce.2.cloned.1.call-start = ((), (), s32[]{:S(2)}) async-start(), calls=%async_computation.5 | async-start | bytes 262144 | tf_op jit(solution)/shard_map/psum | solution.py:77
  211.7 677.3 %reduce-scatter.5.cloned.1.call-start = ((), (), s32[]{:S(2)}) async-start(), calls=%async_computation.4 | async-start | bytes 1114112 | tf_op jit(solution)/shard_map/reduce_scatter | solution.py:101
  384.4 1.0 copy-start.1
Sparse Core Ops, SparseCore 0:
  93.3 114.8 reduce-scatter.2
  210.5 126.4 all-gather.1
  343.9 462.5 all-reduce.1
  811.0 77.9 reduce-scatter.4
where the time goes:
time: 899 us; the launch traced here: 897 us
  waiting for transfers between devices  620 us (69%)
  blocking collectives  151 us (17%)
  matrix products  41.9 us (5%)
  local copies, waits for them, and re-layouts  36.3 us (4%)
  other arithmetic  33.3 us (4%)
  between operations  13.9 us (2%)
    psum x1, waiting for transfers between devices, body(): lax.psum((jnp.einsum('nf,nh->fh', aggregated, grad_pre, preferred_element...  299 us
    all_gather x1, waiting for transfers between devices, body(): target_grad = lax.all_gather(grad_pre, 'src', axis=0, tiled=True)  125 us
    psum x1, blocking collectives, body(): lax.psum((jnp.einsum('nf,nh->fh', aggregated, grad_pre, preferred_element...  122 us
    reduce_scatter x1, waiting for transfers between devices, body(): lax.psum_scatter(partial_sums.reshape(target_rows, F_IN), 'src', scatter_...  115 us
    reduce_scatter x1, waiting for transfers between devices, body(): lax.psum_scatter(back_sums.reshape(-1, F_IN), 'dst', scatter_dimension=0,...  81 us
    all_gather x1, blocking collectives, body(): source_rows = lax.all_gather(features, 'dst', axis=0, tiled=True)  28.9 us
    gather x8, local copies, waits for them, and re-layouts, forward_block(): inputs = jnp.take(source_tiles, source_ids, axis=0)  19.6 us
    dot_general x8, matrix products, backward_block(): jnp.einsum('bij,bif->bjf', dense_tiles, grad_tiles, preferred_element_typ...  18.2 us
  transfers between devices with their start and end apart: 4, of which 4 were waited for; matrix products, arithmetic and copies ran while one was open for 6% of the time, Pallas kernels for 0%

commit v1 on v0

v1 whole, which is shorter than its diff:
```python
import math

import jax
import jax.numpy as jnp
from jax import lax
from jax.experimental import pallas as pl
from jax.experimental.pallas import tpu as pltpu
from jax.sharding import PartitionSpec as P

TILE = 128
BF16 = jnp.bfloat16
F32 = jnp.float32
NT = (((1,), (1,)), ((), ()))
TN = (((0,), (0,)), ((), ()))


def dot(a, b, dims=(((1,), (0,)), ((), ()))):
    return lax.dot_general(a, b, dims, preferred_element_type=F32)


def build_kernel(count_ref, pos_ref, weight_ref, tile_ref, back_ref, pos_pairs, weight_pairs):
    pairs = pos_pairs.shape[0]
    edges = pos_ref.shape[1]
    pos_pairs[...] = jnp.concatenate([pos_ref[:pairs, :], pos_ref[pairs:, :]], axis=1)
    weight_pairs[...] = jnp.concatenate(
        [weight_ref[:pairs, :].astype(F32), weight_ref[pairs:, :].astype(F32)], axis=1
    )
    lane = lax.broadcasted_iota(jnp.int32, (1, 2 * edges), 1)
    second = lane >= edges
    half = jnp.where(second, TILE, 0)
    one_rows = lax.broadcasted_iota(jnp.int32, (TILE, 2 * edges), 0)
    two_rows = lax.broadcasted_iota(jnp.int32, (2 * TILE, 2 * edges), 0)

    def one_pair(i, carry):
        limit = jnp.where(second, count_ref[i + pairs] + edges, count_ref[i])
        position = pos_pairs[pl.ds(i, 1), :]
        values = jnp.where(lane < limit, weight_pairs[pl.ds(i, 1), :], 0.0)
        row = position >> 7
        col = position & (TILE - 1)
        row_hot = jnp.where(one_rows == row, values, 0.0).astype(BF16)
        col_pair = jnp.where(two_rows == col + half, 1.0, 0.0).astype(BF16)
        tile_ref[i] = dot(row_hot, col_pair, NT).astype(BF16)
        col_hot = jnp.where(one_rows == col, 1.0, 0.0).astype(BF16)
        row_pair = jnp.where(two_rows == row + half, values, 0.0).astype(BF16)
        back_ref[i] = dot(col_hot, row_pair, NT).astype(BF16)
        return carry

    lax.fori_loop(0, pairs, one_pair, 0, unroll=2)


def forward_kernel(index_ref, tile_ref, source_ref, out_ref, sums):
    pairs = tile_ref.shape[0]
    source_tiles = source_ref.shape[0]
    shift = source_tiles.bit_length() - 1
    sums[...] = jnp.zeros_like(sums)

    def one_step(step, carry):
        found = []
        for j in range(4):
            i = step * 4 + j
            for part in range(2):
                index = index_ref[i + part * pairs]
                tile = tile_ref[i, :, part * TILE : (part + 1) * TILE]
                found.append((index >> shift, dot(tile, source_ref[index & (source_tiles - 1)])))
        for target, value in found:
            sums[target] = sums[target] + value
        return carry

    lax.fori_loop(0, pairs // 4, one_step, 0)
    out_ref[...] = sums[...].astype(BF16)


def backward_kernel(index_ref, tile_ref, recv_ref, out_ref, chunk_ref, bias_ref, sums):
    pairs = tile_ref.shape[0]
    source_tiles = out_ref.shape[0]
    shift = source_tiles.bit_length() - 1
    sums[...] = jnp.zeros_like(sums)

    def one_step(step, carry):
        found = []
        for j in range(4):
            i = step * 4 + j
            for part in range(2):
                index = index_ref[i + part * pairs]
                tile = tile_ref[i, :, part * TILE : (part + 1) * TILE]
                rows = recv_ref[index >> shift, :TILE, :]
                found.append((index & (source_tiles - 1), dot(tile, rows)))
        for source, value in found:
            sums[source] = sums[source] + value
        return carry

    lax.fori_loop(0, pairs // 4, one_step, 0)
    out_ref[...] = sums[...].astype(BF16)
    extra = jnp.sum(recv_ref[:, TILE:, :].astype(F32), axis=0)
    chunk_ref[...] = extra[0:8] + extra[8:16]
    bias_ref[...] = extra[16:24] + extra[24:32]


def dense_kernel(recv_ref, weight_ref, bias_ref, grad_ref, hidden_ref, send_ref):
    peers = recv_ref.shape[0]
    aggregated = jnp.sum(recv_ref[...].astype(F32), axis=0).astype(BF16)
    weight = weight_ref[...]
    preact = dot(aggregated, weight) + bias_ref[...]
    sigma = 1.0 / (1.0 + jnp.exp(-preact))
    hidden_ref[...] = (preact * sigma).astype(BF16)
    grad_pre = (grad_ref[...].astype(F32) * sigma * (1.0 + preact * (1.0 - sigma))).astype(BF16)
    back_rows = dot(grad_pre, weight, NT).astype(BF16)
    send_ref[:, 0:TILE, :] = jnp.broadcast_to(back_rows[None], (peers, TILE, TILE))
    weight_part = dot(aggregated, grad_pre, TN)
    chunks = jnp.concatenate(
        [weight_part[:, :TILE].reshape(peers // 2, 8, TILE), weight_part[:, TILE:].reshape(peers // 2, 8, TILE)], axis=0
    )
    chunk_high = chunks.astype(BF16)
    chunk_low = (chunks - chunk_high.astype(F32)).astype(BF16)
    bias_part = jnp.sum(grad_pre.astype(F32), axis=0, keepdims=True)
    sub = lax.broadcasted_iota(jnp.int32, (8, TILE), 0)
    bias_rows = jnp.where(sub == 0, bias_part[:, :TILE], jnp.where(sub == 1, bias_part[:, TILE:], 0.0))
    bias_high = bias_rows.astype(BF16).astype(F32)
    bias_low = bias_rows - bias_high
    bias_both = jnp.concatenate([bias_high, bias_low], axis=0).astype(BF16)
    send_ref[:, TILE : TILE + 16, :] = jnp.concatenate([chunk_high, chunk_low], axis=1)
    send_ref[:, TILE + 16 :, :] = jnp.broadcast_to(bias_both[None], (peers, 16, TILE))


def vmem(n):
    return [pl.BlockSpec(memory_space=pltpu.VMEM)] * n


def smem(n):
    return [pl.BlockSpec(memory_space=pltpu.SMEM)] * n


def body(features, weight, bias, tile_index, edge_count, edge_pos, edge_weight, grad_out):
    src = lax.axis_size("src")
    dst = lax.axis_size("dst")
    index = tile_index.reshape(-1)
    counts = edge_count.reshape(-1)
    slots = counts.shape[0]
    positions = edge_pos.reshape(slots, -1)
    weights = edge_weight.reshape(slots, -1)
    edges = positions.shape[1]
    pairs = slots // 2
    params = pltpu.CompilerParams(vmem_limit_bytes=56 << 20)

    sent = jnp.broadcast_to(features[None], (dst,) + features.shape)
    source_tiles = lax.all_to_all(sent, "dst", 0, 0, tiled=True)
    pair_shape = jax.ShapeDtypeStruct((pairs, TILE, 2 * TILE), BF16)
    tiles, back_tiles = pl.pallas_call(
        build_kernel,
        out_shape=(pair_shape, pair_shape),
        in_specs=smem(1) + vmem(2),
        out_specs=tuple(vmem(2)),
        scratch_shapes=[pltpu.VMEM((pairs, 2 * edges), jnp.int32), pltpu.VMEM((pairs, 2 * edges), F32)],
        compiler_params=params,
        name="build_tiles",
    )(counts, positions, weights)
    partial = pl.pallas_call(
        forward_kernel,
        out_shape=jax.ShapeDtypeStruct((src, TILE, TILE), BF16),
        in_specs=smem(1) + vmem(2),
        out_specs=vmem(1)[0],
        scratch_shapes=[pltpu.VMEM((src, TILE, TILE), F32)],
        compiler_params=params,
        name="forward_tiles",
    )(index, tiles, source_tiles)
    parts = lax.all_to_all(partial, "src", 0, 0, tiled=True)
    hidden, send = pl.pallas_call(
        dense_kernel,
        out_shape=(
            jax.ShapeDtypeStruct(grad_out.shape, BF16),
            jax.ShapeDtypeStruct((src, TILE + 32, TILE), BF16),
        ),
        in_specs=vmem(4),
        out_specs=tuple(vmem(2)),
        compiler_params=params,
        name="dense_layer",
    )(parts, weight, bias.reshape(1, -1), grad_out)
    received = lax.all_to_all(send, "src", 0, 0, tiled=True)
    back_partial, chunk, bias_rows = pl.pallas_call(
        backward_kernel,
        out_shape=(
            jax.ShapeDtypeStruct((dst, TILE, TILE), BF16),
            jax.ShapeDtypeStruct((8, TILE), F32),
            jax.ShapeDtypeStruct((8, TILE), F32),
        ),
        in_specs=smem(1) + vmem(2),
        out_specs=tuple(vmem(3)),
        scratch_shapes=[pltpu.VMEM((dst, TILE, TILE), F32)],
        compiler_params=params,
        name="backward_tiles",
    )(index, back_tiles, received)
    back_parts = lax.all_to_all(back_partial, "dst", 0, 0, tiled=True)
    input_grad = jnp.sum(back_parts.astype(F32), axis=0).astype(BF16)
    node_scale = 1.0 / math.sqrt(features.shape[0] * src * dst)
    both = jnp.concatenate([chunk, bias_rows], axis=0)
    both = lax.all_to_all(jnp.broadcast_to(both[None], (dst, 16, TILE)), "dst", 0, 0, tiled=True)
    both = jnp.sum(both, axis=0) * node_scale
    spread = lax.all_to_all(jnp.broadcast_to(both[None, :8], (src, 8, TILE)), "src", 0, 0, tiled=True)
    weight_grad = jnp.concatenate(
        [spread[: src // 2].reshape(TILE, TILE), spread[src // 2 :].reshape(TILE, TILE)], axis=1
    )
    bias_grad = both[8:10].reshape(-1)
    return (hidden, input_grad, weight_grad, bias_grad)


def solution(mesh):
    placed = (
        P(("src", "dst"), None),
        P(),
        P(),
        P("src", "dst", None),
        P("src", "dst", None),
        P("src", "dst", None, None),
        P("src", "dst", None, None),
        P(("src", "dst"), None),
    )
    return jax.shard_map(
        body,
        mesh=mesh,
        in_specs=placed,
        out_specs=(P(("src", "dst"), None), P(("src", "dst"), None), P(), P()),
        check_vma=False,
    )
```

time: 899 us -> 238 us (0.26)
  waiting for transfers between devices: 620 us -> 24.7 us
  matrix products: 41.9 us -> 0 us
  other arithmetic: 33.3 us -> 2.08 us
  local copies, waits for them, and re-layouts: 36.3 us -> 6.65 us
  Pallas kernels: 0 us -> 29.3 us
  starting transfers between devices: 0.16 us -> 17.8 us
  between operations: 13.9 us -> 0.67 us
    psum x1 -> x0, waiting for transfers between devices: 299 us -> none  [body(): lax.psum((jnp.einsum('nf,nh->fh', aggregated, grad_pre, preferred_element...]
    reduce_scatter x2 -> x0, waiting for transfers between devices: 196 us -> none  [the longest x1 115 us: body(): lax.psum_scatter(partial_sums.reshape(target_rows, F_IN), 'src', scatter_...]
    all_to_all x0 -> x3, blocking collectives: none -> 156 us  [the longest x1 75.2 us: body(): received = lax.all_to_all(send, 'src', 0, 0, tiled=True)]
    all_gather x1 -> x0, waiting for transfers between devices: 125 us -> none  [body(): target_grad = lax.all_gather(grad_pre, 'src', axis=0, tiled=True)]
    psum x1 -> x0, blocking collectives: 122 us -> none  [body(): lax.psum((jnp.einsum('nf,nh->fh', aggregated, grad_pre, preferred_element...]
    dot_general x19 -> x0, matrix products: 41.9 us -> none  [the longest x8 18.2 us: backward_block(): jnp.einsum('bij,bif->bjf', dense_tiles, grad_tiles, preferred_element_typ...]
    gather x16 -> x0, local copies, waits for them, and re-layouts: 30.8 us -> none  [the longest x8 19.6 us: forward_block(): inputs = jnp.take(source_tiles, source_ids, axis=0)]
    pallas_call x0 -> x4, Pallas kernels: none -> 29.3 us  [the longest x1 11.8 us: body(): pl.pallas_call(build_kernel, out_shape=(pair_shape, pair_shape), in_specs...]
  transfers between devices with their start and end apart: 4 -> 3, of which waited for: 4 -> 2; matrix products, arithmetic and copies ran while one was open for 6% -> 2% of each run, Pallas kernels for 0% -> 5%
where the time goes in v1:
time: 238 us; the launch traced here: 237 us
  blocking collectives  156 us (66%)
  Pallas kernels  29.3 us (12%)
  waiting for transfers between devices  24.7 us (10%)
  starting transfers between devices  17.8 us (7%)
  local copies, waits for them, and re-layouts  6.65 us (3%)
    all_to_all x1, blocking collectives, body(): received = lax.all_to_all(send, 'src', 0, 0, tiled=True)  75.2 us
    all_to_all x1, blocking collectives, body(): parts = lax.all_to_all(partial, 'src', 0, 0, tiled=True)  62.6 us
    all_to_all x1, blocking collectives, body(): lax.all_to_all(jnp.broadcast_to(both[None], (dst, 16, TILE)), 'dst', 0, 0...  17.9 us
    all_to_all x1, waiting for transfers between devices, body(): lax.all_to_all(jnp.broadcast_to(both[None, :8], (src, 8, TILE)), 'src', 0...  13.6 us
    pallas_call x1, Pallas kernels, body(): pl.pallas_call(build_kernel, out_shape=(pair_shape, pair_shape), in_specs...  11.8 us
    all_to_all x1, waiting for transfers between devices, body(): back_parts = lax.all_to_all(back_partial, 'dst', 0, 0, tiled=True)  11.1 us
    all_to_all x1, starting transfers between devices, body(): source_tiles = lax.all_to_all(sent, 'dst', 0, 0, tiled=True)  10.2 us
    pallas_call x1, Pallas kernels, body(): pl.pallas_call(forward_kernel, out_shape=jax.ShapeDtypeStruct((src, TILE,...  7.36 us
  transfers between devices with their start and end apart: 3, of which 2 were waited for; matrix products, arithmetic and copies ran while one was open for 2% of the time, Pallas kernels for 5%

profile of v1, /device:TPU:1, one launch (start us, length us, event | category | flops | bytes accessed | tf_op | source)
XLA Modules:
  0.0 237.0 jit_solution(2684681404079441023)
XLA Ops:
  0.6 1.7 broadcast_in_dim.6
  2.3 10.2 %all-to-all-start = ((bf16[16,128,128]{2,1,0:T(8,128)(2,1)}), bf16[16,128,128]{2,1,0:T(8,128)(2,1)S(1)}, u32[]{:S(2)}, u32[]{:S(2)}) async-start(bf16[16,128,128]{2,1,0:T(8,128)(2,1)} %broadcast_in_dim.6), calls=%async_computation | async-start | bytes 1048576 | tf_op jit(solution)/shard_map/all_to_all | solution.py:146
  12.6 1.4 copy.15
  14.0 1.5 copy.14
  15.5 11.8 %build_tiles.1 = (bf16[64,128,256]{2,1,0:T(8,128)(2,1)}, bf16[64,128,256]{2,1,0:T(8,128)(2,1)}) custom-call(s32[128]{0:T(128)} %bitcast.16, s32[128,64]{1,0:T(8,128)} %bitcast.11, bf16[128,64]{1,0:T(8,128)(2,1)} %bitcast.12), custom_call_target="tpu_custom_call" | custom-call | tf_op jit(solution)/shard_map/build_tiles/pallas_call | solution.py:148
  27.3 0.0 all-to-all-done.source_ref
  27.3 0.0 copy-start
  27.3 0.8 copy-done
  28.1 7.4 %forward_tiles.1 = bf16[32,128,128]{2,1,0:T(8,128)(2,1)} custom-call(s32[128]{0:T(128)} %bitcast.13, bf16[64,128,256]{2,1,0:T(8,128)(2,1)} %get-tuple-element.11.tile_ref, bf16[16,128,128]{2,1,0:T(8,128)(2,1)} %copy-done), custom_call_target="tpu_custom_call" | custom-call | tf_op jit(solution)/shard_map/forward_tiles/pallas_call | solution.py:157
  35.5 62.6 %all_to_all.30.recv_ref = bf16[32,128,128]{2,1,0:T(8,128)(2,1)} all-to-all(bf16[32,128,128]{2,1,0:T(8,128)(2,1)} %forward_tiles.1), channel_id=1, replica_groups=mesh['src'=32,'dst'=16] {'src'}, dimensions={0} | all-to-all | bytes 2097152 | tf_op jit(solution)/shard_map/all_to_all | solution.py:166
  98.0 2.8 %dense_layer.1 = (bf16[128,256]{1,0:T(8,128)(2,1)}, bf16[32,160,128]{2,1,0:T(8,128)(2,1)}) custom-call(bf16[32,128,128]{2,1,0:T(8,128)(2,1)} %all_to_all.30.recv_ref, bf16[128,256]{1,0:T(8,128)(2,1)} %weight_ref.1, f32[1,256]{1,0:T(1,128)} %bitcast.15, bf16[128,256]{1,0:T(8,128)(2,1)} %grad_ref.1), custom_call_target="tpu_custom_call" | custom-call | tf_op jit(solution)/shard_map/dense_layer/pallas_call | solution.py:167
  100.9 75.2 %all_to_all.31.recv_ref = bf16[32,160,128]{2,1,0:T(8,128)(2,1)} all-to-all(bf16[32,160,128]{2,1,0:T(8,128)(2,1)} %get-tuple-element.14), channel_id=1, replica_groups=mesh['src'=32,'dst'=16] {'src'}, dimensions={0} | all-to-all | bytes 2621440 | tf_op jit(solution)/shard_map/all_to_all | solution.py:178
  176.1 7.3 %backward_tiles.1 = (bf16[16,128,128]{2,1,0:T(8,128)(2,1)}, f32[8,128]{1,0:T(8,128)}, f32[8,128]{1,0:T(8,128)}) custom-call(s32[128]{0:T(128)} %bitcast.14, bf16[64,128,256]{2,1,0:T(8,128)(2,1)} %get-tuple-element.13.tile_ref, bf16[32,160,128]{2,1,0:T(8,128)(2,1)} %all_to_all.31.recv_ref), custom_call_target="tpu_custom_call" | custom-call | tf_op jit(solution)/shard_map/backward_tiles/pallas_call | solution.py:179
  183.4 0.7 pad_maximum_fusion.1
  184.1 17.9 %all_to_all.32 = f32[16,16,128]{2,1,0:T(8,128)S(1)} all-to-all(f32[16,16,128]{2,1,0:T(8,128)S(1)} %broadcast_in_dim.7), channel_id=1, replica_groups=mesh['src'=32,'dst'=16] {'dst'}, dimensions={0} | all-to-all | bytes 262144 | tf_op jit(solution)/shard_map/all_to_all | solution.py:196
  202.0 3.7 %all-to-all-start.3 = ((bf16[16,128,128]{2,1,0:T(8,128)(2,1)}), bf16[16,128,128]{2,1,0:T(8,128)(2,1)S(1)}, u32[]{:S(2)}, u32[]{:S(2)}) async-start(bf16[16,128,128]{2,1,0:T(8,128)(2,1)} %get-tuple-element.15), calls=%async_computation.3 | async-start | bytes 1048576 | tf_op jit(solution)/shard_map/all_to_all | solution.py:192
  205.8 11.1 %all-to-all-done.3 = bf16[16,128,128]{2,1,0:T(8,128)(2,1)S(1)} async-done(((bf16[16,128,128]{2,1,0:T(8,128)(2,1)}), bf16[16,128,128]{2,1,0:T(8,128)(2,1)S(1)}, u32[]{:S(2)}, u32[]{:S(2)}) %all-to-all-start.3) | async-done | bytes 524320 | tf_op jit(solution)/shard_map/all_to_all | solution.py:192
  217.0 0.7 broadcast_in_dim.8
  217.6 3.9 %all-to-all-start.5 = ((f32[32,8,128]{2,1,0:T(8,128)}), f32[32,8,128]{2,1,0:T(8,128)S(1)}, u32[]{:S(2)}, u32[]{:S(2)}) async-start(f32[32,8,128]{2,1,0:T(8,128)} %broadcast_in_dim.8), calls=%async_computation.5 | async-start | bytes 262144 | tf_op jit(solution)/shard_map/all_to_all | solution.py:198
  221.5 0.6 slice_bitcast_fusion.2
  222.1 0.7 reduce_sum.21
  222.8 13.6 %all-to-all-done.5 = f32[32,8,128]{2,1,0:T(8,128)S(1)} async-done(((f32[32,8,128]{2,1,0:T(8,128)}), f32[32,8,128]{2,1,0:T(8,128)S(1)}, u32[]{:S(2)}, u32[]{:S(2)}) %all-to-all-start.5) | async-done | bytes 131104 | tf_op jit(solution)/shard_map/all_to_all | solution.py:198
  236.3 0.7 pad_maximum_fusion
  (5 shorter events, 0.0 us)
Async XLA Ops:
  2.3 25.0 %all-to-all-start = ((bf16[16,128,128]{2,1,0:T(8,128)(2,1)}), bf16[16,128,128]{2,1,0:T(8,128)(2,1)S(1)}, u32[]{:S(2)}, u32[]{:S(2)}) async-start(bf16[16,128,128]{2,1,0:T(8,128)(2,1)} %broadcast_in_dim.6), calls=%async_computation | async-start | bytes 1048576 | tf_op jit(solution)/shard_map/all_to_all | solution.py:146
  27.3 0.8 copy-start
  202.0 14.9 %all-to-all-start.3 = ((bf16[16,128,128]{2,1,0:T(8,128)(2,1)}), bf16[16,128,128]{2,1,0:T(8,128)(2,1)S(1)}, u32[]{:S(2)}, u32[]{:S(2)}) async-start(bf16[16,128,128]{2,1,0:T(8,128)(2,1)} %get-tuple-element.15), calls=%async_computation.3 | async-start | bytes 1048576 | tf_op jit(solution)/shard_map/all_to_all | solution.py:192
  217.6 18.7 %all-to-all-start.5 = ((f32[32,8,128]{2,1,0:T(8,128)}), f32[32,8,128]{2,1,0:T(8,128)S(1)}, u32[]{:S(2)}, u32[]{:S(2)}) async-start(f32[32,8,128]{2,1,0:T(8,128)} %broadcast_in_dim.8), calls=%async_computation.5 | async-start | bytes 262144 | tf_op jit(solution)/shard_map/all_to_all | solution.py:198

commit v2 on v1

v2 whole, which is shorter than its diff:
```python
import math

import jax
import jax.numpy as jnp
from jax import lax
from jax.experimental import pallas as pl
from jax.experimental.pallas import tpu as pltpu
from jax.sharding import Mesh, PartitionSpec as P

TILE = 128
BF16 = jnp.bfloat16
F32 = jnp.float32
NN = (((1,), (0,)), ((), ()))
NT = (((1,), (1,)), ((), ()))
TN = (((0,), (0,)), ((), ()))
SRC = ("ylo", "zq", "z0")
NEAR = ("ylo", "z0")
FAR = "zq"
UNROLL = 8


def dot(a, b, dims=NN):
    return lax.dot_general(a, b, dims, preferred_element_type=F32)


def build_kernel(count_ref, pos_ref, weight_ref, tile_ref, pos_pairs, weight_pairs, *, backward):
    edges, slots = pos_ref.shape
    pairs = slots // 2
    positions = pos_ref[...].T
    weights = weight_ref[...].astype(F32).T
    pos_pairs[...] = jnp.concatenate([positions[:pairs], positions[pairs:]], axis=1)
    weight_pairs[...] = jnp.concatenate([weights[:pairs], weights[pairs:]], axis=1)
    lane = lax.broadcasted_iota(jnp.int32, (1, 2 * edges), 1)
    second = lane >= edges
    half = jnp.where(second, TILE, 0)
    one_rows = lax.broadcasted_iota(jnp.int32, (TILE, 2 * edges), 0)
    two_rows = lax.broadcasted_iota(jnp.int32, (2 * TILE, 2 * edges), 0)

    def one_pair(i, carry):
        limit = jnp.where(second, count_ref[i + pairs] + edges, count_ref[i])
        position = pos_pairs[pl.ds(i, 1), :]
        values = jnp.where(lane < limit, weight_pairs[pl.ds(i, 1), :], 0.0)
        row = position >> 7
        col = position & (TILE - 1)
        if backward:
            left = jnp.where(one_rows == col, 1.0, 0.0).astype(BF16)
            right = jnp.where(two_rows == row + half, values, 0.0).astype(BF16)
        else:
            left = jnp.where(one_rows == row, values, 0.0).astype(BF16)
            right = jnp.where(two_rows == col + half, 1.0, 0.0).astype(BF16)
        both = dot(left, right, NT).astype(BF16)
        tile_ref[i] = both[:, :TILE]
        tile_ref[i + pairs] = both[:, TILE:]
        return carry

    lax.fori_loop(0, pairs, one_pair, 0, unroll=4)


def spread_tiles(from_ref, into_ref, tile_ref, rows_ref, sums):
    sums[...] = jnp.zeros_like(sums)

    def one_step(step, carry):
        found = []
        for j in range(UNROLL):
            i = step * UNROLL + j
            found.append((into_ref[i], dot(tile_ref[i], rows_ref[from_ref[i]])))
        for target, value in found:
            sums[target] = sums[target] + value
        return carry

    lax.fori_loop(0, tile_ref.shape[0] // UNROLL, one_step, 0)


def forward_kernel(from_ref, into_ref, tile_ref, rows_ref, own_ref, *rest):
    sums = rest[-1]
    far = own_ref.shape[0]
    spread_tiles(from_ref, into_ref, tile_ref, rows_ref, sums)
    own_ref[...] = sums[:far]
    for k, out_ref in enumerate(rest[:-1]):
        out_ref[...] = sums[(k + 1) * far : (k + 2) * far].astype(BF16)


def add_kernel(own_ref, *rest):
    total = own_ref[...]
    for recv_ref in rest[:-1]:
        total = total + recv_ref[...].astype(F32)
    rest[-1][...] = total.astype(BF16)


def high_low(value):
    high = value.astype(BF16).astype(F32)
    return high, value - high


def bias_tile(bias_rows):
    return jnp.concatenate(high_low(bias_rows), axis=0).astype(BF16)


def dense_kernel(recv_ref, weight_ref, bias_ref, grad_ref, hidden_ref, send_ref):
    peers = recv_ref.shape[0]
    aggregated = jnp.sum(recv_ref[...].astype(F32), axis=0).astype(BF16)
    weight = weight_ref[...]
    preact = dot(aggregated, weight) + bias_ref[...]
    sigma = 1.0 / (1.0 + jnp.exp(-preact))
    hidden_ref[...] = (preact * sigma).astype(BF16)
    grad_pre = (grad_ref[...].astype(F32) * sigma * (1.0 + preact * (1.0 - sigma))).astype(BF16)
    back_rows = dot(grad_pre, weight, NT).astype(BF16)
    send_ref[:, :TILE, :] = jnp.broadcast_to(back_rows[None], (peers, TILE, TILE))
    part = dot(aggregated, grad_pre, TN).astype(BF16)
    rows = TILE // peers
    send_ref[:, TILE : TILE + rows, :] = part[:, :TILE].reshape(peers, rows, TILE)
    send_ref[:, TILE + rows : TILE + 2 * rows, :] = part[:, TILE:].reshape(peers, rows, TILE)
    bias_part = jnp.sum(grad_pre.astype(F32), axis=0, keepdims=True)
    sub = lax.broadcasted_iota(jnp.int32, (8, TILE), 0)
    bias_rows = jnp.where(sub == 0, bias_part[:, :TILE], jnp.where(sub == 1, bias_part[:, TILE:], 0.0))
    send_ref[:, TILE + 2 * rows :, :] = jnp.broadcast_to(bias_tile(bias_rows)[None], (peers, 16, TILE))


def middle_kernel(recv_ref, out_ref):
    peers = recv_ref.shape[0]
    top = peers * TILE
    out_ref[:top] = recv_ref[:, :TILE, :].reshape(top, TILE)
    total = jnp.sum(recv_ref[:, TILE:, :].astype(F32), axis=0)
    rows = total.shape[0] - 16
    high, low = high_low(total[:rows])
    out_ref[top : top + rows] = high.astype(BF16)
    out_ref[top + rows : top + 2 * rows] = low.astype(BF16)
    out_ref[top + 2 * rows :] = bias_tile(total[rows : rows + 8] + total[rows + 8 :])


def backward_kernel(from_ref, into_ref, tile_ref, *rest):
    near_refs, (out_ref, rows, sums) = rest[:-3], rest[-3:]
    far = rows.shape[0] // len(near_refs)
    top = far * TILE
    for k, near_ref in enumerate(near_refs):
        rows[k * far : (k + 1) * far] = near_ref[:top].reshape(far, TILE, TILE)
    spread_tiles(from_ref, into_ref, tile_ref, rows, sums)
    pieces = out_ref.shape[0]
    out_ref[:, :TILE, :] = sums[...].astype(BF16)
    total = near_refs[0][top:].astype(F32)
    for near_ref in near_refs[1:]:
        total = total + near_ref[top:].astype(F32)
    count = (total.shape[0] - 16) // 2
    chunk = (total[:count] + total[count : 2 * count]).astype(BF16)
    out_ref[:, TILE : TILE + count, :] = jnp.broadcast_to(chunk[None], (pieces, count, TILE))
    bias_rows = bias_tile(total[2 * count : 2 * count + 8] + total[2 * count + 8 :])
    out_ref[:, TILE + count :, :] = jnp.broadcast_to(bias_rows[None], (pieces, 16, TILE))


def input_kernel(recv_ref, input_ref, chunk_ref, bias_grad_ref, *, scale):
    input_ref[...] = jnp.sum(recv_ref[:, :TILE, :].astype(F32), axis=0).astype(BF16)
    total = jnp.sum(recv_ref[:, TILE:, :].astype(F32), axis=0) * scale
    count = total.shape[0] - 16
    chunk_ref[...] = jnp.broadcast_to(total[None, :count], chunk_ref.shape)
    bias_rows = total[count : count + 8] + total[count + 8 :]
    bias_grad_ref[:, :TILE] = bias_rows[0:1]
    bias_grad_ref[:, TILE:] = bias_rows[1:2]


def weight_kernel(recv_ref, weight_grad_ref):
    half = recv_ref.shape[1] // 2
    weight_grad_ref[:, :TILE] = recv_ref[:, :half, :].reshape(TILE, TILE)
    weight_grad_ref[:, TILE:] = recv_ref[:, half:, :].reshape(TILE, TILE)


def vmem(n):
    return [pl.BlockSpec(memory_space=pltpu.VMEM)] * n


def smem(n):
    return [pl.BlockSpec(memory_space=pltpu.SMEM)] * n


def call(kernel, name, outs, scalars, arrays, scratch=(), **more):
    single = not isinstance(outs, tuple)
    return pl.pallas_call(
        kernel,
        out_shape=outs,
        in_specs=smem(len(scalars)) + vmem(len(arrays)),
        out_specs=vmem(1)[0] if single else tuple(vmem(len(outs))),
        scratch_shapes=list(scratch),
        compiler_params=pltpu.CompilerParams(vmem_limit_bytes=56 << 20),
        name=name,
        **more,
    )(*scalars, *arrays)


def shape(dims, dtype):
    return jax.ShapeDtypeStruct(dims, dtype)


def swap(array, step, near):
    return lax.ppermute(array, NEAR, [(i, i ^ step) for i in range(near)])


def body(features, weight, bias, tile_index, edge_count, edge_pos, edge_weight, grad_out):
    near = lax.axis_size(NEAR)
    far = lax.axis_size(FAR)
    src = near * far
    dst = lax.axis_size("dst")
    index = tile_index.reshape(-1)
    counts = edge_count.reshape(-1)
    slots = counts.shape[0]
    positions = edge_pos.reshape(slots, -1).T
    weights = edge_weight.reshape(slots, -1).T
    edges = positions.shape[0]
    target = index // dst
    source = index % dst
    target_near = (target // (2 * far)) * 2 + target % 2
    place = (target_near ^ lax.axis_index(NEAR)) * far + (target // 2) % far
    tile_shape = shape((slots, TILE, TILE), BF16)
    block = shape((far, TILE, TILE), BF16)
    pair_scratch = (pltpu.VMEM((slots // 2, 2 * edges), jnp.int32), pltpu.VMEM((slots // 2, 2 * edges), F32))

    def build(positions, backward):
        return call(
            lambda *refs: build_kernel(*refs, backward=backward),
            "build_back" if backward else "build_tiles",
            tile_shape, (counts,), (positions, weights), pair_scratch,
        )

    sent = jnp.broadcast_to(features[None], (dst,) + features.shape)
    source_rows = lax.all_to_all(sent, "dst", 0, 0, tiled=True)
    tiles = build(positions, False)
    own, *others = call(
        forward_kernel,
        "forward_tiles",
        (shape(block.shape, F32),) + (block,) * (near - 1),
        (source, place),
        (tiles, source_rows),
        (pltpu.VMEM((src, TILE, TILE), F32),),
    )
    others = [swap(other, k + 1, near) for k, other in enumerate(others)]
    late_positions, own = lax.optimization_barrier((positions, own))
    back_tiles = build(late_positions, True)
    near_sums = call(add_kernel, "add_near", block, (), (own, *others))
    near_sums, back_tiles = lax.optimization_barrier((near_sums, back_tiles))
    parts = lax.all_to_all(near_sums, FAR, 0, 0, tiled=True)
    extra = 2 * TILE // far + 16
    hidden, send = call(
        dense_kernel,
        "dense_layer",
        (shape(grad_out.shape, BF16), shape((far, TILE + extra, TILE), BF16)),
        (),
        (parts, weight, bias.reshape(1, -1), grad_out),
    )
    far_rows = lax.all_to_all(send, FAR, 0, 0, tiled=True)
    near_rows = call(
        middle_kernel, "middle_sums", shape((far * TILE + 2 * extra - 16, TILE), BF16), (), (far_rows,)
    )
    near_all = [near_rows] + [swap(near_rows, k, near) for k in range(1, near)]
    back_send = call(
        backward_kernel,
        "backward_tiles",
        shape((dst, TILE + extra, TILE), BF16),
        (place, source),
        (back_tiles, *near_all),
        (pltpu.VMEM((src, TILE, TILE), BF16), pltpu.VMEM((dst, TILE, TILE), F32)),
    )
    received = lax.all_to_all(back_send, "dst", 0, 0, tiled=True)
    node_scale = 1.0 / math.sqrt(features.shape[0] * src * dst)
    input_grad, chunks, bias_grad = call(
        lambda *refs: input_kernel(*refs, scale=node_scale),
        "input_sums",
        (shape(features.shape, BF16), shape((far, extra - 16, TILE), F32), shape((1, 2 * TILE), F32)),
        (),
        (received,),
    )
    chunks = lax.all_to_all(chunks, FAR, 0, 0, tiled=True)
    weight_grad = call(weight_kernel, "weight_rows", shape((TILE, 2 * TILE), F32), (), (chunks,))
    return (hidden, input_grad, weight_grad, bias_grad.reshape(-1))


def solution(mesh):
    src, dst = mesh.devices.shape
    fine = Mesh(mesh.devices.reshape(2, src // 4, 2, dst), ("ylo", "zq", "z0", "dst"))
    rows = P(("ylo", "zq", "z0", "dst"), None)
    placed = (
        rows,
        P(),
        P(),
        P(SRC, "dst", None),
        P(SRC, "dst", None),
        P(SRC, "dst", None, None),
        P(SRC, "dst", None, None),
        rows,
    )
    return jax.shard_map(
        body, mesh=fine, in_specs=placed, out_specs=(rows, rows, P(), P()), check_vma=False
    )
```

time: 238 us -> 185 us (0.78)
  blocking collectives: 156 us -> 101 us
  waiting for transfers between devices: 24.7 us -> 11.8 us
  starting transfers between devices: 17.8 us -> 27 us
  Pallas kernels: 29.3 us -> 37.5 us
    all_to_all x3 -> x4, blocking collectives: 156 us -> 101 us  [the longest x1 31.2 us: body(): parts = lax.all_to_all(near_sums, FAR, 0, 0, tiled=True)]
    all_to_all x3 -> x1, waiting for transfers between devices: 24.7 us -> 3.94 us  [body(): source_rows = lax.all_to_all(sent, 'dst', 0, 0, tiled=True)]
    ppermute x0 -> x6, starting transfers between devices: none -> 16.7 us  [swap(): return lax.ppermute(array, NEAR, [(i, i ^ step) for i in range(near)])]
    pallas_call x4 -> x9, Pallas kernels: 29.3 us -> 37.5 us  [call(): pl.pallas_call(kernel, out_shape=outs, in_specs=smem(len(scalars)) + vmem...]
    ppermute x0 -> x6, waiting for transfers between devices: none -> 7.9 us  [swap(): return lax.ppermute(array, NEAR, [(i, i ^ step) for i in range(near)])]
    all_to_all x3 -> x1, starting transfers between devices: 17.8 us -> 10.2 us  [body(): source_rows = lax.all_to_all(sent, 'dst', 0, 0, tiled=True)]
  transfers between devices with their start and end apart: 3 -> 7, of which waited for: 2 -> 5; matrix products, arithmetic and copies ran while one was open for 2% -> 0% of each run, Pallas kernels for 5% -> 7%
where the time goes in v2:
time: 185 us; the launch traced here: 184 us
  blocking collectives  101 us (55%)
  Pallas kernels  37.5 us (20%)
  starting transfers between devices  27 us (15%)
  waiting for transfers between devices  11.8 us (6%)
  local copies, waits for them, and re-layouts  4.6 us (2%)
    pallas_call x9, Pallas kernels, call(): pl.pallas_call(kernel, out_shape=outs, in_specs=smem(len(scalars)) + vmem...  37.5 us
    all_to_all x1, blocking collectives, body(): parts = lax.all_to_all(near_sums, FAR, 0, 0, tiled=True)  31.2 us
    all_to_all x1, blocking collectives, body(): far_rows = lax.all_to_all(send, FAR, 0, 0, tiled=True)  26.1 us
    all_to_all x1, blocking collectives, body(): received = lax.all_to_all(back_send, 'dst', 0, 0, tiled=True)  25.7 us
    all_to_all x1, blocking collectives, body(): chunks = lax.all_to_all(chunks, FAR, 0, 0, tiled=True)  18.3 us
    ppermute x6, starting transfers between devices, swap(): return lax.ppermute(array, NEAR, [(i, i ^ step) for i in range(near)])  16.7 us
    all_to_all x1, starting transfers between devices, body(): source_rows = lax.all_to_all(sent, 'dst', 0, 0, tiled=True)  10.2 us
    ppermute x6, waiting for transfers between devices, swap(): return lax.ppermute(array, NEAR, [(i, i ^ step) for i in range(near)])  7.9 us
  transfers between devices with their start and end apart: 7, of which 5 were waited for; matrix products, arithmetic and copies ran while one was open for 0% of the time, Pallas kernels for 7%

profile of v2, /device:TPU:1, one launch (start us, length us, event | category | flops | bytes accessed | tf_op | source)
XLA Modules:
  0.0 183.5 jit_solution(4520817199465869551)
XLA Ops:
  0.6 0.0 copy-start.7
  0.6 1.7 broadcast_in_dim.2
  2.3 10.2 %all-to-all-start = ((bf16[16,128,128]{2,1,0:T(8,128)(2,1)}), bf16[16,128,128]{2,1,0:T(8,128)(2,1)S(1)}, u32[]{:S(2)}, u32[]{:S(2)}) async-start(bf16[16,128,128]{2,1,0:T(8,128)(2,1)} %broadcast_in_dim.2), calls=%async_computation | async-start | bytes 1048576 | tf_op jit(solution)/shard_map/all_to_all | solution.py:223
  12.5 6.7 %build_tiles.1.tile_ref = bf16[128,128,128]{2,1,0:T(8,128)(2,1)} custom-call(s32[128]{0:T(128)} %bitcast.30, s32[64,128]{1,0:T(8,128)} %bitcast.26, bf16[64,128]{1,0:T(8,128)(2,1)} %bitcast.28), custom_call_target="tpu_custom_call" | custom-call | tf_op jit(solution)/shard_map/build_tiles/pallas_call | solution.py:176
  19.2 0.0 copy-done.7
  19.2 0.5 fusion.1
  19.8 3.9 %all-to-all-done.rows_ref = bf16[16,128,128]{2,1,0:T(8,128)(2,1)S(1)} async-done(((bf16[16,128,128]{2,1,0:T(8,128)(2,1)}), bf16[16,128,128]{2,1,0:T(8,128)(2,1)S(1)}, u32[]{:S(2)}, u32[]{:S(2)}) %all-to-all-start) | async-done | bytes 524320 | tf_op jit(solution)/shard_map/all_to_all | solution.py:223
  23.7 0.0 copy-start
  23.7 0.8 copy-done
  24.5 7.3 %forward_tiles.1 = (f32[8,128,128]{2,1,0:T(8,128)}, bf16[8,128,128]{2,1,0:T(8,128)(2,1)}, bf16[8,128,128]{2,1,0:T(8,128)(2,1)}, bf16[8,128,128]{2,1,0:T(8,128)(2,1)}) custom-call(s32[128]{0:T(128)} %get-tuple-element.31.from_ref.into_ref, s32[128]{0:T(128)} %get-tuple-element.30.into_ref.from_ref, bf16[128,128,128]{2,1,0:T(8,128)(2,1)} %build_tiles.1.tile_ref, ...), custom_call_target="tpu_custom_call" | custom-call | tf_op jit(solution)/shard_map/forward_tiles/pallas_call | solution.py:176
  31.9 1.9 %collective-permute-start = (bf16[8,128,128]{2,1,0:T(8,128)(2,1)}, bf16[8,128,128]{2,1,0:T(8,128)(2,1)S(1)}, u32[]{:S(2)}, u32[]{:S(2)}) collective-permute-start(bf16[8,128,128]{2,1,0:T(8,128)(2,1)} %get-tuple-element.19), channel_id=1, source_target_pairs={{0,16},{16,0},{256,272},{272,256},{1,17},{17,1},{257,273},{273,257... | collective-permute-start | bytes 786440 | tf_op jit(solution)/shard_map/ppermute | solution.py:193
  33.8 2.1 %collective-permute-start.1 = (bf16[8,128,128]{2,1,0:T(8,128)(2,1)}, bf16[8,128,128]{2,1,0:T(8,128)(2,1)S(1)}, u32[]{:S(2)}, u32[]{:S(2)}) collective-permute-start(bf16[8,128,128]{2,1,0:T(8,128)(2,1)} %get-tuple-element.20), channel_id=1, source_target_pairs={{0,256},{16,272},{256,0},{272,16},{1,257},{17,273},{257,1},{273,17... | collective-permute-start | bytes 786440 | tf_op jit(solution)/shard_map/ppermute | solution.py:193
  35.9 4.4 %collective-permute-start.2 = (bf16[8,128,128]{2,1,0:T(8,128)(2,1)}, bf16[8,128,128]{2,1,0:T(8,128)(2,1)S(1)}, u32[]{:S(2)}, u32[]{:S(2)}) collective-permute-start(bf16[8,128,128]{2,1,0:T(8,128)(2,1)} %get-tuple-element.21), channel_id=1, source_target_pairs={{0,272},{16,256},{256,16},{272,0},{1,273},{17,257},{257,17},{273,1... | collective-permute-start | bytes 786440 | tf_op jit(solution)/shard_map/ppermute | solution.py:193
  40.3 6.8 %build_back.1.tile_ref = bf16[128,128,128]{2,1,0:T(8,128)(2,1)} custom-call(s32[128]{0:T(128)} %bitcast.31, s32[64,128]{1,0:T(8,128)} %bitcast.27, bf16[64,128]{1,0:T(8,128)(2,1)} %bitcast.29), custom_call_target="tpu_custom_call" | custom-call | tf_op jit(solution)/shard_map/build_back/pallas_call | solution.py:176
  47.0 0.0 collective-permute-done.rest_0_
  47.0 0.0 copy-start.4
  47.0 0.9 collective-permute-done.1.rest_1_
  47.9 0.0 copy-start.5
  47.9 0.0 collective-permute-done.2.rest_2_
  47.9 0.0 copy-done.4
  47.9 0.7 copy-done.5
  48.6 0.0 copy-start.6
  48.6 0.7 copy-done.6
  49.3 2.1 %add_near.1 = bf16[8,128,128]{2,1,0:T(8,128)(2,1)} custom-call(f32[8,128,128]{2,1,0:T(8,128)} %get-tuple-element.18.own_ref, bf16[8,128,128]{2,1,0:T(8,128)(2,1)} %copy-done.4, bf16[8,128,128]{2,1,0:T(8,128)(2,1)} %copy-done.5, bf16[8,128,128]{2,1,0:T(8,128)(2,1)} %copy-done.6), custom_call_target="tpu_custom_call" | custom-call | tf_op jit(solution)/shard_map/add_near/pallas_call | solution.py:176
  51.4 31.2 %all_to_all.25.recv_ref = bf16[8,128,128]{2,1,0:T(8,128)(2,1)} all-to-all(bf16[8,128,128]{2,1,0:T(8,128)(2,1)} %add_near.1), channel_id=1, replica_groups=mesh['ylo'=2,'zq'=8,'z0'=2,'dst'=16] {'zq'}, dimensions={0} | all-to-all | bytes 524288 | tf_op jit(solution)/shard_map/all_to_all | solution.py:238
  82.6 2.1 %dense_layer.1 = (bf16[128,256]{1,0:T(8,128)(2,1)}, bf16[8,176,128]{2,1,0:T(8,128)(2,1)}) custom-call(bf16[8,128,128]{2,1,0:T(8,128)(2,1)} %all_to_all.25.recv_ref, bf16[128,256]{1,0:T(8,128)(2,1)} %weight_ref.1, f32[1,256]{1,0:T(1,128)} %bitcast.32, bf16[128,256]{1,0:T(8,128)(2,1)} %grad_ref.1), custom_call_target="tpu_custom_call" | custom-call | tf_op jit(solution)/shard_map/dense_layer/pallas_call | solution.py:176
  84.7 26.1 %all_to_all.26.recv_ref = bf16[8,176,128]{2,1,0:T(8,128)(2,1)} all-to-all(bf16[8,176,128]{2,1,0:T(8,128)(2,1)} %get-tuple-element.26), channel_id=1, replica_groups=mesh['ylo'=2,'zq'=8,'z0'=2,'dst'=16] {'zq'}, dimensions={0} | all-to-all | bytes 720896 | tf_op jit(solution)/shard_map/all_to_all | solution.py:247
  110.8 1.7 middle_sums.1.rest_0_
  112.6 1.9 %collective-permute-start.5 = (bf16[1104,128]{1,0:T(8,128)(2,1)}, bf16[1104,128]{1,0:T(8,128)(2,1)S(1)}, u32[]{:S(2)}, u32[]{:S(2)}) collective-permute-start(bf16[1104,128]{1,0:T(8,128)(2,1)} %middle_sums.1.rest_0_), channel_id=1, source_target_pairs={{0,272},{16,256},{256,16},{272,0},{1,273},{17,257},{257,17},{273,1... | collective-permute-start | bytes 847880 | tf_op jit(solution)/shard_map/ppermute | solution.py:193
  114.5 1.9 %collective-permute-start.4 = (bf16[1104,128]{1,0:T(8,128)(2,1)}, bf16[1104,128]{1,0:T(8,128)(2,1)S(1)}, u32[]{:S(2)}, u32[]{:S(2)}) collective-permute-start(bf16[1104,128]{1,0:T(8,128)(2,1)} %middle_sums.1.rest_0_), channel_id=1, source_target_pairs={{0,256},{16,272},{256,0},{272,16},{1,257},{17,273},{257,1},{273,17... | collective-permute-start | bytes 847880 | tf_op jit(solution)/shard_map/ppermute | solution.py:193
  116.4 4.5 %collective-permute-start.3 = (bf16[1104,128]{1,0:T(8,128)(2,1)}, bf16[1104,128]{1,0:T(8,128)(2,1)S(1)}, u32[]{:S(2)}, u32[]{:S(2)}) collective-permute-start(bf16[1104,128]{1,0:T(8,128)(2,1)} %middle_sums.1.rest_0_), channel_id=1, source_target_pairs={{0,16},{16,0},{256,272},{272,256},{1,17},{17,1},{257,273},{273,257... | collective-permute-start | bytes 847880 | tf_op jit(solution)/shard_map/ppermute | solution.py:193
  121.0 0.2 collective-permute-done.5.rest_3_
  121.1 0.0 copy-start.1
  121.1 3.5 %collective-permute-done.4.rest_2_ = bf16[1104,128]{1,0:T(8,128)(2,1)S(1)} collective-permute-done((bf16[1104,128]{1,0:T(8,128)(2,1)}, bf16[1104,128]{1,0:T(8,128)(2,1)S(1)}, u32[]{:S(2)}, u32[]{:S(2)}) %collective-permute-start.4) | collective-permute-done | bytes 282656 | tf_op jit(solution)/shard_map/ppermute | solution.py:193
  124.6 0.0 copy-start.2
  124.6 3.4 %collective-permute-done.3.rest_1_ = bf16[1104,128]{1,0:T(8,128)(2,1)S(1)} collective-permute-done((bf16[1104,128]{1,0:T(8,128)(2,1)}, bf16[1104,128]{1,0:T(8,128)(2,1)S(1)}, u32[]{:S(2)}, u32[]{:S(2)}) %collective-permute-start.3) | collective-permute-done | bytes 282656 | tf_op jit(solution)/shard_map/ppermute | solution.py:193
  128.0 0.0 copy-done.1
  128.0 0.0 copy-done.2
  128.0 0.0 copy-start.3
  128.0 0.7 copy-done.3
  128.7 7.3 %backward_tiles.1 = bf16[16,176,128]{2,1,0:T(8,128)(2,1)} custom-call(s32[128]{0:T(128)} %get-tuple-element.30.into_ref.from_ref, s32[128]{0:T(128)} %get-tuple-element.31.from_ref.into_ref, bf16[128,128,128]{2,1,0:T(8,128)(2,1)} %build_back.1.tile_ref, bf16[1104,128]{1,0:T(8,128)(2,1)} %middle_sums.1.rest_0_, bf16[1104,128]{1,0:T(8,128)(2,1)} %copy-done.3, ...), custom_call_target="tpu_custom_call" | custom-call | tf_op jit(solution)/shard_map/backward_tiles/pallas_call | solution.py:176
  136.1 25.7 %all_to_all.27.refs_0_ = bf16[16,176,128]{2,1,0:T(8,128)(2,1)} all-to-all(bf16[16,176,128]{2,1,0:T(8,128)(2,1)} %backward_tiles.1), channel_id=1, replica_groups=mesh['ylo'=2,'zq'=8,'z0'=2,'dst'=16] {'dst'}, dimensions={0} | all-to-all | bytes 1441792 | tf_op jit(solution)/shard_map/all_to_all | solution.py:260
  161.8 1.8 input_sums.1
  163.6 18.3 %all_to_all.28.recv_ref = f32[8,32,128]{2,1,0:T(8,128)} all-to-all(f32[8,32,128]{2,1,0:T(8,128)} %get-tuple-element.28), channel_id=1, replica_groups=mesh['ylo'=2,'zq'=8,'z0'=2,'dst'=16] {'zq'}, dimensions={0} | all-to-all | bytes 262144 | tf_op jit(solution)/shard_map/all_to_all | solution.py:269
  181.9 1.6 weight_rows.1
Async XLA Ops:
  0.6 18.6 %copy-start.7 = (s32[1,1,128]{2,1,0:T(1,128)S(1)}, s32[1,1,128]{2,1,0:T(1,128)}, u32[]{:S(2)}) copy-start(s32[1,1,128]{2,1,0:T(1,128)} %param.11) | copy-start | bytes 1540
  2.3 21.4 %all-to-all-start = ((bf16[16,128,128]{2,1,0:T(8,128)(2,1)}), bf16[16,128,128]{2,1,0:T(8,128)(2,1)S(1)}, u32[]{:S(2)}, u32[]{:S(2)}) async-start(bf16[16,128,128]{2,1,0:T(8,128)(2,1)} %broadcast_in_dim.2), calls=%async_computation | async-start | bytes 1048576 | tf_op jit(solution)/shard_map/all_to_all | solution.py:223
  23.7 0.8 copy-start
  31.9 15.2 %collective-permute-start = (bf16[8,128,128]{2,1,0:T(8,128)(2,1)}, bf16[8,128,128]{2,1,0:T(8,128)(2,1)S(1)}, u32[]{:S(2)}, u32[]{:S(2)}) collective-permute-start(bf16[8,128,128]{2,1,0:T(8,128)(2,1)} %get-tuple-element.19), channel_id=1, source_target_pairs={{0,16},{16,0},{256,272},{272,256},{1,17},{17,1},{257,273},{273,257... | collective-permute-start | bytes 786440 | tf_op jit(solution)/shard_map/ppermute | solution.py:193
  33.8 14.1 %collective-permute-start.1 = (bf16[8,128,128]{2,1,0:T(8,128)(2,1)}, bf16[8,128,128]{2,1,0:T(8,128)(2,1)S(1)}, u32[]{:S(2)}, u32[]{:S(2)}) collective-permute-start(bf16[8,128,128]{2,1,0:T(8,128)(2,1)} %get-tuple-element.20), channel_id=1, source_target_pairs={{0,256},{16,272},{256,0},{272,16},{1,257},{17,273},{257,1},{273,17... | collective-permute-start | bytes 786440 | tf_op jit(solution)/shard_map/ppermute | solution.py:193
  35.9 12.1 %collective-permute-start.2 = (bf16[8,128,128]{2,1,0:T(8,128)(2,1)}, bf16[8,128,128]{2,1,0:T(8,128)(2,1)S(1)}, u32[]{:S(2)}, u32[]{:S(2)}) collective-permute-start(bf16[8,128,128]{2,1,0:T(8,128)(2,1)} %get-tuple-element.21), channel_id=1, source_target_pairs={{0,272},{16,256},{256,16},{272,0},{1,273},{17,257},{257,17},{273,1... | collective-permute-start | bytes 786440 | tf_op jit(solution)/shard_map/ppermute | solution.py:193
  47.0 0.9 copy-start.4
  47.9 0.7 copy-start.5
  48.6 0.7 copy-start.6
  112.6 8.5 %collective-permute-start.5 = (bf16[1104,128]{1,0:T(8,128)(2,1)}, bf16[1104,128]{1,0:T(8,128)(2,1)S(1)}, u32[]{:S(2)}, u32[]{:S(2)}) collective-permute-start(bf16[1104,128]{1,0:T(8,128)(2,1)} %middle_sums.1.rest_0_), channel_id=1, source_target_pairs={{0,272},{16,256},{256,16},{272,0},{1,273},{17,257},{257,17},{273,1... | collective-permute-start | bytes 847880 | tf_op jit(solution)/shard_map/ppermute | solution.py:193
  114.5 10.1 %collective-permute-start.4 = (bf16[1104,128]{1,0:T(8,128)(2,1)}, bf16[1104,128]{1,0:T(8,128)(2,1)S(1)}, u32[]{:S(2)}, u32[]{:S(2)}) collective-permute-start(bf16[1104,128]{1,0:T(8,128)(2,1)} %middle_sums.1.rest_0_), channel_id=1, source_target_pairs={{0,256},{16,272},{256,0},{272,16},{1,257},{17,273},{257,1},{273,17... | collective-permute-start | bytes 847880 | tf_op jit(solution)/shard_map/ppermute | solution.py:193
  116.4 11.5 %collective-permute-start.3 = (bf16[1104,128]{1,0:T(8,128)(2,1)}, bf16[1104,128]{1,0:T(8,128)(2,1)S(1)}, u32[]{:S(2)}, u32[]{:S(2)}) collective-permute-start(bf16[1104,128]{1,0:T(8,128)(2,1)} %middle_sums.1.rest_0_), channel_id=1, source_target_pairs={{0,16},{16,0},{256,272},{272,256},{1,17},{17,1},{257,273},{273,257... | collective-permute-start | bytes 847880 | tf_op jit(solution)/shard_map/ppermute | solution.py:193
  121.1 6.9 %copy-start.1 = (bf16[1104,128]{1,0:T(8,128)(2,1)}, bf16[1104,128]{1,0:T(8,128)(2,1)S(1)}, u32[]{:S(2)}) copy-start(bf16[1104,128]{1,0:T(8,128)(2,1)S(1)} %collective-permute-done.5.rest_3_) | copy-start | bytes 847876
  124.6 3.4 %copy-start.2 = (bf16[1104,128]{1,0:T(8,128)(2,1)}, bf16[1104,128]{1,0:T(8,128)(2,1)S(1)}, u32[]{:S(2)}) copy-start(bf16[1104,128]{1,0:T(8,128)(2,1)S(1)} %collective-permute-done.4.rest_2_) | copy-start | bytes 847876
  128.0 0.7 copy-start.3

commit v3 on v2

v3 whole, which is shorter than its diff:
```python
import math

import jax
import jax.numpy as jnp
from jax import lax
from jax.experimental import pallas as pl
from jax.experimental.pallas import tpu as pltpu
from jax.sharding import Mesh, PartitionSpec as P

TILE = 128
BF16 = jnp.bfloat16
F32 = jnp.float32
NN = (((1,), (0,)), ((), ()))
NT = (((1,), (1,)), ((), ()))
TN = (((0,), (0,)), ((), ()))
SRC = ("ylo", "zq", "z0")
DST = ("x", "d0")
NEAR = ("ylo", "z0")
FAR = "zq"
UNROLL = 8


def dot(a, b, dims=NN):
    return lax.dot_general(a, b, dims, preferred_element_type=F32)


def build_kernel(count_ref, pos_ref, weight_ref, tile_ref, pos_pairs, weight_pairs, *, backward):
    edges, slots = pos_ref.shape
    pairs = slots // 2
    positions = pos_ref[...].T
    weights = weight_ref[...].astype(F32).T
    pos_pairs[...] = jnp.concatenate([positions[:pairs], positions[pairs:]], axis=1)
    weight_pairs[...] = jnp.concatenate([weights[:pairs], weights[pairs:]], axis=1)
    lane = lax.broadcasted_iota(jnp.int32, (1, 2 * edges), 1)
    second = lane >= edges
    half = jnp.where(second, TILE, 0)
    one_rows = lax.broadcasted_iota(jnp.int32, (TILE, 2 * edges), 0)
    two_rows = lax.broadcasted_iota(jnp.int32, (2 * TILE, 2 * edges), 0)

    def one_pair(i, carry):
        limit = jnp.where(second, count_ref[i + pairs] + edges, count_ref[i])
        position = pos_pairs[pl.ds(i, 1), :]
        values = jnp.where(lane < limit, weight_pairs[pl.ds(i, 1), :], 0.0)
        row = position >> 7
        col = position & (TILE - 1)
        if backward:
            left = jnp.where(one_rows == col, 1.0, 0.0).astype(BF16)
            right = jnp.where(two_rows == row + half, values, 0.0).astype(BF16)
        else:
            left = jnp.where(one_rows == row, values, 0.0).astype(BF16)
            right = jnp.where(two_rows == col + half, 1.0, 0.0).astype(BF16)
        both = dot(left, right, NT).astype(BF16)
        tile_ref[i] = both[:, :TILE]
        tile_ref[i + pairs] = both[:, TILE:]
        return carry

    lax.fori_loop(0, pairs, one_pair, 0, unroll=4)


def spread_tiles(from_ref, into_ref, tile_ref, rows_ref, sums):
    block = tile_ref.shape[0]
    base = pl.program_id(0) * block
    for start in range(0, block, UNROLL):
        found = []
        for i in range(start, start + UNROLL):
            found.append((into_ref[base + i], dot(tile_ref[i], rows_ref[from_ref[base + i]])))
        for target, value in found:
            sums[target] = sums[target] + value


def forward_kernel(from_ref, into_ref, tile_ref, rows_ref, own_ref, *rest):
    sums = rest[-1]
    far = own_ref.shape[0]
    step = pl.program_id(0)

    @pl.when(step == 0)
    def _():
        sums[...] = jnp.zeros_like(sums)

    spread_tiles(from_ref, into_ref, tile_ref, rows_ref, sums)

    @pl.when(step == pl.num_programs(0) - 1)
    def _():
        own_ref[...] = sums[:far]
        for k, out_ref in enumerate(rest[:-1]):
            out_ref[...] = sums[(k + 1) * far : (k + 2) * far].astype(BF16)


def add_kernel(own_ref, *rest):
    total = own_ref[...]
    for recv_ref in rest[:-1]:
        total = total + recv_ref[...].astype(F32)
    rest[-1][...] = total.astype(BF16)


def high_low(value):
    high = value.astype(BF16).astype(F32)
    return high, value - high


def dense_kernel(recv_ref, weight_ref, bias_ref, grad_ref, hidden_ref, send_ref, agg_ref, grad_pre_ref):
    aggregated = jnp.sum(recv_ref[...].astype(F32), axis=0).astype(BF16)
    agg_ref[...] = aggregated
    weight = weight_ref[...]
    preact = dot(aggregated, weight) + bias_ref[...]
    sigma = 1.0 / (1.0 + jnp.exp(-preact))
    hidden_ref[...] = (preact * sigma).astype(BF16)
    grad_pre = (grad_ref[...].astype(F32) * sigma * (1.0 + preact * (1.0 - sigma))).astype(BF16)
    grad_pre_ref[...] = grad_pre
    back_rows = dot(grad_pre, weight, NT).astype(BF16)
    send_ref[...] = jnp.broadcast_to(back_rows[None], send_ref.shape)


def grad_kernel(place_ref, agg_ref, grad_pre_ref, *rest):
    outs, flat = rest[:-1], rest[-1]
    grad_pre = grad_pre_ref[...]
    part = dot(agg_ref[...], grad_pre, TN)
    flat[:TILE] = part[:, :TILE]
    flat[TILE:] = part[:, TILE:]
    bias_part = jnp.sum(grad_pre.astype(F32), axis=0, keepdims=True)
    sub = lax.broadcasted_iota(jnp.int32, (8, TILE), 0)
    bias_rows = jnp.where(sub == 0, bias_part[:, :TILE], jnp.where(sub == 1, bias_part[:, TILE:], 0.0))
    split_rows(place_ref[0], flat, bias_rows, outs)


def split_rows(place, flat, bias_rows, outs):
    size = outs[0].shape[0] - 8
    for k, out_ref in enumerate(outs):
        out_ref[:size] = flat[pl.ds(pl.multiple_of((place ^ k) * size, 8), size), :]
        out_ref[size:] = bias_rows


def add_parts(parts):
    total = parts[0][...]
    for part_ref in parts[1:]:
        total = total + part_ref[...]
    return total


def regrad_kernel(place_ref, *rest):
    flat = rest[-1]
    parts, outs = rest[: (len(rest) - 1) // 2], rest[(len(rest) - 1) // 2 : -1]
    total = add_parts(parts)
    size = total.shape[0] - 8
    flat[...] = total[:size]
    split_rows(place_ref[0], flat, total[size:], outs)


def share_kernel(*rest):
    out_ref = rest[-1]
    total = add_parts(rest[:-1])
    size = total.shape[0] - 8
    rows = jnp.concatenate([total[:size], bias_tile(total[size:])], axis=0).astype(BF16)
    out_ref[...] = jnp.broadcast_to(rows[None], out_ref.shape)


def bias_tile(bias_rows):
    high, low = high_low(bias_rows)
    return high + jnp.concatenate([jnp.zeros((2, TILE), F32), low[0:2], jnp.zeros((4, TILE), F32)], axis=0)


def backward_kernel(from_ref, into_ref, tile_ref, *rest):
    near_refs, (out_ref, rows, sums) = rest[:-3], rest[-3:]
    far = near_refs[0].shape[0]
    step = pl.program_id(0)

    @pl.when(step == 0)
    def _():
        sums[...] = jnp.zeros_like(sums)
        for k, near_ref in enumerate(near_refs):
            rows[k * far : (k + 1) * far] = near_ref[...]

    spread_tiles(from_ref, into_ref, tile_ref, rows, sums)

    @pl.when(step == pl.num_programs(0) - 1)
    def _():
        out_ref[:, :TILE, :] = sums[...].astype(BF16)
        out_ref[:, TILE:, :] = jnp.zeros((out_ref.shape[0], out_ref.shape[1] - TILE, TILE), BF16)


def chunk_kernel(recv_ref, send_in_ref, send_ref, bias_ref, rows, sem, *, scale):
    total = jnp.sum(recv_ref[...].astype(F32), axis=0) * scale
    size = total.shape[0] - 8
    bias_rows = total[size : size + 2] + total[size + 2 : size + 4]
    bias_ref[:, :TILE] = bias_rows[0:1]
    bias_ref[:, TILE:] = bias_rows[1:2]
    both = jnp.concatenate(high_low(total[:size]), axis=0).astype(BF16)
    rows[...] = jnp.broadcast_to(both[None], rows.shape)
    copy = pltpu.make_async_copy(rows, send_ref.at[:, TILE : TILE + 2 * size, :], sem)
    copy.start()
    copy.wait()


def final_kernel(recv_ref, input_ref, weight_grad_ref, *, group):
    pieces = recv_ref.shape[0]
    input_ref[...] = jnp.sum(recv_ref[:, :TILE, :].astype(F32), axis=0).astype(BF16)
    size = 2 * TILE // pieces
    for d in range(pieces):
        start = ((d % group) * (pieces // group) + d // group) * size
        chunk = recv_ref[d, TILE : TILE + size, :].astype(F32) + recv_ref[d, TILE + size :, :].astype(F32)
        lane = start // TILE * TILE
        weight_grad_ref[start % TILE : start % TILE + size, lane : lane + TILE] = chunk


def vmem(n):
    return [pl.BlockSpec(memory_space=pltpu.VMEM)] * n


def smem(n):
    return [pl.BlockSpec(memory_space=pltpu.SMEM)] * n


def call(kernel, name, outs, scalars, arrays, scratch=(), **more):
    single = not isinstance(outs, tuple)
    return pl.pallas_call(
        kernel,
        out_shape=outs,
        in_specs=smem(len(scalars)) + vmem(len(arrays)),
        out_specs=vmem(1)[0] if single else tuple(vmem(len(outs))),
        scratch_shapes=list(scratch),
        compiler_params=pltpu.CompilerParams(vmem_limit_bytes=56 << 20),
        name=name,
        **more,
    )(*scalars, *arrays)


def shape(dims, dtype):
    return jax.ShapeDtypeStruct(dims, dtype)


def swap(array, step, axis):
    return lax.ppermute(array, axis, [(i, i ^ step) for i in range(lax.axis_size(axis))])


def spread(kernel, name, outs, scalars, tiles, arrays, scratch):
    whole = lambda a: pl.BlockSpec(a.shape, lambda i, n=len(a.shape): (0,) * n)
    block = 16
    return pl.pallas_call(
        kernel,
        out_shape=outs,
        grid=(tiles.shape[0] // block,),
        in_specs=smem(len(scalars))
        + [pl.BlockSpec((block, TILE, TILE), lambda i: (i, 0, 0))]
        + [whole(a) for a in arrays],
        out_specs=tuple(whole(o) for o in outs),
        scratch_shapes=scratch,
        compiler_params=pltpu.CompilerParams(
            vmem_limit_bytes=56 << 20, dimension_semantics=("arbitrary",)
        ),
        name=name,
    )(*scalars, tiles, *arrays)


def body(features, weight, bias, tile_index, edge_count, edge_pos, edge_weight, grad_out):
    near = lax.axis_size(NEAR)
    far = lax.axis_size(FAR)
    group = lax.axis_size("d0")
    src = near * far
    dst = lax.axis_size(DST)
    index = tile_index.reshape(-1)
    counts = edge_count.reshape(-1)
    slots = counts.shape[0]
    positions = edge_pos.reshape(slots, -1).T
    weights = edge_weight.reshape(slots, -1).T
    edges = positions.shape[0]
    target = index // dst
    source = index % dst
    target_near = (target // (2 * far)) * 2 + target % 2
    place = (target_near ^ lax.axis_index(NEAR)) * far + (target // 2) % far
    tile_shape = shape((slots, TILE, TILE), BF16)
    block = shape((far, TILE, TILE), BF16)
    pair_scratch = (pltpu.VMEM((slots // 2, 2 * edges), jnp.int32), pltpu.VMEM((slots // 2, 2 * edges), F32))

    def build(positions, backward):
        return call(
            lambda *refs: build_kernel(*refs, backward=backward),
            "build_back" if backward else "build_tiles",
            tile_shape, (counts,), (positions, weights), pair_scratch,
        )

    sent = jnp.broadcast_to(features[None], (dst,) + features.shape)
    source_rows = lax.all_to_all(sent, DST, 0, 0, tiled=True)
    tiles = build(positions, False)
    own, *others = spread(
        forward_kernel,
        "forward_tiles",
        (shape(block.shape, F32),) + (block,) * (near - 1),
        (source, place),
        tiles,
        (source_rows,),
        [pltpu.VMEM((src, TILE, TILE), F32)],
    )
    others = [swap(other, k + 1, NEAR) for k, other in enumerate(others)]
    near_sums = call(add_kernel, "add_near", block, (), (own, *others))
    late_positions, near_sums = lax.optimization_barrier((positions, near_sums))
    back_tiles = build(late_positions, True)
    parts = lax.all_to_all(near_sums, FAR, 0, 0, tiled=True)
    parts, back_tiles = lax.optimization_barrier((parts, back_tiles))
    hidden, send, aggregated, grad_pre = call(
        dense_kernel,
        "dense_layer",
        (
            shape(grad_out.shape, BF16),
            block,
            shape(features.shape, BF16),
            shape(grad_out.shape, BF16),
        ),
        (),
        (parts, weight, bias.reshape(1, -1), grad_out),
    )
    far_rows = lax.all_to_all(send, FAR, 0, 0, tiled=True)

    quarter = shape((2 * TILE // group + 8, TILE), F32)
    piece = shape((2 * TILE // dst + 8, TILE), F32)
    own_part, *parts = call(
        grad_kernel, "grad_parts", (quarter,) * group, (lax.axis_index("d0").reshape(1),),
        (aggregated, grad_pre), (pltpu.VMEM((2 * TILE, TILE), F32),),
    )
    parts = [swap(part, k + 1, "d0") for k, part in enumerate(parts)]
    own_part, *parts = call(
        regrad_kernel, "grad_pieces", (piece,) * (dst // group), (lax.axis_index("x").reshape(1),),
        (own_part, *parts), (pltpu.VMEM((2 * TILE // group, TILE), F32),),
    )
    parts = [swap(part, k + 1, "x") for k, part in enumerate(parts)]
    share = call(share_kernel, "grad_share", shape((src,) + piece.shape, BF16), (), (own_part, *parts))
    far_rows, share = lax.optimization_barrier((far_rows, share))

    shared = lax.all_to_all(share, SRC, 0, 0, tiled=True)
    near_rows = [far_rows] + [swap(far_rows, k, NEAR) for k in range(1, near)]
    (back_send,) = spread(
        backward_kernel,
        "backward_tiles",
        (shape((dst, TILE + 2 * (piece.shape[0] - 8), TILE), BF16),),
        (place, source),
        back_tiles,
        near_rows,
        [pltpu.VMEM((src, TILE, TILE), BF16), pltpu.VMEM((dst, TILE, TILE), F32)],
    )
    node_scale = 1.0 / math.sqrt(features.shape[0] * src * dst)
    back_send, bias_grad = pl.pallas_call(
        lambda *refs: chunk_kernel(*refs, scale=node_scale),
        out_shape=(shape(back_send.shape, BF16), shape((1, 2 * TILE), F32)),
        in_specs=vmem(1) + [pl.BlockSpec(memory_space=pl.ANY)],
        out_specs=(pl.BlockSpec(memory_space=pl.ANY), pl.BlockSpec(memory_space=pltpu.VMEM)),
        scratch_shapes=[
            pltpu.VMEM((dst, back_send.shape[1] - TILE, TILE), BF16), pltpu.SemaphoreType.DMA(())
        ],
        input_output_aliases={1: 0},
        name="grad_chunk",
    )(shared, back_send)
    received = lax.all_to_all(back_send, DST, 0, 0, tiled=True)
    input_grad, weight_grad = call(
        lambda *refs: final_kernel(*refs, group=group),
        "final_sums",
        (shape(features.shape, BF16), shape((TILE, 2 * TILE), F32)),
        (),
        (received,),
    )
    return (hidden, input_grad, weight_grad, bias_grad.reshape(-1))


def solution(mesh):
    src, dst = mesh.devices.shape
    fine = Mesh(mesh.devices.reshape(2, src // 4, 2, dst // 4, 4), SRC + DST)
    rows = P(SRC + DST, None)
    placed = (
        rows,
        P(),
        P(),
        P(SRC, DST, None),
        P(SRC, DST, None),
        P(SRC, DST, None, None),
        P(SRC, DST, None, None),
        rows,
    )
    return jax.shard_map(
        body, mesh=fine, in_specs=placed, out_specs=(rows, rows, P(), P()), check_vma=False
    )
```

time: 185 us -> 190 us (1.027)
  blocking collectives: 101 us -> 19.5 us
  starting transfers between devices: 27 us -> 78.9 us
  waiting for transfers between devices: 11.8 us -> 41.3 us
  Pallas kernels: 37.5 us -> 41.1 us
  local copies, waits for them, and re-layouts: 4.6 us -> 6.58 us
    all_to_all x4 -> x1, blocking collectives: 101 us -> 19.5 us  [body(): received = lax.all_to_all(back_send, DST, 0, 0, tiled=True)]
    all_to_all x1 -> x4, starting transfers between devices: 10.2 us -> 40.9 us  [the longest x1 13.5 us: body(): parts = lax.all_to_all(near_sums, FAR, 0, 0, tiled=True)]
    ppermute x6 -> x12, starting transfers between devices: 16.7 us -> 38 us  [swap(): lax.ppermute(array, axis, [(i, i ^ step) for i in range(lax.axis_size(axi...]
    ppermute x6 -> x12, waiting for transfers between devices: 7.9 us -> 26.6 us  [swap(): lax.ppermute(array, axis, [(i, i ^ step) for i in range(lax.axis_size(axi...]
    pallas_call x0 -> x3, Pallas kernels: none -> 16.9 us  [the longest x2 14.7 us: spread(): pl.pallas_call(kernel, out_shape=outs, grid=(tiles.shape[0] // block,), i...]
    pallas_call x9 -> x8, Pallas kernels: 37.5 us -> 24.1 us  [call(): pl.pallas_call(kernel, out_shape=outs, in_specs=smem(len(scalars)) + vmem...]
    all_to_all x1 -> x4, waiting for transfers between devices: 3.94 us -> 14.6 us  [the longest x1 10.8 us: body(): parts = lax.all_to_all(near_sums, FAR, 0, 0, tiled=True)]
    unnamed x16 -> x34, local copies, waits for them, and re-layouts: 2.95 us -> 4.92 us
  transfers between devices with their start and end apart: 7 -> 16, of which waited for: 5 -> 9; matrix products, arithmetic and copies ran while one was open for 0% -> 0% of each run, Pallas kernels for 7% -> 13%
where the time goes in v3:
time: 190 us; the launch traced here: 189 us
  starting transfers between devices  78.9 us (42%)
  waiting for transfers between devices  41.3 us (22%)
  Pallas kernels  41.1 us (22%)
  blocking collectives  19.5 us (10%)
  local copies, waits for them, and re-layouts  6.58 us (3%)
    ppermute x12, starting transfers between devices, swap(): lax.ppermute(array, axis, [(i, i ^ step) for i in range(lax.axis_size(axi...  38 us
    ppermute x12, waiting for transfers between devices, swap(): lax.ppermute(array, axis, [(i, i ^ step) for i in range(lax.axis_size(axi...  26.6 us
    pallas_call x8, Pallas kernels, call(): pl.pallas_call(kernel, out_shape=outs, in_specs=smem(len(scalars)) + vmem...  24.1 us
    all_to_all x1, blocking collectives, body(): received = lax.all_to_all(back_send, DST, 0, 0, tiled=True)  19.5 us
    pallas_call x2, Pallas kernels, spread(): pl.pallas_call(kernel, out_shape=outs, grid=(tiles.shape[0] // block,), i...  14.7 us
    all_to_all x1, starting transfers between devices, body(): parts = lax.all_to_all(near_sums, FAR, 0, 0, tiled=True)  13.5 us
    all_to_all x1, starting transfers between devices, body(): shared = lax.all_to_all(share, SRC, 0, 0, tiled=True)  11.9 us
    all_to_all x1, waiting for transfers between devices, body(): parts = lax.all_to_all(near_sums, FAR, 0, 0, tiled=True)  10.8 us
  transfers between devices with their start and end apart: 16, of which 9 were waited for; matrix products, arithmetic and copies ran while one was open for 0% of the time, Pallas kernels for 13%

profile of v3, /device:TPU:1, one launch (start us, length us, event | category | flops | bytes accessed | tf_op | source)
XLA Modules:
  0.0 188.8 jit_solution(2604218663399385581)
XLA Ops:
  0.6 1.7 broadcast_in_dim.2
  2.3 10.2 %all-to-all-start = ((bf16[16,128,128]{2,1,0:T(8,128)(2,1)}), bf16[16,128,128]{2,1,0:T(8,128)(2,1)S(1)}, u32[]{:S(2)}, u32[]{:S(2)}) async-start(bf16[16,128,128]{2,1,0:T(8,128)(2,1)} %broadcast_in_dim.2), calls=%async_computation | async-start | bytes 1048576 | tf_op jit(solution)/shard_map/all_to_all | solution.py:282
  12.5 6.7 %build_tiles.1.tile_ref = bf16[128,128,128]{2,1,0:T(8,128)(2,1)} custom-call(s32[128]{0:T(128)} %bitcast.32, s32[64,128]{1,0:T(8,128)} %bitcast.28, bf16[64,128]{1,0:T(8,128)(2,1)} %bitcast.30), custom_call_target="tpu_custom_call" | custom-call | tf_op jit(solution)/shard_map/build_tiles/pallas_call | solution.py:215
  19.3 0.6 fusion.1
  19.9 3.9 %all-to-all-done.rows_ref = bf16[16,128,128]{2,1,0:T(8,128)(2,1)S(1)} async-done(((bf16[16,128,128]{2,1,0:T(8,128)(2,1)}), bf16[16,128,128]{2,1,0:T(8,128)(2,1)S(1)}, u32[]{:S(2)}, u32[]{:S(2)}) %all-to-all-start) | async-done | bytes 524320 | tf_op jit(solution)/shard_map/all_to_all | solution.py:282
  23.7 0.8 copy-done
  24.6 7.4 %forward_tiles.1 = (f32[8,128,128]{2,1,0:T(8,128)}, bf16[8,128,128]{2,1,0:T(8,128)(2,1)}, bf16[8,128,128]{2,1,0:T(8,128)(2,1)}, bf16[8,128,128]{2,1,0:T(8,128)(2,1)}) custom-call(s32[128]{0:T(128)} %get-tuple-element.57.from_ref.into_ref, s32[128]{0:T(128)} %get-tuple-element.56.into_ref.from_ref, bf16[128,128,128]{2,1,0:T(8,128)(2,1)} %build_tiles.1.tile_ref, ...), custom_call_target="tpu_custom_call" | custom-call | tf_op jit(solution)/shard_map/forward_tiles/pallas_call | solution.py:238
  32.0 1.9 %collective-permute-start = (bf16[8,128,128]{2,1,0:T(8,128)(2,1)}, bf16[8,128,128]{2,1,0:T(8,128)(2,1)S(1)}, u32[]{:S(2)}, u32[]{:S(2)}) collective-permute-start(bf16[8,128,128]{2,1,0:T(8,128)(2,1)} %get-tuple-element.31), channel_id=1, source_target_pairs={{0,16},{16,0},{256,272},{272,256},{1,17},{17,1},{257,273},{273,257... | collective-permute-start | bytes 786440 | tf_op jit(solution)/shard_map/ppermute | solution.py:232
  33.9 2.1 %collective-permute-start.1 = (bf16[8,128,128]{2,1,0:T(8,128)(2,1)}, bf16[8,128,128]{2,1,0:T(8,128)(2,1)S(1)}, u32[]{:S(2)}, u32[]{:S(2)}) collective-permute-start(bf16[8,128,128]{2,1,0:T(8,128)(2,1)} %get-tuple-element.32), channel_id=1, source_target_pairs={{0,256},{16,272},{256,0},{272,16},{1,257},{17,273},{257,1},{273,17... | collective-permute-start | bytes 786440 | tf_op jit(solution)/shard_map/ppermute | solution.py:232
  36.0 4.4 %collective-permute-start.2 = (bf16[8,128,128]{2,1,0:T(8,128)(2,1)}, bf16[8,128,128]{2,1,0:T(8,128)(2,1)S(1)}, u32[]{:S(2)}, u32[]{:S(2)}) collective-permute-start(bf16[8,128,128]{2,1,0:T(8,128)(2,1)} %get-tuple-element.33), channel_id=1, source_target_pairs={{0,272},{16,256},{256,16},{272,0},{1,273},{17,257},{257,17},{273,1... | collective-permute-start | bytes 786440 | tf_op jit(solution)/shard_map/ppermute | solution.py:232
  40.4 0.2 collective-permute-done.rest_0_
  40.5 7.5 %collective-permute-done.1.rest_1_ = bf16[8,128,128]{2,1,0:T(8,128)(2,1)S(1)} collective-permute-done((bf16[8,128,128]{2,1,0:T(8,128)(2,1)}, bf16[8,128,128]{2,1,0:T(8,128)(2,1)S(1)}, u32[]{:S(2)}, u32[]{:S(2)}) %collective-permute-start.1) | collective-permute-done | bytes 262176 | tf_op jit(solution)/shard_map/ppermute | solution.py:232
  48.1 0.7 copy-done.8
  48.8 0.1 copy-done.9
  48.9 2.1 %add_near.1 = bf16[8,128,128]{2,1,0:T(8,128)(2,1)} custom-call(f32[8,128,128]{2,1,0:T(8,128)} %get-tuple-element.30.own_ref, bf16[8,128,128]{2,1,0:T(8,128)(2,1)} %copy-done.7, bf16[8,128,128]{2,1,0:T(8,128)(2,1)} %copy-done.8, bf16[8,128,128]{2,1,0:T(8,128)(2,1)} %copy-done.9), custom_call_target="tpu_custom_call" | custom-call | tf_op jit(solution)/shard_map/add_near/pallas_call | solution.py:215
  50.9 13.5 %all-to-all-start.1 = ((bf16[8,128,128]{2,1,0:T(8,128)(2,1)}), bf16[8,128,128]{2,1,0:T(8,128)(2,1)S(1)}, u32[]{:S(2)}, u32[]{:S(2)}) async-start(bf16[8,128,128]{2,1,0:T(8,128)(2,1)} %add_near.1), calls=%async_computation.1 | async-start | bytes 524288 | tf_op jit(solution)/shard_map/all_to_all | solution.py:297
  64.4 6.8 %build_back.1.tile_ref = bf16[128,128,128]{2,1,0:T(8,128)(2,1)} custom-call(s32[128]{0:T(128)} %bitcast.33, s32[64,128]{1,0:T(8,128)} %bitcast.29, bf16[64,128]{1,0:T(8,128)(2,1)} %bitcast.31), custom_call_target="tpu_custom_call" | custom-call | tf_op jit(solution)/shard_map/build_back/pallas_call | solution.py:215
  71.2 10.8 %all-to-all-done.1.recv_ref = bf16[8,128,128]{2,1,0:T(8,128)(2,1)S(1)} async-done(((bf16[8,128,128]{2,1,0:T(8,128)(2,1)}), bf16[8,128,128]{2,1,0:T(8,128)(2,1)S(1)}, u32[]{:S(2)}, u32[]{:S(2)}) %all-to-all-start.1) | async-done | bytes 262176 | tf_op jit(solution)/shard_map/all_to_all | solution.py:297
  82.0 0.7 copy-done.2
  82.7 2.0 %dense_layer.1 = (bf16[128,256]{1,0:T(8,128)(2,1)}, bf16[8,128,128]{2,1,0:T(8,128)(2,1)}, bf16[128,128]{1,0:T(8,128)(2,1)}, bf16[128,256]{1,0:T(8,128)(2,1)}) custom-call(bf16[8,128,128]{2,1,0:T(8,128)(2,1)} %copy-done.2, bf16[128,256]{1,0:T(8,128)(2,1)} %weight_ref.1, f32[1,256]{1,0:T(1,128)} %bitcast.34, bf16[128,256]{1,0:T(8,128)(2,1)} %grad_ref.1), custom_call_target="tpu_custom_call" | custom-call | tf_op jit(solution)/shard_map/dense_layer/pallas_call | solution.py:215
  84.7 5.3 %all-to-all-start.2 = ((bf16[8,128,128]{2,1,0:T(8,128)(2,1)}), bf16[8,128,128]{2,1,0:T(8,128)(2,1)S(1)}, u32[]{:S(2)}, u32[]{:S(2)}) async-start(bf16[8,128,128]{2,1,0:T(8,128)(2,1)} %get-tuple-element.38), calls=%async_computation.2 | async-start | bytes 524288 | tf_op jit(solution)/shard_map/all_to_all | solution.py:311
  90.0 1.7 grad_parts.1
  91.8 4.7 %collective-permute-start.3 = (f32[72,128]{1,0:T(8,128)}, f32[72,128]{1,0:T(8,128)S(1)}, u32[]{:S(2)}, u32[]{:S(2)}) collective-permute-start(f32[72,128]{1,0:T(8,128)} %get-tuple-element.42), channel_id=1, source_target_pairs={{0,1},{1,0},{2,3},{3,2},{4,5},{5,4},{6,7},{7,6},{8,9},{9,8},{10,11... | collective-permute-start | bytes 110600 | tf_op jit(solution)/shard_map/ppermute | solution.py:232
  96.5 4.3 %collective-permute-start.4 = (f32[72,128]{1,0:T(8,128)}, f32[72,128]{1,0:T(8,128)S(1)}, u32[]{:S(2)}, u32[]{:S(2)}) collective-permute-start(f32[72,128]{1,0:T(8,128)} %get-tuple-element.43), channel_id=1, source_target_pairs={{0,2},{1,3},{2,0},{3,1},{4,6},{5,7},{6,4},{7,5},{8,10},{9,11},{10,... | collective-permute-start | bytes 110600 | tf_op jit(solution)/shard_map/ppermute | solution.py:232
  100.8 2.6 %collective-permute-start.5 = (f32[72,128]{1,0:T(8,128)}, f32[72,128]{1,0:T(8,128)S(1)}, u32[]{:S(2)}, u32[]{:S(2)}) collective-permute-start(f32[72,128]{1,0:T(8,128)} %get-tuple-element.44), channel_id=1, source_target_pairs={{0,3},{1,2},{2,1},{3,0},{4,7},{5,6},{6,5},{7,4},{8,11},{9,10},{10,... | collective-permute-start | bytes 110600 | tf_op jit(solution)/shard_map/ppermute | solution.py:232
  103.5 4.6 %collective-permute-done.5.rest_3_ = f32[72,128]{1,0:T(8,128)S(1)} collective-permute-done((f32[72,128]{1,0:T(8,128)}, f32[72,128]{1,0:T(8,128)S(1)}, u32[]{:S(2)}, u32[]{:S(2)}) %collective-permute-start.5) | collective-permute-done | bytes 36896 | tf_op jit(solution)/shard_map/ppermute | solution.py:232
  108.1 0.6 copy-done.12
  108.7 1.4 grad_pieces.1
  110.2 1.9 %collective-permute-start.6 = (f32[24,128]{1,0:T(8,128)}, f32[24,128]{1,0:T(8,128)S(1)}, u32[]{:S(2)}, u32[]{:S(2)}) collective-permute-start(f32[24,128]{1,0:T(8,128)} %get-tuple-element.46), channel_id=1, source_target_pairs={{0,4},{4,0},{8,12},{12,8},{1,5},{5,1},{9,13},{13,9},{2,6},{6,2},{1... | collective-permute-start | bytes 36872 | tf_op jit(solution)/shard_map/ppermute | solution.py:232
  112.1 2.8 %collective-permute-start.7 = (f32[24,128]{1,0:T(8,128)}, f32[24,128]{1,0:T(8,128)S(1)}, u32[]{:S(2)}, u32[]{:S(2)}) collective-permute-start(f32[24,128]{1,0:T(8,128)} %get-tuple-element.47), channel_id=1, source_target_pairs={{0,8},{4,12},{8,0},{12,4},{1,9},{5,13},{9,1},{13,5},{2,10},{6,14},... | collective-permute-start | bytes 36872 | tf_op jit(solution)/shard_map/ppermute | solution.py:232
  114.9 4.8 %collective-permute-start.8 = (f32[24,128]{1,0:T(8,128)}, f32[24,128]{1,0:T(8,128)S(1)}, u32[]{:S(2)}, u32[]{:S(2)}) collective-permute-start(f32[24,128]{1,0:T(8,128)} %get-tuple-element.48), channel_id=1, source_target_pairs={{0,12},{4,8},{8,4},{12,0},{1,13},{5,9},{9,5},{13,1},{2,14},{6,10},... | collective-permute-start | bytes 36872 | tf_op jit(solution)/shard_map/ppermute | solution.py:232
  119.8 0.0 copy-start.13
  119.8 1.2 collective-permute-done.8.rest_3_
  121.0 0.6 copy-done.15
  121.6 1.5 grad_share.1
  123.1 11.9 %all-to-all-start.3 = ((bf16[32,24,128]{2,1,0:T(8,128)(2,1)}), bf16[32,24,128]{2,1,0:T(8,128)(2,1)S(1)}, u32[]{:S(2)}, u32[]{:S(2)}) async-start(bf16[32,24,128]{2,1,0:T(8,128)(2,1)} %grad_share.1), calls=%async_computation.3 | async-start | bytes 393216 | tf_op jit(solution)/shard_map/all_to_all | solution.py:328
  135.0 4.0 %collective-permute-start.11 = (bf16[8,128,128]{2,1,0:T(8,128)(2,1)S(1)}, bf16[8,128,128]{2,1,0:T(8,128)(2,1)S(1)}, u32[]{:S(2)}, u32[]{:S(2)}) collective-permute-start(bf16[8,128,128]{2,1,0:T(8,128)(2,1)S(1)} %all-to-all-done.2.rest_0_), channel_id=1, source_target_pairs={{0,272},{16,256},{256,16},{272,0},{1,273},{17,257},{257,17},{273,1... | collective-permute-start | bytes 786440 | tf_op jit(solution)/shard_map/ppermute | solution.py:232
  139.0 2.2 %collective-permute-start.10 = (bf16[8,128,128]{2,1,0:T(8,128)(2,1)S(1)}, bf16[8,128,128]{2,1,0:T(8,128)(2,1)S(1)}, u32[]{:S(2)}, u32[]{:S(2)}) collective-permute-start(bf16[8,128,128]{2,1,0:T(8,128)(2,1)S(1)} %all-to-all-done.2.rest_0_), channel_id=1, source_target_pairs={{0,256},{16,272},{256,0},{272,16},{1,257},{17,273},{257,1},{273,17... | collective-permute-start | bytes 786440 | tf_op jit(solution)/shard_map/ppermute | solution.py:232
  141.2 2.1 %collective-permute-start.9 = (bf16[8,128,128]{2,1,0:T(8,128)(2,1)S(1)}, bf16[8,128,128]{2,1,0:T(8,128)(2,1)S(1)}, u32[]{:S(2)}, u32[]{:S(2)}) collective-permute-start(bf16[8,128,128]{2,1,0:T(8,128)(2,1)S(1)} %all-to-all-done.2.rest_0_), channel_id=1, source_target_pairs={{0,16},{16,0},{256,272},{272,256},{1,17},{17,1},{257,273},{273,257... | collective-permute-start | bytes 786440 | tf_op jit(solution)/shard_map/ppermute | solution.py:232
  143.4 7.6 %collective-permute-done.11.rest_3_ = bf16[8,128,128]{2,1,0:T(8,128)(2,1)S(1)} collective-permute-done((bf16[8,128,128]{2,1,0:T(8,128)(2,1)S(1)}, bf16[8,128,128]{2,1,0:T(8,128)(2,1)S(1)}, u32[]{:S(2)}, u32[]{:S(2)}) %collective-permute-start.11) | collective-permute-done | bytes 262176 | tf_op jit(solution)/shard_map/ppermute | solution.py:232
  151.0 1.6 collective-permute-done.10.rest_2_
  152.6 3.9 %collective-permute-done.9.rest_1_ = bf16[8,128,128]{2,1,0:T(8,128)(2,1)S(1)} collective-permute-done((bf16[8,128,128]{2,1,0:T(8,128)(2,1)S(1)}, bf16[8,128,128]{2,1,0:T(8,128)(2,1)S(1)}, u32[]{:S(2)}, u32[]{:S(2)}) %collective-permute-start.9) | collective-permute-done | bytes 262176 | tf_op jit(solution)/shard_map/ppermute | solution.py:232
  156.5 0.7 copy-done.6
  157.2 7.3 %backward_tiles.1.refs_1_ = bf16[16,160,128]{2,1,0:T(8,128)(2,1)} custom-call(s32[128]{0:T(128)} %get-tuple-element.56.into_ref.from_ref, s32[128]{0:T(128)} %get-tuple-element.57.from_ref.into_ref, bf16[128,128,128]{2,1,0:T(8,128)(2,1)} %build_back.1.tile_ref, bf16[8,128,128]{2,1,0:T(8,128)(2,1)} %copy-done.1, bf16[8,128,128]{2,1,0:T(8,128)(2,1)} %copy-done.6, ...), custom_call_target="tpu_custom_call" | custom-call | tf_op jit(solution)/shard_map/backward_tiles/pallas_call | solution.py:238
  164.5 0.7 copy-done.3
  165.2 2.2 %grad_chunk.1 = (bf16[16,160,128]{2,1,0:T(8,128)(2,1)}, f32[1,256]{1,0:T(1,128)}) custom-call(bf16[32,24,128]{2,1,0:T(8,128)(2,1)} %copy-done.3, bf16[16,160,128]{2,1,0:T(8,128)(2,1)} %backward_tiles.1.refs_1_), custom_call_target="tpu_custom_call", output_to_operand_aliasing={{0}: (1, {})} | custom-call | tf_op jit(solution)/shard_map/grad_chunk/pallas_call | solution.py:340
  167.4 19.5 %all_to_all.25.refs_0_ = bf16[16,160,128]{2,1,0:T(8,128)(2,1)} all-to-all(bf16[16,160,128]{2,1,0:T(8,128)(2,1)} %get-tuple-element.52), channel_id=1, replica_groups=mesh['ylo'=2,'zq'=8,'z0'=2,'x'=4,'d0'=4] {'x','d0'}, dimensions={0} | all-to-all | bytes 1310720 | tf_op jit(solution)/shard_map/all_to_all | solution.py:351
  186.9 1.8 final_sums.1
  (32 shorter events, 0.1 us)
Async XLA Ops:
  0.6 18.6 %copy-start.16 = (s32[1,1,128]{2,1,0:T(1,128)S(1)}, s32[1,1,128]{2,1,0:T(1,128)}, u32[]{:S(2)}) copy-start(s32[1,1,128]{2,1,0:T(1,128)} %param.11) | copy-start | bytes 1540
  2.3 21.4 %all-to-all-start = ((bf16[16,128,128]{2,1,0:T(8,128)(2,1)}), bf16[16,128,128]{2,1,0:T(8,128)(2,1)S(1)}, u32[]{:S(2)}, u32[]{:S(2)}) async-start(bf16[16,128,128]{2,1,0:T(8,128)(2,1)} %broadcast_in_dim.2), calls=%async_computation | async-start | bytes 1048576 | tf_op jit(solution)/shard_map/all_to_all | solution.py:282
  23.7 0.8 copy-start
  32.0 8.5 %collective-permute-start = (bf16[8,128,128]{2,1,0:T(8,128)(2,1)}, bf16[8,128,128]{2,1,0:T(8,128)(2,1)S(1)}, u32[]{:S(2)}, u32[]{:S(2)}) collective-permute-start(bf16[8,128,128]{2,1,0:T(8,128)(2,1)} %get-tuple-element.31), channel_id=1, source_target_pairs={{0,16},{16,0},{256,272},{272,256},{1,17},{17,1},{257,273},{273,257... | collective-permute-start | bytes 786440 | tf_op jit(solution)/shard_map/ppermute | solution.py:232
  33.9 14.1 %collective-permute-start.1 = (bf16[8,128,128]{2,1,0:T(8,128)(2,1)}, bf16[8,128,128]{2,1,0:T(8,128)(2,1)S(1)}, u32[]{:S(2)}, u32[]{:S(2)}) collective-permute-start(bf16[8,128,128]{2,1,0:T(8,128)(2,1)} %get-tuple-element.32), channel_id=1, source_target_pairs={{0,256},{16,272},{256,0},{272,16},{1,257},{17,273},{257,1},{273,17... | collective-permute-start | bytes 786440 | tf_op jit(solution)/shard_map/ppermute | solution.py:232
  36.0 12.1 %collective-permute-start.2 = (bf16[8,128,128]{2,1,0:T(8,128)(2,1)}, bf16[8,128,128]{2,1,0:T(8,128)(2,1)S(1)}, u32[]{:S(2)}, u32[]{:S(2)}) collective-permute-start(bf16[8,128,128]{2,1,0:T(8,128)(2,1)} %get-tuple-element.33), channel_id=1, source_target_pairs={{0,272},{16,256},{256,16},{272,0},{1,273},{17,257},{257,17},{273,1... | collective-permute-start | bytes 786440 | tf_op jit(solution)/shard_map/ppermute | solution.py:232
  40.5 7.5 %copy-start.7 = (bf16[8,128,128]{2,1,0:T(8,128)(2,1)}, bf16[8,128,128]{2,1,0:T(8,128)(2,1)S(1)}, u32[]{:S(2)}) copy-start(bf16[8,128,128]{2,1,0:T(8,128)(2,1)S(1)} %collective-permute-done.rest_0_) | copy-start | bytes 786436
  48.0 0.7 copy-start.8
  48.1 0.8 copy-start.9
  50.9 31.0 %all-to-all-start.1 = ((bf16[8,128,128]{2,1,0:T(8,128)(2,1)}), bf16[8,128,128]{2,1,0:T(8,128)(2,1)S(1)}, u32[]{:S(2)}, u32[]{:S(2)}) async-start(bf16[8,128,128]{2,1,0:T(8,128)(2,1)} %add_near.1), calls=%async_computation.1 | async-start | bytes 524288 | tf_op jit(solution)/shard_map/all_to_all | solution.py:297
  82.0 0.7 copy-start.2
  84.7 38.4 %all-to-all-start.2 = ((bf16[8,128,128]{2,1,0:T(8,128)(2,1)}), bf16[8,128,128]{2,1,0:T(8,128)(2,1)S(1)}, u32[]{:S(2)}, u32[]{:S(2)}) async-start(bf16[8,128,128]{2,1,0:T(8,128)(2,1)} %get-tuple-element.38), calls=%async_computation.2 | async-start | bytes 524288 | tf_op jit(solution)/shard_map/all_to_all | solution.py:311
  91.8 11.7 %collective-permute-start.3 = (f32[72,128]{1,0:T(8,128)}, f32[72,128]{1,0:T(8,128)S(1)}, u32[]{:S(2)}, u32[]{:S(2)}) collective-permute-start(f32[72,128]{1,0:T(8,128)} %get-tuple-element.42), channel_id=1, source_target_pairs={{0,1},{1,0},{2,3},{3,2},{4,5},{5,4},{6,7},{7,6},{8,9},{9,8},{10,11... | collective-permute-start | bytes 110600 | tf_op jit(solution)/shard_map/ppermute | solution.py:232
  96.5 7.0 %collective-permute-start.4 = (f32[72,128]{1,0:T(8,128)}, f32[72,128]{1,0:T(8,128)S(1)}, u32[]{:S(2)}, u32[]{:S(2)}) collective-permute-start(f32[72,128]{1,0:T(8,128)} %get-tuple-element.43), channel_id=1, source_target_pairs={{0,2},{1,3},{2,0},{3,1},{4,6},{5,7},{6,4},{7,5},{8,10},{9,11},{10,... | collective-permute-start | bytes 110600 | tf_op jit(solution)/shard_map/ppermute | solution.py:232
  100.8 7.3 %collective-permute-start.5 = (f32[72,128]{1,0:T(8,128)}, f32[72,128]{1,0:T(8,128)S(1)}, u32[]{:S(2)}, u32[]{:S(2)}) collective-permute-start(f32[72,128]{1,0:T(8,128)} %get-tuple-element.44), channel_id=1, source_target_pairs={{0,3},{1,2},{2,1},{3,0},{4,7},{5,6},{6,5},{7,4},{8,11},{9,10},{10,... | collective-permute-start | bytes 110600 | tf_op jit(solution)/shard_map/ppermute | solution.py:232
  103.5 4.6 %copy-start.10 = (f32[72,128]{1,0:T(8,128)}, f32[72,128]{1,0:T(8,128)S(1)}, u32[]{:S(2)}) copy-start(f32[72,128]{1,0:T(8,128)S(1)} %collective-permute-done.3.rest_1_) | copy-start | bytes 110596
  103.5 4.6 %copy-start.11 = (f32[72,128]{1,0:T(8,128)}, f32[72,128]{1,0:T(8,128)S(1)}, u32[]{:S(2)}) copy-start(f32[72,128]{1,0:T(8,128)S(1)} %collective-permute-done.4.rest_2_) | copy-start | bytes 110596
  108.1 0.6 copy-start.12
  110.2 9.6 %collective-permute-start.6 = (f32[24,128]{1,0:T(8,128)}, f32[24,128]{1,0:T(8,128)S(1)}, u32[]{:S(2)}, u32[]{:S(2)}) collective-permute-start(f32[24,128]{1,0:T(8,128)} %get-tuple-element.46), channel_id=1, source_target_pairs={{0,4},{4,0},{8,12},{12,8},{1,5},{5,1},{9,13},{13,9},{2,6},{6,2},{1... | collective-permute-start | bytes 36872 | tf_op jit(solution)/shard_map/ppermute | solution.py:232
  112.1 7.7 %collective-permute-start.7 = (f32[24,128]{1,0:T(8,128)}, f32[24,128]{1,0:T(8,128)S(1)}, u32[]{:S(2)}, u32[]{:S(2)}) collective-permute-start(f32[24,128]{1,0:T(8,128)} %get-tuple-element.47), channel_id=1, source_target_pairs={{0,8},{4,12},{8,0},{12,4},{1,9},{5,13},{9,1},{13,5},{2,10},{6,14},... | collective-permute-start | bytes 36872 | tf_op jit(solution)/shard_map/ppermute | solution.py:232
  114.9 6.1 %collective-permute-start.8 = (f32[24,128]{1,0:T(8,128)}, f32[24,128]{1,0:T(8,128)S(1)}, u32[]{:S(2)}, u32[]{:S(2)}) collective-permute-start(f32[24,128]{1,0:T(8,128)} %get-tuple-element.48), channel_id=1, source_target_pairs={{0,12},{4,8},{8,4},{12,0},{1,13},{5,9},{9,5},{13,1},{2,14},{6,10},... | collective-permute-start | bytes 36872 | tf_op jit(solution)/shard_map/ppermute | solution.py:232
  119.8 1.3 copy-start.13
  119.8 1.3 copy-start.14
  121.0 0.6 copy-start.15
  123.1 33.4 %copy-start.1 = (bf16[8,128,128]{2,1,0:T(8,128)(2,1)}, bf16[8,128,128]{2,1,0:T(8,128)(2,1)S(1)}, u32[]{:S(2)}) copy-start(bf16[8,128,128]{2,1,0:T(8,128)(2,1)S(1)} %all-to-all-done.2.rest_0_) | copy-start | bytes 786436
  123.1 41.4 %all-to-all-start.3 = ((bf16[32,24,128]{2,1,0:T(8,128)(2,1)}), bf16[32,24,128]{2,1,0:T(8,128)(2,1)S(1)}, u32[]{:S(2)}, u32[]{:S(2)}) async-start(bf16[32,24,128]{2,1,0:T(8,128)(2,1)} %grad_share.1), calls=%async_computation.3 | async-start | bytes 393216 | tf_op jit(solution)/shard_map/all_to_all | solution.py:328
  135.0 16.0 %collective-permute-start.11 = (bf16[8,128,128]{2,1,0:T(8,128)(2,1)S(1)}, bf16[8,128,128]{2,1,0:T(8,128)(2,1)S(1)}, u32[]{:S(2)}, u32[]{:S(2)}) collective-permute-start(bf16[8,128,128]{2,1,0:T(8,128)(2,1)S(1)} %all-to-all-done.2.rest_0_), channel_id=1, source_target_pairs={{0,272},{16,256},{256,16},{272,0},{1,273},{17,257},{257,17},{273,1... | collective-permute-start | bytes 786440 | tf_op jit(solution)/shard_map/ppermute | solution.py:232
  139.0 13.6 %collective-permute-start.10 = (bf16[8,128,128]{2,1,0:T(8,128)(2,1)S(1)}, bf16[8,128,128]{2,1,0:T(8,128)(2,1)S(1)}, u32[]{:S(2)}, u32[]{:S(2)}) collective-permute-start(bf16[8,128,128]{2,1,0:T(8,128)(2,1)S(1)} %all-to-all-done.2.rest_0_), channel_id=1, source_target_pairs={{0,256},{16,272},{256,0},{272,16},{1,257},{17,273},{257,1},{273,17... | collective-permute-start | bytes 786440 | tf_op jit(solution)/shard_map/ppermute | solution.py:232
  141.2 15.3 %collective-permute-start.9 = (bf16[8,128,128]{2,1,0:T(8,128)(2,1)S(1)}, bf16[8,128,128]{2,1,0:T(8,128)(2,1)S(1)}, u32[]{:S(2)}, u32[]{:S(2)}) collective-permute-start(bf16[8,128,128]{2,1,0:T(8,128)(2,1)S(1)} %all-to-all-done.2.rest_0_), channel_id=1, source_target_pairs={{0,16},{16,0},{256,272},{272,256},{1,17},{17,1},{257,273},{273,257... | collective-permute-start | bytes 786440 | tf_op jit(solution)/shard_map/ppermute | solution.py:232
  151.0 5.5 %copy-start.4 = (bf16[8,128,128]{2,1,0:T(8,128)(2,1)}, bf16[8,128,128]{2,1,0:T(8,128)(2,1)S(1)}, u32[]{:S(2)}) copy-start(bf16[8,128,128]{2,1,0:T(8,128)(2,1)S(1)} %collective-permute-done.11.rest_3_) | copy-start | bytes 786436
  152.6 3.9 %copy-start.5 = (bf16[8,128,128]{2,1,0:T(8,128)(2,1)}, bf16[8,128,128]{2,1,0:T(8,128)(2,1)S(1)}, u32[]{:S(2)}) copy-start(bf16[8,128,128]{2,1,0:T(8,128)(2,1)S(1)} %collective-permute-done.10.rest_2_) | copy-start | bytes 786436
  156.5 0.7 copy-start.6
  164.5 0.7 copy-start.3

commit v4 on v2

--- a/solution.py
+++ b/solution.py
@@ -71,20 +71,9 @@
     lax.fori_loop(0, tile_ref.shape[0] // UNROLL, one_step, 0)
 
 
-def forward_kernel(from_ref, into_ref, tile_ref, rows_ref, own_ref, *rest):
-    sums = rest[-1]
-    far = own_ref.shape[0]
+def forward_kernel(from_ref, into_ref, tile_ref, rows_ref, out_ref, sums):
     spread_tiles(from_ref, into_ref, tile_ref, rows_ref, sums)
-    own_ref[...] = sums[:far]
-    for k, out_ref in enumerate(rest[:-1]):
-        out_ref[...] = sums[(k + 1) * far : (k + 2) * far].astype(BF16)
-
-
-def add_kernel(own_ref, *rest):
-    total = own_ref[...]
-    for recv_ref in rest[:-1]:
-        total = total + recv_ref[...].astype(F32)
-    rest[-1][...] = total.astype(BF16)
+    out_ref[...] = sums[...].astype(BF16)
 
 
 def high_low(value):
@@ -93,7 +82,12 @@
 
 
 def bias_tile(bias_rows):
-    return jnp.concatenate(high_low(bias_rows), axis=0).astype(BF16)
+    high, low = high_low(bias_rows[0:2])
+    return jnp.concatenate([high, low, jnp.zeros((4, TILE), F32)], axis=0).astype(BF16)
+
+
+def bias_sum(tile):
+    return tile[0:2] + tile[2:4]
 
 
 def dense_kernel(recv_ref, weight_ref, bias_ref, grad_ref, hidden_ref, send_ref):
@@ -111,9 +105,8 @@
     send_ref[:, TILE : TILE + rows, :] = part[:, :TILE].reshape(peers, rows, TILE)
     send_ref[:, TILE + rows : TILE + 2 * rows, :] = part[:, TILE:].reshape(peers, rows, TILE)
     bias_part = jnp.sum(grad_pre.astype(F32), axis=0, keepdims=True)
-    sub = lax.broadcasted_iota(jnp.int32, (8, TILE), 0)
-    bias_rows = jnp.where(sub == 0, bias_part[:, :TILE], jnp.where(sub == 1, bias_part[:, TILE:], 0.0))
-    send_ref[:, TILE + 2 * rows :, :] = jnp.broadcast_to(bias_tile(bias_rows)[None], (peers, 16, TILE))
+    bias_rows = jnp.concatenate([bias_part[:, :TILE], bias_part[:, TILE:]], axis=0)
+    send_ref[:, TILE + 2 * rows :, :] = jnp.broadcast_to(bias_tile(bias_rows)[None], (peers, 8, TILE))
 
 
 def middle_kernel(recv_ref, out_ref):
@@ -121,11 +114,32 @@
     top = peers * TILE
     out_ref[:top] = recv_ref[:, :TILE, :].reshape(top, TILE)
     total = jnp.sum(recv_ref[:, TILE:, :].astype(F32), axis=0)
-    rows = total.shape[0] - 16
+    rows = total.shape[0] - 8
     high, low = high_low(total[:rows])
     out_ref[top : top + rows] = high.astype(BF16)
     out_ref[top + rows : top + 2 * rows] = low.astype(BF16)
-    out_ref[top + 2 * rows :] = bias_tile(total[rows : rows + 8] + total[rows + 8 :])
+    out_ref[top + 2 * rows :] = bias_tile(bias_sum(total[rows:]))
+
+
+def share_kernel(*rest):
+    extra_refs, out_ref = rest[:-1], rest[-1]
+    total = extra_refs[0][...].astype(F32)
+    for extra_ref in extra_refs[1:]:
+        total = total + extra_ref[...].astype(F32)
+    rows = (total.shape[0] - 8) // 2
+    chunk = (total[:rows] + total[rows : 2 * rows]).astype(BF16)
+    out_ref[:, :rows, :] = jnp.broadcast_to(chunk[None], (out_ref.shape[0], rows, TILE))
+    tile = bias_tile(bias_sum(total[2 * rows :]))
+    out_ref[:, rows:, :] = jnp.broadcast_to(tile[None], (out_ref.shape[0], 8, TILE))
+
+
+def chunk_kernel(recv_ref, chunk_ref, bias_grad_ref, *, scale):
+    total = jnp.sum(recv_ref[...].astype(F32), axis=0) * scale
+    rows = total.shape[0] - 8
+    chunk_ref[...] = total[:rows]
+    bias_rows = bias_sum(total[rows:])
+    bias_grad_ref[:, :TILE] = bias_rows[0:1]
+    bias_grad_ref[:, TILE:] = bias_rows[1:2]
 
 
 def backward_kernel(from_ref, into_ref, tile_ref, *rest):
@@ -135,32 +149,18 @@
     for k, near_ref in enumerate(near_refs):
         rows[k * far : (k + 1) * far] = near_ref[:top].reshape(far, TILE, TILE)
     spread_tiles(from_ref, into_ref, tile_ref, rows, sums)
-    pieces = out_ref.shape[0]
-    out_ref[:, :TILE, :] = sums[...].astype(BF16)
-    total = near_refs[0][top:].astype(F32)
-    for near_ref in near_refs[1:]:
-        total = total + near_ref[top:].astype(F32)
-    count = (total.shape[0] - 16) // 2
-    chunk = (total[:count] + total[count : 2 * count]).astype(BF16)
-    out_ref[:, TILE : TILE + count, :] = jnp.broadcast_to(chunk[None], (pieces, count, TILE))
-    bias_rows = bias_tile(total[2 * count : 2 * count + 8] + total[2 * count + 8 :])
-    out_ref[:, TILE + count :, :] = jnp.broadcast_to(bias_rows[None], (pieces, 16, TILE))
-
-
-def input_kernel(recv_ref, input_ref, chunk_ref, bias_grad_ref, *, scale):
-    input_ref[...] = jnp.sum(recv_ref[:, :TILE, :].astype(F32), axis=0).astype(BF16)
-    total = jnp.sum(recv_ref[:, TILE:, :].astype(F32), axis=0) * scale
-    count = total.shape[0] - 16
-    chunk_ref[...] = jnp.broadcast_to(total[None, :count], chunk_ref.shape)
-    bias_rows = total[count : count + 8] + total[count + 8 :]
-    bias_grad_ref[:, :TILE] = bias_rows[0:1]
-    bias_grad_ref[:, TILE:] = bias_rows[1:2]
-
-
-def weight_kernel(recv_ref, weight_grad_ref):
-    half = recv_ref.shape[1] // 2
-    weight_grad_ref[:, :TILE] = recv_ref[:, :half, :].reshape(TILE, TILE)
-    weight_grad_ref[:, TILE:] = recv_ref[:, half:, :].reshape(TILE, TILE)
+    out_ref[...] = sums[...].astype(BF16)
+
+
+def weight_kernel(own_ref, *rest):
+    pair_refs, out_ref = rest[:-1], rest[-1]
+    rows = pair_refs[0].shape[1]
+    half = rows // 2
+    for k, pair_ref in enumerate(pair_refs):
+        for j in range(2):
+            start = pl.multiple_of((own_ref[0] ^ (2 * k + j)) * half, 8)
+            out_ref[pl.ds(start, half), :TILE] = pair_ref[j, :half, :]
+            out_ref[pl.ds(start, half), TILE:] = pair_ref[j, half:, :]
 
 
 def vmem(n):
@@ -189,8 +189,8 @@
     return jax.ShapeDtypeStruct(dims, dtype)
 
 
-def swap(array, step, near):
-    return lax.ppermute(array, NEAR, [(i, i ^ step) for i in range(near)])
+def swap(array, step, axis):
+    return lax.ppermute(array, axis, [(i, i ^ step) for i in range(lax.axis_size(axis))])
 
 
 def body(features, weight, bias, tile_index, edge_count, edge_pos, edge_weight, grad_out):
@@ -207,7 +207,9 @@
     target = index // dst
     source = index % dst
     target_near = (target // (2 * far)) * 2 + target % 2
-    place = (target_near ^ lax.axis_index(NEAR)) * far + (target // 2) % far
+    target_far = (target // 2) % far
+    place = target_near * far + target_far
+    back_place = (target_near ^ lax.axis_index(NEAR)) * far + target_far
     tile_shape = shape((slots, TILE, TILE), BF16)
     block = shape((far, TILE, TILE), BF16)
     pair_scratch = (pltpu.VMEM((slots // 2, 2 * edges), jnp.int32), pltpu.VMEM((slots // 2, 2 * edges), F32))
@@ -222,52 +224,58 @@
     sent = jnp.broadcast_to(features[None], (dst,) + features.shape)
     source_rows = lax.all_to_all(sent, "dst", 0, 0, tiled=True)
     tiles = build(positions, False)
-    own, *others = call(
-        forward_kernel,
-        "forward_tiles",
-        (shape(block.shape, F32),) + (block,) * (near - 1),
-        (source, place),
-        (tiles, source_rows),
-        (pltpu.VMEM((src, TILE, TILE), F32),),
-    )
-    others = [swap(other, k + 1, near) for k, other in enumerate(others)]
-    late_positions, own = lax.optimization_barrier((positions, own))
+    partial = call(
+        forward_kernel, "forward_tiles", shape((src, TILE, TILE), BF16), (source, place),
+        (tiles, source_rows), (pltpu.VMEM((src, TILE, TILE), F32),),
+    )
+    near_parts = lax.all_to_all(partial.reshape(near, far, TILE, TILE), NEAR, 0, 0, tiled=True)
+    late_positions, partial = lax.optimization_barrier((positions, partial))
     back_tiles = build(late_positions, True)
-    near_sums = call(add_kernel, "add_near", block, (), (own, *others))
+    near_sums = jnp.sum(near_parts.astype(F32), axis=0).astype(BF16)
     near_sums, back_tiles = lax.optimization_barrier((near_sums, back_tiles))
     parts = lax.all_to_all(near_sums, FAR, 0, 0, tiled=True)
-    extra = 2 * TILE // far + 16
+    rows = 2 * TILE // far
     hidden, send = call(
         dense_kernel,
         "dense_layer",
-        (shape(grad_out.shape, BF16), shape((far, TILE + extra, TILE), BF16)),
+        (shape(grad_out.shape, BF16), shape((far, TILE + rows + 8, TILE), BF16)),
         (),
         (parts, weight, bias.reshape(1, -1), grad_out),
     )
     far_rows = lax.all_to_all(send, FAR, 0, 0, tiled=True)
+    top = far * TILE
     near_rows = call(
-        middle_kernel, "middle_sums", shape((far * TILE + 2 * extra - 16, TILE), BF16), (), (far_rows,)
-    )
-    near_all = [near_rows] + [swap(near_rows, k, near) for k in range(1, near)]
+        middle_kernel, "middle_sums", shape((top + 2 * rows + 8, TILE), BF16), (), (far_rows,)
+    )
+    near_all = [near_rows] + [swap(near_rows, k, NEAR) for k in range(1, near)]
+    share = call(
+        share_kernel, "grad_share", shape((dst, rows + 8, TILE), BF16), (), [part[top:] for part in near_all]
+    )
+    shared = lax.all_to_all(share, "dst", 0, 0, tiled=True)
     back_send = call(
         backward_kernel,
         "backward_tiles",
-        shape((dst, TILE + extra, TILE), BF16),
-        (place, source),
+        shape((dst, TILE, TILE), BF16),
+        (back_place, source),
         (back_tiles, *near_all),
         (pltpu.VMEM((src, TILE, TILE), BF16), pltpu.VMEM((dst, TILE, TILE), F32)),
     )
+    shared, back_send = lax.optimization_barrier((shared, back_send))
     received = lax.all_to_all(back_send, "dst", 0, 0, tiled=True)
     node_scale = 1.0 / math.sqrt(features.shape[0] * src * dst)
-    input_grad, chunks, bias_grad = call(
-        lambda *refs: input_kernel(*refs, scale=node_scale),
-        "input_sums",
-        (shape(features.shape, BF16), shape((far, extra - 16, TILE), F32), shape((1, 2 * TILE), F32)),
+    chunk, bias_grad = call(
+        lambda *refs: chunk_kernel(*refs, scale=node_scale),
+        "grad_chunk",
+        (shape((rows, TILE), F32), shape((1, 2 * TILE), F32)),
         (),
-        (received,),
-    )
-    chunks = lax.all_to_all(chunks, FAR, 0, 0, tiled=True)
-    weight_grad = call(weight_kernel, "weight_rows", shape((TILE, 2 * TILE), F32), (), (chunks,))
+        (shared,),
+    )
+    pair = jnp.stack([chunk, swap(chunk, 1, FAR)])
+    pairs = [pair] + [swap(pair, k, FAR) for k in range(2, far, 2)]
+    weight_grad = call(
+        weight_kernel, "weight_rows", shape((TILE, 2 * TILE), F32), (lax.axis_index(FAR).reshape(1),), pairs
+    )
+    input_grad = jnp.sum(received.astype(F32), axis=0).astype(BF16)
     return (hidden, input_grad, weight_grad, bias_grad.reshape(-1))
 
 

time: 185 us -> 186 us (level)
  the two profiles are of different devices: /device:TPU:1 before, /device:TPU:24 now
where the time goes in v4:
time: 186 us; the launch traced here: 184 us
  blocking collectives  60.7 us (33%)
  starting transfers between devices  58.1 us (31%)
  Pallas kernels  36.3 us (20%)
  waiting for transfers between devices  18.1 us (10%)
  local copies, waits for them, and re-layouts  6.42 us (3%)
  other arithmetic  3.84 us (2%)
    pallas_call x9, Pallas kernels, call(): pl.pallas_call(kernel, out_shape=outs, in_specs=smem(len(scalars)) + vmem...  36.3 us
    all_to_all x1, blocking collectives, body(): parts = lax.all_to_all(near_sums, FAR, 0, 0, tiled=True)  33.8 us
    ppermute x7, starting transfers between devices, swap(): lax.ppermute(array, axis, [(i, i ^ step) for i in range(lax.axis_size(axi...  31.3 us
    all_to_all x1, blocking collectives, body(): far_rows = lax.all_to_all(send, FAR, 0, 0, tiled=True)  26.9 us
    ppermute x7, waiting for transfers between devices, swap(): lax.ppermute(array, axis, [(i, i ^ step) for i in range(lax.axis_size(axi...  10.7 us
    all_to_all x1, starting transfers between devices, body(): source_rows = lax.all_to_all(sent, 'dst', 0, 0, tiled=True)  7.28 us
    all_to_all x1, starting transfers between devices, body(): received = lax.all_to_all(back_send, 'dst', 0, 0, tiled=True)  7.24 us
    all_to_all x1, waiting for transfers between devices, body(): lax.all_to_all(partial.reshape(near, far, TILE, TILE), NEAR, 0, 0, tiled=...  7.06 us
  transfers between devices with their start and end apart: 11, of which 7 were waited for; matrix products, arithmetic and copies ran while one was open for 3% of the time, Pallas kernels for 13%

profile of v4, /device:TPU:24, one launch (start us, length us, event | category | flops | bytes accessed | tf_op | source)
XLA Modules:
  0.0 184.3 jit_solution(4493932500436337702)
XLA Ops:
  0.6 1.7 broadcast_in_dim.2
  2.3 7.3 %all-to-all-start = ((bf16[16,128,128]{2,1,0:T(8,128)(2,1)}), bf16[16,128,128]{2,1,0:T(8,128)(2,1)S(1)}, u32[]{:S(2)}, u32[]{:S(2)}) async-start(bf16[16,128,128]{2,1,0:T(8,128)(2,1)} %broadcast_in_dim.2), calls=%async_computation | async-start | bytes 1048576 | tf_op jit(solution)/shard_map/all_to_all | solution.py:225
  9.6 1.2 and_select_fusion.4
  10.7 6.7 %build_tiles.1.tile_ref = bf16[128,128,128]{2,1,0:T(8,128)(2,1)} custom-call(s32[128]{0:T(128)} %bitcast.35, s32[64,128]{1,0:T(8,128)} %bitcast.29, bf16[64,128]{1,0:T(8,128)(2,1)} %bitcast.31), custom_call_target="tpu_custom_call" | custom-call | tf_op jit(solution)/shard_map/build_tiles/pallas_call | solution.py:176
  17.4 0.5 multiply_add_fusion
  18.0 0.5 multiply_add_fusion.1.into_ref
  18.5 0.4 all-to-all-done.rows_ref
  18.9 0.8 copy-done
  19.7 7.3 %forward_tiles.1 = bf16[32,128,128]{2,1,0:T(8,128)(2,1)} custom-call(s32[128]{0:T(128)} %get-tuple-element.26.from_ref.into_ref, s32[128]{0:T(128)} %multiply_add_fusion.1.into_ref, bf16[128,128,128]{2,1,0:T(8,128)(2,1)} %build_tiles.1.tile_ref, bf16[16,128,128]{2,1,0:T(8,128)(2,1)} %copy-done), custom_call_target="tpu_custom_call" | custom-call | tf_op jit(solution)/shard_map/forward_tiles/pallas_call | solution.py:176
  27.0 6.1 %all-to-all-start.1 = ((bf16[4,8,128,128]{3,2,1,0:T(8,128)(2,1)}), bf16[4,8,128,128]{3,2,1,0:T(8,128)(2,1)S(1)}, u32[]{:S(2)}, u32[]{:S(2)}) async-start(bf16[4,8,128,128]{3,2,1,0:T(8,128)(2,1)} %bitcast.28), calls=%async_computation.1 | async-start | bytes 2097152 | tf_op jit(solution)/shard_map/all_to_all | solution.py:231
  33.1 6.8 %build_back.1.tile_ref = bf16[128,128,128]{2,1,0:T(8,128)(2,1)} custom-call(s32[128]{0:T(128)} %bitcast.36, s32[64,128]{1,0:T(8,128)} %bitcast.30, bf16[64,128]{1,0:T(8,128)(2,1)} %bitcast.32), custom_call_target="tpu_custom_call" | custom-call | tf_op jit(solution)/shard_map/build_back/pallas_call | solution.py:176
  39.8 7.1 %all-to-all-done.1 = bf16[4,8,128,128]{3,2,1,0:T(8,128)(2,1)S(1)} async-done(((bf16[4,8,128,128]{3,2,1,0:T(8,128)(2,1)}), bf16[4,8,128,128]{3,2,1,0:T(8,128)(2,1)S(1)}, u32[]{:S(2)}, u32[]{:S(2)}) %all-to-all-start.1) | async-done | bytes 1048608 | tf_op jit(solution)/shard_map/all_to_all | solution.py:231
  46.9 0.2 reduce_sum.24
  47.1 33.8 %all_to_all.30.recv_ref = bf16[8,128,128]{2,1,0:T(8,128)(2,1)} all-to-all(bf16[8,128,128]{2,1,0:T(8,128)(2,1)S(1)} %reduce_sum.24), channel_id=1, replica_groups=mesh['ylo'=2,'zq'=8,'z0'=2,'dst'=16] {'zq'}, dimensions={0} | all-to-all | bytes 524288 | tf_op jit(solution)/shard_map/all_to_all | solution.py:236
  80.9 2.1 %dense_layer.1 = (bf16[128,256]{1,0:T(8,128)(2,1)}, bf16[8,168,128]{2,1,0:T(8,128)(2,1)}) custom-call(bf16[8,128,128]{2,1,0:T(8,128)(2,1)} %all_to_all.30.recv_ref, bf16[128,256]{1,0:T(8,128)(2,1)} %weight_ref.1, f32[1,256]{1,0:T(1,128)} %bitcast.37, bf16[128,256]{1,0:T(8,128)(2,1)} %grad_ref.1), custom_call_target="tpu_custom_call" | custom-call | tf_op jit(solution)/shard_map/dense_layer/pallas_call | solution.py:176
  83.0 26.9 %all_to_all.31.recv_ref = bf16[8,168,128]{2,1,0:T(8,128)(2,1)} all-to-all(bf16[8,168,128]{2,1,0:T(8,128)(2,1)} %get-tuple-element.16), channel_id=1, replica_groups=mesh['ylo'=2,'zq'=8,'z0'=2,'dst'=16] {'zq'}, dimensions={0} | all-to-all | bytes 688128 | tf_op jit(solution)/shard_map/all_to_all | solution.py:245
  109.9 1.7 middle_sums.1.rest_0_
  111.6 4.1 %collective-permute-start.2 = (bf16[1096,128]{1,0:T(8,128)(2,1)}, bf16[1096,128]{1,0:T(8,128)(2,1)S(1)}, u32[]{:S(2)}, u32[]{:S(2)}) collective-permute-start(bf16[1096,128]{1,0:T(8,128)(2,1)} %middle_sums.1.rest_0_), channel_id=1, source_target_pairs={{0,272},{16,256},{256,16},{272,0},{1,273},{17,257},{257,17},{273,1... | collective-permute-start | bytes 841736 | tf_op jit(solution)/shard_map/ppermute | solution.py:193
  115.8 2.0 %collective-permute-start.1 = (bf16[1096,128]{1,0:T(8,128)(2,1)}, bf16[1096,128]{1,0:T(8,128)(2,1)S(1)}, u32[]{:S(2)}, u32[]{:S(2)}) collective-permute-start(bf16[1096,128]{1,0:T(8,128)(2,1)} %middle_sums.1.rest_0_), channel_id=1, source_target_pairs={{0,256},{16,272},{256,0},{272,16},{1,257},{17,273},{257,1},{273,17... | collective-permute-start | bytes 841736 | tf_op jit(solution)/shard_map/ppermute | solution.py:193
  117.8 3.4 %collective-permute-start = (bf16[1096,128]{1,0:T(8,128)(2,1)}, bf16[1096,128]{1,0:T(8,128)(2,1)S(1)}, u32[]{:S(2)}, u32[]{:S(2)}) collective-permute-start(bf16[1096,128]{1,0:T(8,128)(2,1)} %middle_sums.1.rest_0_), channel_id=1, source_target_pairs={{0,16},{16,0},{256,272},{272,256},{1,17},{17,1},{257,273},{273,257... | collective-permute-start | bytes 841736 | tf_op jit(solution)/shard_map/ppermute | solution.py:193
  121.2 1.3 slice.16.rest_0_
  122.5 0.0 collective-permute-done.2.rest_3_
  122.5 0.7 slice.19.rest_3_
  123.2 4.0 %collective-permute-done.1.rest_2_ = bf16[1096,128]{1,0:T(8,128)(2,1)S(1)} collective-permute-done((bf16[1096,128]{1,0:T(8,128)(2,1)}, bf16[1096,128]{1,0:T(8,128)(2,1)S(1)}, u32[]{:S(2)}, u32[]{:S(2)}) %collective-permute-start.1) | collective-permute-done | bytes 280608 | tf_op jit(solution)/shard_map/ppermute | solution.py:193
  127.2 0.7 slice.18.rest_2_
  127.9 0.2 collective-permute-done.rest_1_
  128.1 0.7 slice.17.rest_1_
  128.8 1.5 grad_share.1
  130.3 6.2 %all-to-all-start.4 = ((bf16[16,40,128]{2,1,0:T(8,128)(2,1)}), bf16[16,40,128]{2,1,0:T(8,128)(2,1)S(1)}, u32[]{:S(2)}, u32[]{:S(2)}) async-start(bf16[16,40,128]{2,1,0:T(8,128)(2,1)} %grad_share.1), calls=%async_computation.4 | async-start | bytes 327680 | tf_op jit(solution)/shard_map/all_to_all | solution.py:254
  136.5 7.2 %backward_tiles.1 = bf16[16,128,128]{2,1,0:T(8,128)(2,1)} custom-call(s32[128]{0:T(128)} %get-tuple-element.22.from_ref, s32[128]{0:T(128)} %get-tuple-element.26.from_ref.into_ref, bf16[128,128,128]{2,1,0:T(8,128)(2,1)} %build_back.1.tile_ref, bf16[1096,128]{1,0:T(8,128)(2,1)} %middle_sums.1.rest_0_, bf16[1096,128]{1,0:T(8,128)(2,1)} %copy-done.4, ...), custom_call_target="tpu_custom_call" | custom-call | tf_op jit(solution)/shard_map/backward_tiles/pallas_call | solution.py:176
  143.7 0.0 all-to-all-done.4.refs_0_
  143.7 7.2 %all-to-all-start.5 = ((bf16[16,128,128]{2,1,0:T(8,128)(2,1)}), bf16[16,128,128]{2,1,0:T(8,128)(2,1)S(1)}, u32[]{:S(2)}, u32[]{:S(2)}) async-start(bf16[16,128,128]{2,1,0:T(8,128)(2,1)} %backward_tiles.1), calls=%async_computation.5 | async-start | bytes 1048576 | tf_op jit(solution)/shard_map/all_to_all | solution.py:264
  151.0 1.6 grad_chunk.1
  152.5 4.8 %collective-permute-start.3 = (f32[32,128]{1,0:T(8,128)}, f32[32,128]{1,0:T(8,128)S(1)}, u32[]{:S(2)}, u32[]{:S(2)}) collective-permute-start(f32[32,128]{1,0:T(8,128)} %get-tuple-element.20), channel_id=1, source_target_pairs={{0,32},{32,0},{64,96},{96,64},{128,160},{160,128},{192,224},{224,1... | collective-permute-start | bytes 49160 | tf_op jit(solution)/shard_map/ppermute | solution.py:193
  157.3 2.0 %collective-permute-done.3 = f32[32,128]{1,0:T(8,128)S(1)} collective-permute-done((f32[32,128]{1,0:T(8,128)}, f32[32,128]{1,0:T(8,128)S(1)}, u32[]{:S(2)}, u32[]{:S(2)}) %collective-permute-start.3) | collective-permute-done | bytes 16416 | tf_op jit(solution)/shard_map/ppermute | solution.py:193
  159.3 0.7 pad_maximum_fusion.rest_0_
  160.1 3.6 %collective-permute-start.6 = (f32[2,32,128]{2,1,0:T(8,128)S(1)}, f32[2,32,128]{2,1,0:T(8,128)S(1)}, u32[]{:S(2)}, u32[]{:S(2)}) collective-permute-start(f32[2,32,128]{2,1,0:T(8,128)S(1)} %pad_maximum_fusion.rest_0_), channel_id=1, source_target_pairs={{0,192},{32,224},{64,128},{96,160},{128,64},{160,96},{192,0},{224,... | collective-permute-start | bytes 98312 | tf_op jit(solution)/shard_map/ppermute | solution.py:193
  163.7 6.4 %collective-permute-start.5 = (f32[2,32,128]{2,1,0:T(8,128)S(1)}, f32[2,32,128]{2,1,0:T(8,128)S(1)}, u32[]{:S(2)}, u32[]{:S(2)}) collective-permute-start(f32[2,32,128]{2,1,0:T(8,128)S(1)} %pad_maximum_fusion.rest_0_), channel_id=1, source_target_pairs={{0,128},{32,160},{64,192},{96,224},{128,0},{160,32},{192,64},{224,... | collective-permute-start | bytes 98312 | tf_op jit(solution)/shard_map/ppermute | solution.py:193
  170.1 7.0 %collective-permute-start.4 = (f32[2,32,128]{2,1,0:T(8,128)S(1)}, f32[2,32,128]{2,1,0:T(8,128)S(1)}, u32[]{:S(2)}, u32[]{:S(2)}) collective-permute-start(f32[2,32,128]{2,1,0:T(8,128)S(1)} %pad_maximum_fusion.rest_0_), channel_id=1, source_target_pairs={{0,64},{32,96},{64,0},{96,32},{128,192},{160,224},{192,128},{224,1... | collective-permute-start | bytes 98312 | tf_op jit(solution)/shard_map/ppermute | solution.py:193
  177.1 0.0 collective-permute-done.6.rest_3_
  177.1 0.0 copy-start.6
  177.1 1.5 collective-permute-done.5.rest_2_
  178.6 2.9 %collective-permute-done.4.rest_1_ = f32[2,32,128]{2,1,0:T(8,128)S(1)} collective-permute-done((f32[2,32,128]{2,1,0:T(8,128)S(1)}, f32[2,32,128]{2,1,0:T(8,128)S(1)}, u32[]{:S(2)}, u32[]{:S(2)}) %collective-permute-start.4) | collective-permute-done | bytes 32800 | tf_op jit(solution)/shard_map/ppermute | solution.py:193
  181.5 0.0 copy-done.5
  181.5 0.6 copy-done.8
  182.1 1.5 weight_rows.1
  183.6 0.0 all-to-all-done.5
  183.6 0.7 reduce_sum.25
  (14 shorter events, 0.0 us)
Async XLA Ops:
  2.3 16.6 %all-to-all-start = ((bf16[16,128,128]{2,1,0:T(8,128)(2,1)}), bf16[16,128,128]{2,1,0:T(8,128)(2,1)S(1)}, u32[]{:S(2)}, u32[]{:S(2)}) async-start(bf16[16,128,128]{2,1,0:T(8,128)(2,1)} %broadcast_in_dim.2), calls=%async_computation | async-start | bytes 1048576 | tf_op jit(solution)/shard_map/all_to_all | solution.py:225
  18.9 0.8 copy-start
  27.0 19.9 %all-to-all-start.1 = ((bf16[4,8,128,128]{3,2,1,0:T(8,128)(2,1)}), bf16[4,8,128,128]{3,2,1,0:T(8,128)(2,1)S(1)}, u32[]{:S(2)}, u32[]{:S(2)}) async-start(bf16[4,8,128,128]{3,2,1,0:T(8,128)(2,1)} %bitcast.28), calls=%async_computation.1 | async-start | bytes 2097152 | tf_op jit(solution)/shard_map/all_to_all | solution.py:231
  111.6 10.9 %collective-permute-start.2 = (bf16[1096,128]{1,0:T(8,128)(2,1)}, bf16[1096,128]{1,0:T(8,128)(2,1)S(1)}, u32[]{:S(2)}, u32[]{:S(2)}) collective-permute-start(bf16[1096,128]{1,0:T(8,128)(2,1)} %middle_sums.1.rest_0_), channel_id=1, source_target_pairs={{0,272},{16,256},{256,16},{272,0},{1,273},{17,257},{257,17},{273,1... | collective-permute-start | bytes 841736 | tf_op jit(solution)/shard_map/ppermute | solution.py:193
  115.8 11.4 %collective-permute-start.1 = (bf16[1096,128]{1,0:T(8,128)(2,1)}, bf16[1096,128]{1,0:T(8,128)(2,1)S(1)}, u32[]{:S(2)}, u32[]{:S(2)}) collective-permute-start(bf16[1096,128]{1,0:T(8,128)(2,1)} %middle_sums.1.rest_0_), channel_id=1, source_target_pairs={{0,256},{16,272},{256,0},{272,16},{1,257},{17,273},{257,1},{273,17... | collective-permute-start | bytes 841736 | tf_op jit(solution)/shard_map/ppermute | solution.py:193
  117.8 10.3 %collective-permute-start = (bf16[1096,128]{1,0:T(8,128)(2,1)}, bf16[1096,128]{1,0:T(8,128)(2,1)S(1)}, u32[]{:S(2)}, u32[]{:S(2)}) collective-permute-start(bf16[1096,128]{1,0:T(8,128)(2,1)} %middle_sums.1.rest_0_), channel_id=1, source_target_pairs={{0,16},{16,0},{256,272},{272,256},{1,17},{17,1},{257,273},{273,257... | collective-permute-start | bytes 841736 | tf_op jit(solution)/shard_map/ppermute | solution.py:193
  122.5 14.0 %copy-start.2 = (bf16[1096,128]{1,0:T(8,128)(2,1)}, bf16[1096,128]{1,0:T(8,128)(2,1)S(1)}, u32[]{:S(2)}) copy-start(bf16[1096,128]{1,0:T(8,128)(2,1)S(1)} %collective-permute-done.2.rest_3_) | copy-start | bytes 841732
  127.2 9.3 %copy-start.3 = (bf16[1096,128]{1,0:T(8,128)(2,1)}, bf16[1096,128]{1,0:T(8,128)(2,1)S(1)}, u32[]{:S(2)}) copy-start(bf16[1096,128]{1,0:T(8,128)(2,1)S(1)} %collective-permute-done.1.rest_2_) | copy-start | bytes 841732
  128.1 8.4 %copy-start.4 = (bf16[1096,128]{1,0:T(8,128)(2,1)}, bf16[1096,128]{1,0:T(8,128)(2,1)S(1)}, u32[]{:S(2)}) copy-start(bf16[1096,128]{1,0:T(8,128)(2,1)S(1)} %collective-permute-done.rest_1_) | copy-start | bytes 841732
  130.3 13.5 %all-to-all-start.4 = ((bf16[16,40,128]{2,1,0:T(8,128)(2,1)}), bf16[16,40,128]{2,1,0:T(8,128)(2,1)S(1)}, u32[]{:S(2)}, u32[]{:S(2)}) async-start(bf16[16,40,128]{2,1,0:T(8,128)(2,1)} %grad_share.1), calls=%async_computation.4 | async-start | bytes 327680 | tf_op jit(solution)/shard_map/all_to_all | solution.py:254
  143.7 7.2 %copy-start.1 = (bf16[16,40,128]{2,1,0:T(8,128)(2,1)}, bf16[16,40,128]{2,1,0:T(8,128)(2,1)S(1)}, u32[]{:S(2)}) copy-start(bf16[16,40,128]{2,1,0:T(8,128)(2,1)S(1)} %all-to-all-done.4.refs_0_) | copy-start | bytes 491524
  143.7 39.9 %all-to-all-start.5 = ((bf16[16,128,128]{2,1,0:T(8,128)(2,1)}), bf16[16,128,128]{2,1,0:T(8,128)(2,1)S(1)}, u32[]{:S(2)}, u32[]{:S(2)}) async-start(bf16[16,128,128]{2,1,0:T(8,128)(2,1)} %backward_tiles.1), calls=%async_computation.5 | async-start | bytes 1048576 | tf_op jit(solution)/shard_map/all_to_all | solution.py:264
  152.5 6.8 %collective-permute-start.3 = (f32[32,128]{1,0:T(8,128)}, f32[32,128]{1,0:T(8,128)S(1)}, u32[]{:S(2)}, u32[]{:S(2)}) collective-permute-start(f32[32,128]{1,0:T(8,128)} %get-tuple-element.20), channel_id=1, source_target_pairs={{0,32},{32,0},{64,96},{96,64},{128,160},{160,128},{192,224},{224,1... | collective-permute-start | bytes 49160 | tf_op jit(solution)/shard_map/ppermute | solution.py:193
  160.1 21.5 %copy-start.5 = (f32[2,32,128]{2,1,0:T(8,128)}, f32[2,32,128]{2,1,0:T(8,128)S(1)}, u32[]{:S(2)}) copy-start(f32[2,32,128]{2,1,0:T(8,128)S(1)} %pad_maximum_fusion.rest_0_) | copy-start | bytes 98308
  160.1 17.0 %collective-permute-start.6 = (f32[2,32,128]{2,1,0:T(8,128)S(1)}, f32[2,32,128]{2,1,0:T(8,128)S(1)}, u32[]{:S(2)}, u32[]{:S(2)}) collective-permute-start(f32[2,32,128]{2,1,0:T(8,128)S(1)} %pad_maximum_fusion.rest_0_), channel_id=1, source_target_pairs={{0,192},{32,224},{64,128},{96,160},{128,64},{160,96},{192,0},{224,... | collective-permute-start | bytes 98312 | tf_op jit(solution)/shard_map/ppermute | solution.py:193
  163.7 14.9 %collective-permute-start.5 = (f32[2,32,128]{2,1,0:T(8,128)S(1)}, f32[2,32,128]{2,1,0:T(8,128)S(1)}, u32[]{:S(2)}, u32[]{:S(2)}) collective-permute-start(f32[2,32,128]{2,1,0:T(8,128)S(1)} %pad_maximum_fusion.rest_0_), channel_id=1, source_target_pairs={{0,128},{32,160},{64,192},{96,224},{128,0},{160,32},{192,64},{224,... | collective-permute-start | bytes 98312 | tf_op jit(solution)/shard_map/ppermute | solution.py:193
  170.1 11.4 %collective-permute-start.4 = (f32[2,32,128]{2,1,0:T(8,128)S(1)}, f32[2,32,128]{2,1,0:T(8,128)S(1)}, u32[]{:S(2)}, u32[]{:S(2)}) collective-permute-start(f32[2,32,128]{2,1,0:T(8,128)S(1)} %pad_maximum_fusion.rest_0_), channel_id=1, source_target_pairs={{0,64},{32,96},{64,0},{96,32},{128,192},{160,224},{192,128},{224,1... | collective-permute-start | bytes 98312 | tf_op jit(solution)/shard_map/ppermute | solution.py:193
  177.1 4.4 %copy-start.6 = (f32[2,32,128]{2,1,0:T(8,128)}, f32[2,32,128]{2,1,0:T(8,128)S(1)}, u32[]{:S(2)}) copy-start(f32[2,32,128]{2,1,0:T(8,128)S(1)} %collective-permute-done.6.rest_3_) | copy-start | bytes 98308
  178.6 2.9 %copy-start.7 = (f32[2,32,128]{2,1,0:T(8,128)}, f32[2,32,128]{2,1,0:T(8,128)S(1)}, u32[]{:S(2)}) copy-start(f32[2,32,128]{2,1,0:T(8,128)S(1)} %collective-permute-done.5.rest_2_) | copy-start | bytes 98308
  181.5 0.6 copy-start.8

commit v5 on v4

v5 whole, which is shorter than its diff:
```python
import math

import jax
import jax.numpy as jnp
from jax import lax
from jax.experimental import pallas as pl
from jax.experimental.pallas import tpu as pltpu
from jax.sharding import Mesh, PartitionSpec as P

TILE = 128
BF16 = jnp.bfloat16
F32 = jnp.float32
NN = (((1,), (0,)), ((), ()))
NT = (((1,), (1,)), ((), ()))
TN = (((0,), (0,)), ((), ()))
SRC = ("ylo", "zq", "z0")
NEAR = ("ylo", "z0")
FAR = "zq"
GROUP = 16
BLOCKS = 2


def dot(a, b, dims=NN):
    return lax.dot_general(a, b, dims, preferred_element_type=F32)


def build_kernel(count_ref, pos_ref, weight_ref, tile_ref, pos_pairs, weight_pairs, *, backward):
    edges, slots = pos_ref.shape
    pairs = slots // 2
    positions = pos_ref[...].T
    weights = weight_ref[...].astype(F32).T
    pos_pairs[...] = jnp.concatenate([positions[:pairs], positions[pairs:]], axis=1)
    weight_pairs[...] = jnp.concatenate([weights[:pairs], weights[pairs:]], axis=1)
    lane = lax.broadcasted_iota(jnp.int32, (1, 2 * edges), 1)
    second = lane >= edges
    half = jnp.where(second, TILE, 0)
    one_rows = lax.broadcasted_iota(jnp.int32, (TILE, 2 * edges), 0)
    two_rows = lax.broadcasted_iota(jnp.int32, (2 * TILE, 2 * edges), 0)

    def one_pair(i, carry):
        limit = jnp.where(second, count_ref[i + pairs] + edges, count_ref[i])
        position = pos_pairs[pl.ds(i, 1), :]
        values = jnp.where(lane < limit, weight_pairs[pl.ds(i, 1), :], 0.0)
        row = position >> 7
        col = position & (TILE - 1)
        if backward:
            left = jnp.where(one_rows == col, 1.0, 0.0).astype(BF16)
            right = jnp.where(two_rows == row + half, values, 0.0).astype(BF16)
        else:
            left = jnp.where(one_rows == row, values, 0.0).astype(BF16)
            right = jnp.where(two_rows == col + half, 1.0, 0.0).astype(BF16)
        both = dot(left, right, NT).astype(BF16)
        tile_ref[i] = both[:, :TILE]
        tile_ref[i + pairs] = both[:, TILE:]
        return carry

    lax.fori_loop(0, pairs, one_pair, 0, unroll=4)


def spread_tiles(index_ref, tile_ref, rows_ref, sums, split, backward):
    block = tile_ref.shape[0]
    step = pl.program_id(0)
    shift = split.bit_length() - 1
    for start in range(0, block, GROUP):
        found = []
        for i in range(start, start + GROUP):
            index = index_ref[step * block + i]
            target = index >> shift
            source = index & (split - 1)
            if backward:
                found.append((source, dot(tile_ref[i], rows_ref[target])))
            else:
                found.append((target, dot(tile_ref[i], rows_ref[source])))
        for place, value in found:
            sums[place] = sums[place] + value


def forward_kernel(index_ref, tile_ref, rows_ref, out_ref, sums):
    near, far = out_ref.shape[:2]
    step = pl.program_id(0)

    @pl.when(step == 0)
    def _():
        sums[...] = jnp.zeros_like(sums)

    spread_tiles(index_ref, tile_ref, rows_ref, sums, rows_ref.shape[0], False)

    @pl.when(step == pl.num_programs(0) - 1)
    def _():
        for target in range(sums.shape[0]):
            place = target // (2 * far) * 2 + target % 2
            out_ref[place, target // 2 % far] = sums[target].astype(BF16)


def high_low(value):
    high = value.astype(BF16).astype(F32)
    return high, value - high


def bias_tile(bias_rows):
    high, low = high_low(bias_rows[0:2])
    return jnp.concatenate([high, low, jnp.zeros((4, TILE), F32)], axis=0).astype(BF16)


def bias_sum(tile):
    return tile[0:2] + tile[2:4]


def dense_kernel(agg_ref, weight_ref, bias_ref, grad_ref, hidden_ref, send_ref):
    peers = send_ref.shape[0]
    aggregated = agg_ref[...]
    weight = weight_ref[...]
    preact = dot(aggregated, weight) + bias_ref[...]
    sigma = 1.0 / (1.0 + jnp.exp(-preact))
    hidden_ref[...] = (preact * sigma).astype(BF16)
    grad_pre = (grad_ref[...].astype(F32) * sigma * (1.0 + preact * (1.0 - sigma))).astype(BF16)
    back_rows = dot(grad_pre, weight, NT).astype(BF16)
    send_ref[:, :TILE, :] = jnp.broadcast_to(back_rows[None], (peers, TILE, TILE))
    part = dot(aggregated, grad_pre, TN).astype(BF16)
    rows = TILE // peers
    send_ref[:, TILE : TILE + rows, :] = part[:, :TILE].reshape(peers, rows, TILE)
    send_ref[:, TILE + rows : TILE + 2 * rows, :] = part[:, TILE:].reshape(peers, rows, TILE)
    bias_part = jnp.sum(grad_pre.astype(F32), axis=0, keepdims=True)
    bias_rows = jnp.concatenate([bias_part[:, :TILE], bias_part[:, TILE:]], axis=0)
    send_ref[:, TILE + 2 * rows :, :] = jnp.broadcast_to(bias_tile(bias_rows)[None], (peers, 8, TILE))


def middle_kernel(recv_ref, out_ref):
    near = out_ref.shape[0]
    peers = recv_ref.shape[0]
    top = peers * TILE
    back_rows = recv_ref[:, :TILE, :].reshape(top, TILE)
    total = jnp.sum(recv_ref[:, TILE:, :].astype(F32), axis=0)
    rows = total.shape[0] - 8
    high, low = high_low(total[:rows])
    tile = bias_tile(bias_sum(total[rows:]))
    extra = jnp.concatenate([high.astype(BF16), low.astype(BF16), tile], axis=0)
    for k in range(near):
        out_ref[k, :top] = back_rows
        out_ref[k, top:] = extra


def backward_kernel(index_ref, tile_ref, recv_ref, out_ref, rows, sums):
    near = recv_ref.shape[0]
    far = rows.shape[0] // near
    top = far * TILE
    pieces = out_ref.shape[0]
    step = pl.program_id(0)

    @pl.when(step == 0)
    def _():
        sums[...] = jnp.zeros_like(sums)
        for target in range(near * far):
            start = target // 2 % far * TILE
            rows[target] = recv_ref[target // (2 * far) * 2 + target % 2, start : start + TILE]

    spread_tiles(index_ref, tile_ref, rows, sums, pieces, True)

    @pl.when(step == pl.num_programs(0) - 1)
    def _():
        out_ref[:, :TILE, :] = sums[...].astype(BF16)
        total = jnp.sum(recv_ref[:, top:, :].astype(F32), axis=0)
        count = (total.shape[0] - 8) // 2
        chunk = (total[:count] + total[count : 2 * count]).astype(BF16)
        out_ref[:, TILE : TILE + count, :] = jnp.broadcast_to(chunk[None], (pieces, count, TILE))
        tile = bias_tile(bias_sum(total[2 * count :]))
        out_ref[:, TILE + count :, :] = jnp.broadcast_to(tile[None], (pieces, 8, TILE))


def vmem(n):
    return [pl.BlockSpec(memory_space=pltpu.VMEM)] * n


def smem(n):
    return [pl.BlockSpec(memory_space=pltpu.SMEM)] * n


def call(kernel, name, outs, scalars, arrays, scratch=(), **more):
    single = not isinstance(outs, tuple)
    return pl.pallas_call(
        kernel,
        out_shape=outs,
        in_specs=smem(len(scalars)) + vmem(len(arrays)),
        out_specs=vmem(1)[0] if single else tuple(vmem(len(outs))),
        scratch_shapes=list(scratch),
        compiler_params=pltpu.CompilerParams(vmem_limit_bytes=56 << 20),
        name=name,
        **more,
    )(*scalars, *arrays)


def shape(dims, dtype):
    return jax.ShapeDtypeStruct(dims, dtype)


def spread(kernel, name, out, index, tiles, rows, scratch):
    whole = lambda a: pl.BlockSpec(a.shape, lambda i, n=len(a.shape): (0,) * n)
    block = tiles.shape[0] // BLOCKS
    return pl.pallas_call(
        kernel,
        out_shape=out,
        grid=(BLOCKS,),
        in_specs=smem(1) + [pl.BlockSpec((block, TILE, TILE), lambda i: (i, 0, 0)), whole(rows)],
        out_specs=whole(out),
        scratch_shapes=scratch,
        compiler_params=pltpu.CompilerParams(
            vmem_limit_bytes=56 << 20, dimension_semantics=("arbitrary",)
        ),
        name=name,
    )(index, tiles, rows)


def body(features, weight, bias, tile_index, edge_count, edge_pos, edge_weight, grad_out):
    near = lax.axis_size(NEAR)
    far = lax.axis_size(FAR)
    src = near * far
    dst = lax.axis_size("dst")
    index = tile_index.reshape(-1)
    counts = edge_count.reshape(-1)
    slots = counts.shape[0]
    positions = edge_pos.reshape(slots, -1).T
    weights = edge_weight.reshape(slots, -1).T
    edges = positions.shape[0]
    tile_shape = shape((slots, TILE, TILE), BF16)
    pair_scratch = (pltpu.VMEM((slots // 2, 2 * edges), jnp.int32), pltpu.VMEM((slots // 2, 2 * edges), F32))

    def build(positions, backward):
        return call(
            lambda *refs: build_kernel(*refs, backward=backward),
            "build_back" if backward else "build_tiles",
            tile_shape, (counts,), (positions, weights), pair_scratch,
        )

    sent = jnp.broadcast_to(features[None], (dst,) + features.shape)
    source_rows = lax.all_to_all(sent, "dst", 0, 0, tiled=True)
    tiles = build(positions, False)
    partial = spread(
        forward_kernel, "forward_tiles", shape((near, far, TILE, TILE), BF16),
        index, tiles, source_rows, [pltpu.VMEM((src, TILE, TILE), F32)],
    )
    near_parts = lax.all_to_all(partial, NEAR, 0, 0, tiled=True)
    late_positions, partial = lax.optimization_barrier((positions, partial))
    back_tiles = build(late_positions, True)
    near_sums = jnp.sum(near_parts.astype(F32), axis=0).astype(BF16)
    near_sums, back_tiles = lax.optimization_barrier((near_sums, back_tiles))
    parts = lax.all_to_all(near_sums, FAR, 0, 0, tiled=True)
    aggregated = jnp.sum(parts.astype(F32), axis=0).astype(BF16)
    rows = 2 * TILE // far
    hidden, send = call(
        dense_kernel,
        "dense_layer",
        (shape(grad_out.shape, BF16), shape((far, TILE + rows + 8, TILE), BF16)),
        (),
        (aggregated, weight, bias.reshape(1, -1), grad_out),
    )
    far_rows = lax.all_to_all(send, FAR, 0, 0, tiled=True)
    near_rows = call(
        middle_kernel, "middle_sums", shape((near, far * TILE + 2 * rows + 8, TILE), BF16), (), (far_rows,)
    )
    near_rows = lax.all_to_all(near_rows, NEAR, 0, 0, tiled=True)
    back_send = spread(
        backward_kernel, "backward_tiles", shape((dst, TILE + rows + 8, TILE), BF16),
        index, back_tiles, near_rows,
        [pltpu.VMEM((src, TILE, TILE), BF16), pltpu.VMEM((dst, TILE, TILE), F32)],
    )
    received = lax.all_to_all(back_send, "dst", 0, 0, tiled=True)
    node_scale = 1.0 / math.sqrt(features.shape[0] * src * dst)
    extra = jnp.sum(received[:, TILE:, :].astype(F32), axis=0) * node_scale
    chunk = jnp.concatenate([extra[: rows // 2], extra[rows // 2 : rows]], axis=1).astype(BF16)
    chunks = lax.all_to_all(jnp.broadcast_to(chunk[None], (far,) + chunk.shape), FAR, 0, 0, tiled=True)
    weight_grad = chunks.reshape(TILE, 2 * TILE).astype(F32)
    bias_grad = bias_sum(extra[rows:]).reshape(-1)
    input_grad = jnp.sum(received[:, :TILE, :].astype(F32), axis=0).astype(BF16)
    return (hidden, input_grad, weight_grad, bias_grad)


def solution(mesh):
    src, dst = mesh.devices.shape
    fine = Mesh(mesh.devices.reshape(2, src // 4, 2, dst), ("ylo", "zq", "z0", "dst"))
    rows = P(("ylo", "zq", "z0", "dst"), None)
    placed = (
        rows,
        P(),
        P(),
        P(SRC, "dst", None),
        P(SRC, "dst", None),
        P(SRC, "dst", None, None),
        P(SRC, "dst", None, None),
        rows,
    )
    return jax.shard_map(
        body, mesh=fine, in_specs=placed, out_specs=(rows, rows, P(), P()), check_vma=False
    )
```

time: 186 us -> 171 us (0.919)
  the two profiles are of different devices: /device:TPU:24 before, /device:TPU:1 now
where the time goes in v5:
time: 171 us; the launch traced here: 170 us
  blocking collectives  96.2 us (56%)
  Pallas kernels  26.9 us (16%)
  waiting for transfers between devices  21.5 us (13%)
  starting transfers between devices  18.4 us (11%)
  local copies, waits for them, and re-layouts  3.1 us (2%)
  other arithmetic  2.82 us (2%)
    all_to_all x1, blocking collectives, body(): parts = lax.all_to_all(near_sums, FAR, 0, 0, tiled=True)  29.7 us
    all_to_all x1, blocking collectives, body(): received = lax.all_to_all(back_send, 'dst', 0, 0, tiled=True)  27.8 us
    all_to_all x1, blocking collectives, body(): far_rows = lax.all_to_all(send, FAR, 0, 0, tiled=True)  24.8 us
    pallas_call x4, Pallas kernels, call(): pl.pallas_call(kernel, out_shape=outs, in_specs=smem(len(scalars)) + vmem...  17.6 us
    all_to_all x1, blocking collectives, body(): near_rows = lax.all_to_all(near_rows, NEAR, 0, 0, tiled=True)  13.9 us
    all_to_all x1, waiting for transfers between devices, body(): lax.all_to_all(jnp.broadcast_to(chunk[None], (far,) + chunk.shape), FAR,...  10.7 us
    all_to_all x1, starting transfers between devices, body(): source_rows = lax.all_to_all(sent, 'dst', 0, 0, tiled=True)  10.2 us
    pallas_call x2, Pallas kernels, spread(): pl.pallas_call(kernel, out_shape=out, grid=(BLOCKS,), in_specs=smem(1) +...  9.26 us
  transfers between devices with their start and end apart: 3, of which 3 were waited for; matrix products, arithmetic and copies ran while one was open for 1% of the time, Pallas kernels for 8%

profile of v5, /device:TPU:1, one launch (start us, length us, event | category | flops | bytes accessed | tf_op | source)
XLA Modules:
  0.0 169.6 jit_solution(12161459936771523629)
XLA Ops:
  0.6 1.7 broadcast_in_dim.4
  2.3 10.2 %all-to-all-start = ((bf16[16,128,128]{2,1,0:T(8,128)(2,1)}), bf16[16,128,128]{2,1,0:T(8,128)(2,1)S(1)}, u32[]{:S(2)}, u32[]{:S(2)}) async-start(bf16[16,128,128]{2,1,0:T(8,128)(2,1)} %broadcast_in_dim.4), calls=%async_computation | async-start | bytes 1048576 | tf_op jit(solution)/shard_map/all_to_all | solution.py:235
  12.5 6.7 %build_tiles.1.tile_ref = bf16[128,128,128]{2,1,0:T(8,128)(2,1)} custom-call(s32[128]{0:T(128)} %bitcast.18, s32[64,128]{1,0:T(8,128)} %bitcast.14, bf16[64,128]{1,0:T(8,128)(2,1)} %bitcast.16), custom_call_target="tpu_custom_call" | custom-call | tf_op jit(solution)/shard_map/build_tiles/pallas_call | solution.py:180
  19.2 4.5 %all-to-all-done.rows_ref = bf16[16,128,128]{2,1,0:T(8,128)(2,1)S(1)} async-done(((bf16[16,128,128]{2,1,0:T(8,128)(2,1)}), bf16[16,128,128]{2,1,0:T(8,128)(2,1)S(1)}, u32[]{:S(2)}, u32[]{:S(2)}) %all-to-all-start) | async-done | bytes 524320 | tf_op jit(solution)/shard_map/all_to_all | solution.py:235
  23.7 0.0 copy-start
  23.7 0.8 copy-done
  24.5 4.6 %forward_tiles.1 = bf16[4,8,128,128]{3,2,1,0:T(8,128)(2,1)} custom-call(s32[128]{0:T(128)} %bitcast.20, bf16[128,128,128]{2,1,0:T(8,128)(2,1)} %build_tiles.1.tile_ref, bf16[16,128,128]{2,1,0:T(8,128)(2,1)} %copy-done), custom_call_target="tpu_custom_call" | custom-call | tf_op jit(solution)/shard_map/forward_tiles/pallas_call | solution.py:199
  29.1 3.5 %all-to-all-start.1 = ((bf16[4,8,128,128]{3,2,1,0:T(8,128)(2,1)}), bf16[4,8,128,128]{3,2,1,0:T(8,128)(2,1)S(1)}, u32[]{:S(2)}, u32[]{:S(2)}) async-start(bf16[4,8,128,128]{3,2,1,0:T(8,128)(2,1)} %forward_tiles.1), calls=%async_computation.1 | async-start | bytes 2097152 | tf_op jit(solution)/shard_map/all_to_all | solution.py:241
  32.6 6.7 %build_back.1.tile_ref = bf16[128,128,128]{2,1,0:T(8,128)(2,1)} custom-call(s32[128]{0:T(128)} %bitcast.19, s32[64,128]{1,0:T(8,128)} %bitcast.15, bf16[64,128]{1,0:T(8,128)(2,1)} %bitcast.17), custom_call_target="tpu_custom_call" | custom-call | tf_op jit(solution)/shard_map/build_back/pallas_call | solution.py:180
  39.4 6.3 %all-to-all-done.1 = bf16[4,8,128,128]{3,2,1,0:T(8,128)(2,1)S(1)} async-done(((bf16[4,8,128,128]{3,2,1,0:T(8,128)(2,1)}), bf16[4,8,128,128]{3,2,1,0:T(8,128)(2,1)S(1)}, u32[]{:S(2)}, u32[]{:S(2)}) %all-to-all-start.1) | async-done | bytes 1048608 | tf_op jit(solution)/shard_map/all_to_all | solution.py:241
  45.7 0.2 reduce_sum.45
  45.9 29.7 %all_to_all.35 = bf16[8,128,128]{2,1,0:T(8,128)(2,1)S(1)} all-to-all(bf16[8,128,128]{2,1,0:T(8,128)(2,1)S(1)} %reduce_sum.45), channel_id=1, replica_groups=mesh['ylo'=2,'zq'=8,'z0'=2,'dst'=16] {'zq'}, dimensions={0} | all-to-all | bytes 524288 | tf_op jit(solution)/shard_map/all_to_all | solution.py:246
  75.6 0.7 reduce_sum.46.agg_ref
  76.2 2.0 %dense_layer.1 = (bf16[128,256]{1,0:T(8,128)(2,1)}, bf16[8,168,128]{2,1,0:T(8,128)(2,1)}) custom-call(bf16[128,128]{1,0:T(8,128)(2,1)} %reduce_sum.46.agg_ref, bf16[128,256]{1,0:T(8,128)(2,1)} %weight_ref.1, f32[1,256]{1,0:T(1,128)} %bitcast.22, bf16[128,256]{1,0:T(8,128)(2,1)} %grad_ref.1), custom_call_target="tpu_custom_call" | custom-call | tf_op jit(solution)/shard_map/dense_layer/pallas_call | solution.py:180
  78.2 24.8 %all_to_all.36.recv_ref = bf16[8,168,128]{2,1,0:T(8,128)(2,1)} all-to-all(bf16[8,168,128]{2,1,0:T(8,128)(2,1)} %get-tuple-element.13), channel_id=1, replica_groups=mesh['ylo'=2,'zq'=8,'z0'=2,'dst'=16] {'zq'}, dimensions={0} | all-to-all | bytes 688128 | tf_op jit(solution)/shard_map/all_to_all | solution.py:256
  103.0 2.2 %middle_sums.1 = bf16[4,1096,128]{2,1,0:T(8,128)(2,1)} custom-call(bf16[8,168,128]{2,1,0:T(8,128)(2,1)} %all_to_all.36.recv_ref), custom_call_target="tpu_custom_call" | custom-call | tf_op jit(solution)/shard_map/middle_sums/pallas_call | solution.py:180
  105.2 13.9 %all_to_all.37.recv_ref = bf16[4,1096,128]{2,1,0:T(8,128)(2,1)} all-to-all(bf16[4,1096,128]{2,1,0:T(8,128)(2,1)} %middle_sums.1), channel_id=1, replica_groups=mesh['ylo'=2,'zq'=8,'z0'=2,'dst'=16] {'ylo','z0'}, dimensions={0} | all-to-all | bytes 2244608 | tf_op jit(solution)/shard_map/all_to_all | solution.py:260
  119.1 4.7 %backward_tiles.1 = bf16[16,168,128]{2,1,0:T(8,128)(2,1)} custom-call(s32[128]{0:T(128)} %bitcast.21, bf16[128,128,128]{2,1,0:T(8,128)(2,1)} %build_back.1.tile_ref, bf16[4,1096,128]{2,1,0:T(8,128)(2,1)} %all_to_all.37.recv_ref), custom_call_target="tpu_custom_call" | custom-call | tf_op jit(solution)/shard_map/backward_tiles/pallas_call | solution.py:199
  123.8 27.8 %all_to_all.38 = bf16[16,168,128]{2,1,0:T(8,128)(2,1)S(1)} all-to-all(bf16[16,168,128]{2,1,0:T(8,128)(2,1)} %backward_tiles.1), channel_id=1, replica_groups=mesh['ylo'=2,'zq'=8,'z0'=2,'dst'=16] {'dst'}, dimensions={0} | all-to-all | bytes 1376256 | tf_op jit(solution)/shard_map/all_to_all | solution.py:266
  151.7 0.6 broadcast_in_dim.5
  152.3 4.7 %all-to-all-start.6 = ((bf16[8,16,256]{2,1,0:T(8,128)(2,1)}), bf16[8,16,256]{2,1,0:T(8,128)(2,1)S(1)}, u32[]{:S(2)}, u32[]{:S(2)}) async-start(bf16[8,16,256]{2,1,0:T(8,128)(2,1)} %broadcast_in_dim.5), calls=%async_computation.6 | async-start | bytes 131072 | tf_op jit(solution)/shard_map/all_to_all | solution.py:270
  157.0 0.7 slice_reduce_fusion
  157.7 0.6 fusion
  158.2 10.7 %all-to-all-done.6 = bf16[8,16,256]{2,1,0:T(8,128)(2,1)S(1)} async-done(((bf16[8,16,256]{2,1,0:T(8,128)(2,1)}), bf16[8,16,256]{2,1,0:T(8,128)(2,1)S(1)}, u32[]{:S(2)}, u32[]{:S(2)}) %all-to-all-start.6) | async-done | bytes 65568 | tf_op jit(solution)/shard_map/all_to_all | solution.py:270
  168.9 0.7 bitcast_convert_fusion
  (4 shorter events, 0.0 us)
Async XLA Ops:
  2.3 21.4 %all-to-all-start = ((bf16[16,128,128]{2,1,0:T(8,128)(2,1)}), bf16[16,128,128]{2,1,0:T(8,128)(2,1)S(1)}, u32[]{:S(2)}, u32[]{:S(2)}) async-start(bf16[16,128,128]{2,1,0:T(8,128)(2,1)} %broadcast_in_dim.4), calls=%async_computation | async-start | bytes 1048576 | tf_op jit(solution)/shard_map/all_to_all | solution.py:235
  23.7 0.8 copy-start
  29.1 16.6 %all-to-all-start.1 = ((bf16[4,8,128,128]{3,2,1,0:T(8,128)(2,1)}), bf16[4,8,128,128]{3,2,1,0:T(8,128)(2,1)S(1)}, u32[]{:S(2)}, u32[]{:S(2)}) async-start(bf16[4,8,128,128]{3,2,1,0:T(8,128)(2,1)} %forward_tiles.1), calls=%async_computation.1 | async-start | bytes 2097152 | tf_op jit(solution)/shard_map/all_to_all | solution.py:241
  152.3 16.6 %all-to-all-start.6 = ((bf16[8,16,256]{2,1,0:T(8,128)(2,1)}), bf16[8,16,256]{2,1,0:T(8,128)(2,1)S(1)}, u32[]{:S(2)}, u32[]{:S(2)}) async-start(bf16[8,16,256]{2,1,0:T(8,128)(2,1)} %broadcast_in_dim.5), calls=%async_computation.6 | async-start | bytes 131072 | tf_op jit(solution)/shard_map/all_to_all | solution.py:270

commit v6 on v5

--- a/solution.py
+++ b/solution.py
@@ -16,8 +16,7 @@
 SRC = ("ylo", "zq", "z0")
 NEAR = ("ylo", "z0")
 FAR = "zq"
-GROUP = 16
-BLOCKS = 2
+GROUP = 32
 
 
 def dot(a, b, dims=NN):
@@ -58,38 +57,33 @@
 
 
 def spread_tiles(index_ref, tile_ref, rows_ref, sums, split, backward):
-    block = tile_ref.shape[0]
-    step = pl.program_id(0)
     shift = split.bit_length() - 1
-    for start in range(0, block, GROUP):
+    sums[...] = jnp.zeros_like(sums)
+
+    def one_step(step, carry):
         found = []
-        for i in range(start, start + GROUP):
-            index = index_ref[step * block + i]
+        for i in range(GROUP):
+            slot = step * GROUP + i
+            index = index_ref[slot]
             target = index >> shift
             source = index & (split - 1)
             if backward:
-                found.append((source, dot(tile_ref[i], rows_ref[target])))
+                found.append((source, dot(tile_ref[slot], rows_ref[target])))
             else:
-                found.append((target, dot(tile_ref[i], rows_ref[source])))
+                found.append((target, dot(tile_ref[slot], rows_ref[source])))
         for place, value in found:
             sums[place] = sums[place] + value
+        return carry
+
+    lax.fori_loop(0, tile_ref.shape[0] // GROUP, one_step, 0)
 
 
 def forward_kernel(index_ref, tile_ref, rows_ref, out_ref, sums):
     near, far = out_ref.shape[:2]
-    step = pl.program_id(0)
-
-    @pl.when(step == 0)
-    def _():
-        sums[...] = jnp.zeros_like(sums)
-
     spread_tiles(index_ref, tile_ref, rows_ref, sums, rows_ref.shape[0], False)
-
-    @pl.when(step == pl.num_programs(0) - 1)
-    def _():
-        for target in range(sums.shape[0]):
-            place = target // (2 * far) * 2 + target % 2
-            out_ref[place, target // 2 % far] = sums[target].astype(BF16)
+    for target in range(near * far):
+        place = target // (2 * far) * 2 + target % 2
+        out_ref[place, target // 2 % far] = sums[target].astype(BF16)
 
 
 def high_low(value):
@@ -145,26 +139,17 @@
     far = rows.shape[0] // near
     top = far * TILE
     pieces = out_ref.shape[0]
-    step = pl.program_id(0)
-
-    @pl.when(step == 0)
-    def _():
-        sums[...] = jnp.zeros_like(sums)
-        for target in range(near * far):
-            start = target // 2 % far * TILE
-            rows[target] = recv_ref[target // (2 * far) * 2 + target % 2, start : start + TILE]
-
+    for target in range(near * far):
+        start = target // 2 % far * TILE
+        rows[target] = recv_ref[target // (2 * far) * 2 + target % 2, start : start + TILE]
     spread_tiles(index_ref, tile_ref, rows, sums, pieces, True)
-
-    @pl.when(step == pl.num_programs(0) - 1)
-    def _():
-        out_ref[:, :TILE, :] = sums[...].astype(BF16)
-        total = jnp.sum(recv_ref[:, top:, :].astype(F32), axis=0)
-        count = (total.shape[0] - 8) // 2
-        chunk = (total[:count] + total[count : 2 * count]).astype(BF16)
-        out_ref[:, TILE : TILE + count, :] = jnp.broadcast_to(chunk[None], (pieces, count, TILE))
-        tile = bias_tile(bias_sum(total[2 * count :]))
-        out_ref[:, TILE + count :, :] = jnp.broadcast_to(tile[None], (pieces, 8, TILE))
+    out_ref[:, :TILE, :] = sums[...].astype(BF16)
+    total = jnp.sum(recv_ref[:, top:, :].astype(F32), axis=0)
+    count = (total.shape[0] - 8) // 2
+    chunk = (total[:count] + total[count : 2 * count]).astype(BF16)
+    out_ref[:, TILE : TILE + count, :] = jnp.broadcast_to(chunk[None], (pieces, count, TILE))
+    tile = bias_tile(bias_sum(total[2 * count :]))
+    out_ref[:, TILE + count :, :] = jnp.broadcast_to(tile[None], (pieces, 8, TILE))
 
 
 def vmem(n):
@@ -183,7 +168,7 @@
         in_specs=smem(len(scalars)) + vmem(len(arrays)),
         out_specs=vmem(1)[0] if single else tuple(vmem(len(outs))),
         scratch_shapes=list(scratch),
-        compiler_params=pltpu.CompilerParams(vmem_limit_bytes=56 << 20),
+        compiler_params=pltpu.CompilerParams(vmem_limit_bytes=20 << 20),
         name=name,
         **more,
     )(*scalars, *arrays)
@@ -191,23 +176,6 @@
 
 def shape(dims, dtype):
     return jax.ShapeDtypeStruct(dims, dtype)
-
-
-def spread(kernel, name, out, index, tiles, rows, scratch):
-    whole = lambda a: pl.BlockSpec(a.shape, lambda i, n=len(a.shape): (0,) * n)
-    block = tiles.shape[0] // BLOCKS
-    return pl.pallas_call(
-        kernel,
-        out_shape=out,
-        grid=(BLOCKS,),
-        in_specs=smem(1) + [pl.BlockSpec((block, TILE, TILE), lambda i: (i, 0, 0)), whole(rows)],
-        out_specs=whole(out),
-        scratch_shapes=scratch,
-        compiler_params=pltpu.CompilerParams(
-            vmem_limit_bytes=56 << 20, dimension_semantics=("arbitrary",)
-        ),
-        name=name,
-    )(index, tiles, rows)
 
 
 def body(features, weight, bias, tile_index, edge_count, edge_pos, edge_weight, grad_out):
@@ -234,16 +202,16 @@
     sent = jnp.broadcast_to(features[None], (dst,) + features.shape)
     source_rows = lax.all_to_all(sent, "dst", 0, 0, tiled=True)
     tiles = build(positions, False)
-    partial = spread(
+    partial = call(
         forward_kernel, "forward_tiles", shape((near, far, TILE, TILE), BF16),
-        index, tiles, source_rows, [pltpu.VMEM((src, TILE, TILE), F32)],
+        (index,), (tiles, source_rows), [pltpu.VMEM((src, TILE, TILE), F32)],
     )
     near_parts = lax.all_to_all(partial, NEAR, 0, 0, tiled=True)
-    late_positions, partial = lax.optimization_barrier((positions, partial))
+    near_sums = jnp.sum(near_parts.astype(F32), axis=0).astype(BF16)
+    late_positions, near_sums = lax.optimization_barrier((positions, near_sums))
     back_tiles = build(late_positions, True)
-    near_sums = jnp.sum(near_parts.astype(F32), axis=0).astype(BF16)
-    near_sums, back_tiles = lax.optimization_barrier((near_sums, back_tiles))
     parts = lax.all_to_all(near_sums, FAR, 0, 0, tiled=True)
+    parts, back_tiles = lax.optimization_barrier((parts, back_tiles))
     aggregated = jnp.sum(parts.astype(F32), axis=0).astype(BF16)
     rows = 2 * TILE // far
     hidden, send = call(
@@ -258,9 +226,9 @@
         middle_kernel, "middle_sums", shape((near, far * TILE + 2 * rows + 8, TILE), BF16), (), (far_rows,)
     )
     near_rows = lax.all_to_all(near_rows, NEAR, 0, 0, tiled=True)
-    back_send = spread(
+    back_send = call(
         backward_kernel, "backward_tiles", shape((dst, TILE + rows + 8, TILE), BF16),
-        index, back_tiles, near_rows,
+        (index,), (back_tiles, near_rows),
         [pltpu.VMEM((src, TILE, TILE), BF16), pltpu.VMEM((dst, TILE, TILE), F32)],
     )
     received = lax.all_to_all(back_send, "dst", 0, 0, tiled=True)

time: 171 us -> 164 us (0.959)
  blocking collectives: 96.2 us -> 80.9 us
  Pallas kernels: 26.9 us -> 15.5 us
  starting transfers between devices: 18.4 us -> 28.5 us
  local copies, waits for them, and re-layouts: 3.1 us -> 10.5 us
  waiting for transfers between devices: 21.5 us -> 23.5 us
    all_to_all x1, blocking collectives: 29.7 us -> 14.8 us  [body(): near_parts = lax.all_to_all(partial, NEAR, 0, 0, tiled=True)]
    all_to_all x1, starting transfers between devices: 3.51 us -> 13 us  [body(): parts = lax.all_to_all(near_sums, FAR, 0, 0, tiled=True)]
    pallas_call x2 -> x0, Pallas kernels: 9.26 us -> none  [spread(): pl.pallas_call(kernel, out_shape=out, grid=(BLOCKS,), in_specs=smem(1) +...]
    unnamed x2 -> x28, local copies, waits for them, and re-layouts: 0.81 us -> 8.25 us
    all_to_all x1, blocking collectives: 27.8 us -> 23.8 us  [body(): received = lax.all_to_all(back_send, 'dst', 0, 0, tiled=True)]
    all_to_all x1, waiting for transfers between devices: 6.31 us -> 10.2 us  [body(): parts = lax.all_to_all(near_sums, FAR, 0, 0, tiled=True)]
    all_to_all x1, blocking collectives: 13.9 us -> 16.8 us  [body(): near_rows = lax.all_to_all(near_rows, NEAR, 0, 0, tiled=True)]
    pallas_call x4 -> x6, Pallas kernels: 17.6 us -> 15.5 us  [call(): pl.pallas_call(kernel, out_shape=outs, in_specs=smem(len(scalars)) + vmem...]
  transfers between devices with their start and end apart: 3 -> 3, of which waited for: 3 -> 3; matrix products, arithmetic and copies ran while one was open for 1% -> 1% of each run, Pallas kernels for 8% -> 6%
where the time goes in v6:
time: 164 us; the launch traced here: 163 us
  blocking collectives  80.9 us (49%)
  starting transfers between devices  28.5 us (17%)
  waiting for transfers between devices  23.5 us (14%)
  Pallas kernels  15.5 us (9%)
  local copies, waits for them, and re-layouts  10.5 us (6%)
  other arithmetic  2.93 us (2%)
    all_to_all x1, blocking collectives, body(): far_rows = lax.all_to_all(send, FAR, 0, 0, tiled=True)  25.5 us
    all_to_all x1, blocking collectives, body(): received = lax.all_to_all(back_send, 'dst', 0, 0, tiled=True)  23.8 us
    all_to_all x1, blocking collectives, body(): near_rows = lax.all_to_all(near_rows, NEAR, 0, 0, tiled=True)  16.8 us
    pallas_call x6, Pallas kernels, call(): pl.pallas_call(kernel, out_shape=outs, in_specs=smem(len(scalars)) + vmem...  15.5 us
    all_to_all x1, blocking collectives, body(): near_parts = lax.all_to_all(partial, NEAR, 0, 0, tiled=True)  14.8 us
    all_to_all x1, starting transfers between devices, body(): parts = lax.all_to_all(near_sums, FAR, 0, 0, tiled=True)  13 us
    all_to_all x1, waiting for transfers between devices, body(): lax.all_to_all(jnp.broadcast_to(chunk[None], (far,) + chunk.shape), FAR,...  10.7 us
    all_to_all x1, starting transfers between devices, body(): source_rows = lax.all_to_all(sent, 'dst', 0, 0, tiled=True)  10.2 us
  transfers between devices with their start and end apart: 3, of which 3 were waited for; matrix products, arithmetic and copies ran while one was open for 1% of the time, Pallas kernels for 6%

profile of v6, /device:TPU:1, one launch (start us, length us, event | category | flops | bytes accessed | tf_op | source)
XLA Modules:
  0.0 162.7 jit_solution(301957904513142902)
XLA Ops:
  0.6 0.0 copy-start.12
  0.6 1.7 %broadcast_in_dim.4 = bf16[16,128,128]{2,1,0:T(8,128)(2,1)} broadcast(bf16[128,128]{1,0:T(8,128)(2,1)} %param.8), dimensions={1,2} | broadcast | bytes 557056 | tf_op jit(solution)/shard_map/broadcast_in_dim | solution.py:202
  2.3 10.2 %all-to-all-start = ((bf16[16,128,128]{2,1,0:T(8,128)(2,1)}), bf16[16,128,128]{2,1,0:T(8,128)(2,1)S(1)}, u32[]{:S(2)}, u32[]{:S(2)}) async-start(bf16[16,128,128]{2,1,0:T(8,128)(2,1)} %broadcast_in_dim.4), calls=%async_computation | async-start | bytes 1048576 | tf_op jit(solution)/shard_map/all_to_all | solution.py:203
  12.5 0.0 copy-start.4
  12.5 0.8 copy-done.4
  13.3 0.0 copy-start.6
  13.3 0.7 copy-done.6
  14.0 0.0 copy-start.10
  14.0 0.7 copy-done.10
  14.7 4.5 %build_tiles.1.tile_ref = bf16[128,128,128]{2,1,0:T(8,128)(2,1)S(1)} custom-call(s32[128]{0:T(128)S(1)} %bitcast.18, s32[64,128]{1,0:T(8,128)S(1)} %bitcast.14, bf16[64,128]{1,0:T(8,128)(2,1)S(1)} %bitcast.16), custom_call_target="tpu_custom_call" | custom-call | tf_op jit(solution)/shard_map/build_tiles/pallas_call | solution.py:165
  19.2 0.0 copy-start.2
  19.2 1.9 %copy-done.2 = bf16[128,128,128]{2,1,0:T(8,128)(2,1)} copy-done((bf16[128,128,128]{2,1,0:T(8,128)(2,1)}, bf16[128,128,128]{2,1,0:T(8,128)(2,1)S(1)}, u32[]{:S(2)}) %copy-start.2) | copy-done | bytes 4194328
  21.2 2.6 %all-to-all-done.rows_ref = bf16[16,128,128]{2,1,0:T(8,128)(2,1)S(1)} async-done(((bf16[16,128,128]{2,1,0:T(8,128)(2,1)}), bf16[16,128,128]{2,1,0:T(8,128)(2,1)S(1)}, u32[]{:S(2)}, u32[]{:S(2)}) %all-to-all-start) | async-done | bytes 524320 | tf_op jit(solution)/shard_map/all_to_all | solution.py:203
  23.7 0.0 copy-done.12
  23.7 0.0 copy-start.3
  23.7 2.2 %copy-done.3 = bf16[128,128,128]{2,1,0:T(8,128)(2,1)S(1)} copy-done((bf16[128,128,128]{2,1,0:T(8,128)(2,1)S(1)}, bf16[128,128,128]{2,1,0:T(8,128)(2,1)}, u32[]{:S(2)}) %copy-start.3) | copy-done | bytes 4194328
  25.9 0.0 copy-start.5
  25.9 2.7 %forward_tiles.1 = bf16[4,8,128,128]{3,2,1,0:T(8,128)(2,1)S(1)} custom-call(s32[128]{0:T(128)S(1)} %bitcast.20, bf16[128,128,128]{2,1,0:T(8,128)(2,1)S(1)} %copy-done.3, bf16[16,128,128]{2,1,0:T(8,128)(2,1)S(1)} %all-to-all-done.rows_ref), custom_call_target="tpu_custom_call" | custom-call | tf_op jit(solution)/shard_map/forward_tiles/pallas_call | solution.py:165
  28.6 0.0 copy-start.8
  28.6 0.0 copy-start.9
  28.6 0.0 copy-start.13
  28.6 14.8 %all_to_all.35 = bf16[4,8,128,128]{3,2,1,0:T(8,128)(2,1)S(1)} all-to-all(bf16[4,8,128,128]{3,2,1,0:T(8,128)(2,1)S(1)} %forward_tiles.1), channel_id=1, replica_groups=mesh['ylo'=2,'zq'=8,'z0'=2,'dst'=16] {'ylo','z0'}, dimensions={0} | all-to-all | bytes 2097152 | tf_op jit(solution)/shard_map/all_to_all | solution.py:209
  43.5 0.9 reduce_sum.45
  44.4 13.0 %all-to-all-start.2 = ((bf16[8,128,128]{2,1,0:T(8,128)(2,1)}), bf16[8,128,128]{2,1,0:T(8,128)(2,1)S(1)}, u32[]{:S(2)}, u32[]{:S(2)}) async-start(bf16[8,128,128]{2,1,0:T(8,128)(2,1)} %reduce_sum.45), calls=%async_computation.2 | async-start | bytes 524288 | tf_op jit(solution)/shard_map/all_to_all | solution.py:213
  57.4 0.0 copy-done.5
  57.4 0.0 copy-done.7
  57.4 0.0 copy-done.11
  57.4 4.6 %build_back.1.tile_ref = bf16[128,128,128]{2,1,0:T(8,128)(2,1)S(1)} custom-call(s32[128]{0:T(128)S(1)} %bitcast.19, s32[64,128]{1,0:T(8,128)S(1)} %bitcast.15, bf16[64,128]{1,0:T(8,128)(2,1)S(1)} %bitcast.17), custom_call_target="tpu_custom_call" | custom-call | tf_op jit(solution)/shard_map/build_back/pallas_call | solution.py:165
  62.0 0.0 copy-start
  62.0 1.9 %copy-done = bf16[128,128,128]{2,1,0:T(8,128)(2,1)} copy-done((bf16[128,128,128]{2,1,0:T(8,128)(2,1)}, bf16[128,128,128]{2,1,0:T(8,128)(2,1)S(1)}, u32[]{:S(2)}) %copy-start) | copy-done | bytes 4194328
  63.9 10.2 %all-to-all-done.2 = bf16[8,128,128]{2,1,0:T(8,128)(2,1)S(1)} async-done(((bf16[8,128,128]{2,1,0:T(8,128)(2,1)}), bf16[8,128,128]{2,1,0:T(8,128)(2,1)S(1)}, u32[]{:S(2)}, u32[]{:S(2)}) %all-to-all-start.2) | async-done | bytes 262176 | tf_op jit(solution)/shard_map/all_to_all | solution.py:213
  74.2 0.0 copy-start.1
  74.2 0.0 copy-done.8
  74.2 0.0 copy-done.9
  74.2 0.0 copy-done.13
  74.2 0.8 dense_layer.1
  75.1 25.5 %all_to_all.36.recv_ref = bf16[8,168,128]{2,1,0:T(8,128)(2,1)S(1)} all-to-all(bf16[8,168,128]{2,1,0:T(8,128)(2,1)S(1)} %get-tuple-element.15), channel_id=1, replica_groups=mesh['ylo'=2,'zq'=8,'z0'=2,'dst'=16] {'zq'}, dimensions={0} | all-to-all | bytes 688128 | tf_op jit(solution)/shard_map/all_to_all | solution.py:224
  100.5 0.2 middle_sums.1
  100.7 16.8 %all_to_all.37.recv_ref = bf16[4,1096,128]{2,1,0:T(8,128)(2,1)S(1)} all-to-all(bf16[4,1096,128]{2,1,0:T(8,128)(2,1)S(1)} %middle_sums.1), channel_id=1, replica_groups=mesh['ylo'=2,'zq'=8,'z0'=2,'dst'=16] {'ylo','z0'}, dimensions={0} | all-to-all | bytes 2244608 | tf_op jit(solution)/shard_map/all_to_all | solution.py:228
  117.5 0.0 copy-done.1
  117.5 2.7 %backward_tiles.1 = bf16[16,168,128]{2,1,0:T(8,128)(2,1)S(1)} custom-call(s32[128]{0:T(128)S(1)} %bitcast.21, bf16[128,128,128]{2,1,0:T(8,128)(2,1)S(1)} %copy-done.1, bf16[4,1096,128]{2,1,0:T(8,128)(2,1)S(1)} %all_to_all.37.recv_ref), custom_call_target="tpu_custom_call" | custom-call | tf_op jit(solution)/shard_map/backward_tiles/pallas_call | solution.py:165
  120.2 23.8 %all_to_all.38 = bf16[16,168,128]{2,1,0:T(8,128)(2,1)S(1)} all-to-all(bf16[16,168,128]{2,1,0:T(8,128)(2,1)S(1)} %backward_tiles.1), channel_id=1, replica_groups=mesh['ylo'=2,'zq'=8,'z0'=2,'dst'=16] {'dst'}, dimensions={0} | all-to-all | bytes 1376256 | tf_op jit(solution)/shard_map/all_to_all | solution.py:234
  144.1 0.6 broadcast_in_dim.5
  144.8 5.3 %all-to-all-start.6 = ((bf16[8,16,256]{2,1,0:T(8,128)(2,1)}), bf16[8,16,256]{2,1,0:T(8,128)(2,1)S(1)}, u32[]{:S(2)}, u32[]{:S(2)}) async-start(bf16[8,16,256]{2,1,0:T(8,128)(2,1)} %broadcast_in_dim.5), calls=%async_computation.6 | async-start | bytes 131072 | tf_op jit(solution)/shard_map/all_to_all | solution.py:238
  150.0 0.7 slice_reduce_fusion
  150.7 0.6 fusion
  151.3 10.7 %all-to-all-done.6 = bf16[8,16,256]{2,1,0:T(8,128)(2,1)S(1)} async-done(((bf16[8,16,256]{2,1,0:T(8,128)(2,1)}), bf16[8,16,256]{2,1,0:T(8,128)(2,1)S(1)}, u32[]{:S(2)}, u32[]{:S(2)}) %all-to-all-start.6) | async-done | bytes 65568 | tf_op jit(solution)/shard_map/all_to_all | solution.py:238
  162.0 0.7 bitcast_convert_fusion
  (7 shorter events, 0.1 us)
Async XLA Ops:
  0.6 23.1 %copy-start.12 = (s32[1,1,128]{2,1,0:T(1,128)S(1)}, s32[1,1,128]{2,1,0:T(1,128)}, u32[]{:S(2)}) copy-start(s32[1,1,128]{2,1,0:T(1,128)} %param.11) | copy-start | bytes 1540
  2.3 21.4 %all-to-all-start = ((bf16[16,128,128]{2,1,0:T(8,128)(2,1)}), bf16[16,128,128]{2,1,0:T(8,128)(2,1)S(1)}, u32[]{:S(2)}, u32[]{:S(2)}) async-start(bf16[16,128,128]{2,1,0:T(8,128)(2,1)} %broadcast_in_dim.4), calls=%async_computation | async-start | bytes 1048576 | tf_op jit(solution)/shard_map/all_to_all | solution.py:203
  12.5 0.8 copy-start.4
  13.3 0.7 copy-start.6
  14.0 0.7 copy-start.10
  19.2 2.0 %copy-start.2 = (bf16[128,128,128]{2,1,0:T(8,128)(2,1)}, bf16[128,128,128]{2,1,0:T(8,128)(2,1)S(1)}, u32[]{:S(2)}) copy-start(bf16[128,128,128]{2,1,0:T(8,128)(2,1)S(1)} %build_tiles.1.tile_ref) | copy-start | bytes 12582916
  23.7 2.2 %copy-start.3 = (bf16[128,128,128]{2,1,0:T(8,128)(2,1)S(1)}, bf16[128,128,128]{2,1,0:T(8,128)(2,1)}, u32[]{:S(2)}) copy-start(bf16[128,128,128]{2,1,0:T(8,128)(2,1)} %copy-done.2) | copy-start | bytes 12582916
  25.9 31.5 %copy-start.5 = (s32[1,1,128,64]{2,3,1,0:T(8,128)S(1)}, s32[1,1,128,64]{2,3,1,0:T(8,128)}, u32[]{:S(2)}) copy-start(s32[1,1,128,64]{2,3,1,0:T(8,128)} %param.13) | copy-start | bytes 98308
  25.9 31.5 %copy-start.7 = (bf16[1,1,128,64]{2,3,1,0:T(8,128)(2,1)S(1)}, bf16[1,1,128,64]{2,3,1,0:T(8,128)(2,1)}, u32[]{:S(2)}) copy-start(bf16[1,1,128,64]{2,3,1,0:T(8,128)(2,1)} %param.14) | copy-start | bytes 49156
  25.9 31.5 %copy-start.11 = (s32[1,1,128]{2,1,0:T(1,128)S(1)}, s32[1,1,128]{2,1,0:T(1,128)}, u32[]{:S(2)}) copy-start(s32[1,1,128]{2,1,0:T(1,128)} %param.12) | copy-start | bytes 1540
  28.6 45.6 %copy-start.8 = (bf16[128,256]{1,0:T(8,128)(2,1)S(1)}, bf16[128,256]{1,0:T(8,128)(2,1)}, u32[]{:S(2)}) copy-start(bf16[128,256]{1,0:T(8,128)(2,1)} %weight_ref.1) | copy-start | bytes 196612
  28.6 45.6 %copy-start.9 = (bf16[128,256]{1,0:T(8,128)(2,1)S(1)}, bf16[128,256]{1,0:T(8,128)(2,1)}, u32[]{:S(2)}) copy-start(bf16[128,256]{1,0:T(8,128)(2,1)} %grad_ref.1) | copy-start | bytes 196612
  28.6 45.6 %copy-start.13 = (f32[256]{0:T(256)S(1)}, f32[256]{0:T(256)}, u32[]{:S(2)}) copy-start(f32[256]{0:T(256)} %param.10) | copy-start | bytes 3076
  44.4 29.8 %all-to-all-start.2 = ((bf16[8,128,128]{2,1,0:T(8,128)(2,1)}), bf16[8,128,128]{2,1,0:T(8,128)(2,1)S(1)}, u32[]{:S(2)}, u32[]{:S(2)}) async-start(bf16[8,128,128]{2,1,0:T(8,128)(2,1)} %reduce_sum.45), calls=%async_computation.2 | async-start | bytes 524288 | tf_op jit(solution)/shard_map/all_to_all | solution.py:213
  62.0 2.0 %copy-start = (bf16[128,128,128]{2,1,0:T(8,128)(2,1)}, bf16[128,128,128]{2,1,0:T(8,128)(2,1)S(1)}, u32[]{:S(2)}) copy-start(bf16[128,128,128]{2,1,0:T(8,128)(2,1)S(1)} %build_back.1.tile_ref) | copy-start | bytes 12582916
  74.2 43.3 %copy-start.1 = (bf16[128,128,128]{2,1,0:T(8,128)(2,1)S(1)}, bf16[128,128,128]{2,1,0:T(8,128)(2,1)}, u32[]{:S(2)}) copy-start(bf16[128,128,128]{2,1,0:T(8,128)(2,1)} %copy-done) | copy-start | bytes 12582916
  144.8 17.2 %all-to-all-start.6 = ((bf16[8,16,256]{2,1,0:T(8,128)(2,1)}), bf16[8,16,256]{2,1,0:T(8,128)(2,1)S(1)}, u32[]{:S(2)}, u32[]{:S(2)}) async-start(bf16[8,16,256]{2,1,0:T(8,128)(2,1)} %broadcast_in_dim.5), calls=%async_computation.6 | async-start | bytes 131072 | tf_op jit(solution)/shard_map/all_to_all | solution.py:238

commit v7 on v6

--- a/solution.py
+++ b/solution.py
@@ -14,6 +14,7 @@
 NT = (((1,), (1,)), ((), ()))
 TN = (((0,), (0,)), ((), ()))
 SRC = ("ylo", "zq", "z0")
+DST = ("x", "d0")
 NEAR = ("ylo", "z0")
 FAR = "zq"
 GROUP = 32
@@ -100,56 +101,107 @@
     return tile[0:2] + tile[2:4]
 
 
-def dense_kernel(agg_ref, weight_ref, bias_ref, grad_ref, hidden_ref, send_ref):
-    peers = send_ref.shape[0]
+def dense_kernel(agg_ref, weight_ref, bias_ref, grad_ref, hidden_ref, send_ref, grad_pre_ref):
     aggregated = agg_ref[...]
     weight = weight_ref[...]
     preact = dot(aggregated, weight) + bias_ref[...]
     sigma = 1.0 / (1.0 + jnp.exp(-preact))
     hidden_ref[...] = (preact * sigma).astype(BF16)
     grad_pre = (grad_ref[...].astype(F32) * sigma * (1.0 + preact * (1.0 - sigma))).astype(BF16)
+    grad_pre_ref[...] = grad_pre
     back_rows = dot(grad_pre, weight, NT).astype(BF16)
-    send_ref[:, :TILE, :] = jnp.broadcast_to(back_rows[None], (peers, TILE, TILE))
-    part = dot(aggregated, grad_pre, TN).astype(BF16)
-    rows = TILE // peers
-    send_ref[:, TILE : TILE + rows, :] = part[:, :TILE].reshape(peers, rows, TILE)
-    send_ref[:, TILE + rows : TILE + 2 * rows, :] = part[:, TILE:].reshape(peers, rows, TILE)
+    send_ref[...] = jnp.broadcast_to(back_rows[None], send_ref.shape)
+
+
+def part_kernel(agg_ref, grad_pre_ref, out_ref):
+    grad_pre = grad_pre_ref[...]
+    part = dot(agg_ref[...], grad_pre, TN)
+    out_ref[:TILE] = part[:, :TILE]
+    out_ref[TILE : 2 * TILE] = part[:, TILE:]
     bias_part = jnp.sum(grad_pre.astype(F32), axis=0, keepdims=True)
-    bias_rows = jnp.concatenate([bias_part[:, :TILE], bias_part[:, TILE:]], axis=0)
-    send_ref[:, TILE + 2 * rows :, :] = jnp.broadcast_to(bias_tile(bias_rows)[None], (peers, 8, TILE))
-
-
-def middle_kernel(recv_ref, out_ref):
+    bias_rows = [bias_part[:, :TILE], bias_part[:, TILE:], jnp.zeros((6, TILE), F32)]
+    out_ref[2 * TILE :] = jnp.concatenate(bias_rows, axis=0)
+
+
+def pick_kernel(place_ref, recv_ref, out_ref):
+    peers = recv_ref.shape[0]
+    size = out_ref.shape[0] - 8
+    start = pl.multiple_of(place_ref[0] * size, 8)
+    total = recv_ref[0, pl.ds(start, size), :]
+    last = recv_ref[0, peers * size :, :]
+    for k in range(1, peers):
+        total = total + recv_ref[k, pl.ds(start, size), :]
+        last = last + recv_ref[k, peers * size :, :]
+    out_ref[:size] = total
+    out_ref[size:] = last
+
+
+def split_rows(total):
+    high, low = high_low(total[:-8])
+    return jnp.concatenate([high.astype(BF16), low.astype(BF16), bias_tile(total[-8:])], axis=0)
+
+
+def join_rows(rows):
+    count = (rows.shape[0] - 8) // 2
+    bias_rows = jnp.concatenate([bias_sum(rows[2 * count :]), jnp.zeros((6, TILE), F32)], axis=0)
+    return jnp.concatenate([rows[:count] + rows[count : 2 * count], bias_rows], axis=0)
+
+
+def middle_kernel(place_ref, recv_ref, part_ref, out_ref):
     near = out_ref.shape[0]
-    peers = recv_ref.shape[0]
-    top = peers * TILE
-    back_rows = recv_ref[:, :TILE, :].reshape(top, TILE)
-    total = jnp.sum(recv_ref[:, TILE:, :].astype(F32), axis=0)
-    rows = total.shape[0] - 8
-    high, low = high_low(total[:rows])
-    tile = bias_tile(bias_sum(total[rows:]))
-    extra = jnp.concatenate([high.astype(BF16), low.astype(BF16), tile], axis=0)
+    peers = part_ref.shape[0]
+    top = recv_ref.shape[0] * TILE
+    back_rows = recv_ref[...].reshape(top, TILE)
+    size = (part_ref.shape[1] - 8) // peers
+    start = pl.multiple_of(place_ref[0] * size, 8)
+    total = part_ref[0, pl.ds(start, size), :]
+    last = part_ref[0, peers * size :, :]
+    for k in range(1, peers):
+        total = total + part_ref[k, pl.ds(start, size), :]
+        last = last + part_ref[k, peers * size :, :]
+    extra = split_rows(jnp.concatenate([total, last], axis=0))
     for k in range(near):
         out_ref[k, :top] = back_rows
         out_ref[k, top:] = extra
 
 
+def share_kernel(recv_ref, out_ref):
+    top = recv_ref.shape[1] - out_ref.shape[1]
+    total = jnp.sum(recv_ref[:, top:, :].astype(F32), axis=0)
+    out_ref[...] = jnp.broadcast_to(split_rows(join_rows(total))[None], out_ref.shape)
+
+
+def chunk_kernel(recv_ref, back_ref, out_ref, bias_grad_ref, *, scale):
+    total = join_rows(jnp.sum(recv_ref[...].astype(F32), axis=0)) * scale
+    size = total.shape[0] - 8
+    bias_grad_ref[:, :TILE] = total[size : size + 1]
+    bias_grad_ref[:, TILE:] = total[size + 1 : size + 2]
+    high, low = high_low(total[:size])
+    both = jnp.concatenate([high, low], axis=0).astype(BF16)
+    out_ref[:, :TILE, :] = back_ref[...]
+    out_ref[:, TILE:, :] = jnp.broadcast_to(both[None], (out_ref.shape[0], 2 * size, TILE))
+
+
+def final_kernel(recv_ref, input_ref, weight_grad_ref, *, group):
+    pieces = recv_ref.shape[0]
+    input_ref[...] = jnp.sum(recv_ref[:, :TILE, :].astype(F32), axis=0).astype(BF16)
+    size = 2 * TILE // pieces
+    for d in range(pieces):
+        start = ((d % group) * (pieces // group) + d // group) * size
+        chunk = recv_ref[d, TILE : TILE + size, :].astype(F32) + recv_ref[d, TILE + size :, :].astype(F32)
+        lane = start // TILE * TILE
+        weight_grad_ref[start % TILE : start % TILE + size, lane : lane + TILE] = chunk
+
+
 def backward_kernel(index_ref, tile_ref, recv_ref, out_ref, rows, sums):
     near = recv_ref.shape[0]
     far = rows.shape[0] // near
-    top = far * TILE
     pieces = out_ref.shape[0]
     for target in range(near * far):
         start = target // 2 % far * TILE
         rows[target] = recv_ref[target // (2 * far) * 2 + target % 2, start : start + TILE]
     spread_tiles(index_ref, tile_ref, rows, sums, pieces, True)
-    out_ref[:, :TILE, :] = sums[...].astype(BF16)
-    total = jnp.sum(recv_ref[:, top:, :].astype(F32), axis=0)
-    count = (total.shape[0] - 8) // 2
-    chunk = (total[:count] + total[count : 2 * count]).astype(BF16)
-    out_ref[:, TILE : TILE + count, :] = jnp.broadcast_to(chunk[None], (pieces, count, TILE))
-    tile = bias_tile(bias_sum(total[2 * count :]))
-    out_ref[:, TILE + count :, :] = jnp.broadcast_to(tile[None], (pieces, 8, TILE))
+    out_ref[...] = sums[...].astype(BF16)
 
 
 def vmem(n):
@@ -182,7 +234,7 @@
     near = lax.axis_size(NEAR)
     far = lax.axis_size(FAR)
     src = near * far
-    dst = lax.axis_size("dst")
+    dst = lax.axis_size(DST)
     index = tile_index.reshape(-1)
     counts = edge_count.reshape(-1)
     slots = counts.shape[0]
@@ -200,7 +252,7 @@
         )
 
     sent = jnp.broadcast_to(features[None], (dst,) + features.shape)
-    source_rows = lax.all_to_all(sent, "dst", 0, 0, tiled=True)
+    source_rows = lax.all_to_all(sent, DST, 0, 0, tiled=True)
     tiles = build(positions, False)
     partial = call(
         forward_kernel, "forward_tiles", shape((near, far, TILE, TILE), BF16),
@@ -213,47 +265,65 @@
     parts = lax.all_to_all(near_sums, FAR, 0, 0, tiled=True)
     parts, back_tiles = lax.optimization_barrier((parts, back_tiles))
     aggregated = jnp.sum(parts.astype(F32), axis=0).astype(BF16)
-    rows = 2 * TILE // far
-    hidden, send = call(
+    hidden, send, grad_pre = call(
         dense_kernel,
         "dense_layer",
-        (shape(grad_out.shape, BF16), shape((far, TILE + rows + 8, TILE), BF16)),
+        (shape(grad_out.shape, BF16), shape((far, TILE, TILE), BF16), shape(grad_out.shape, BF16)),
         (),
         (aggregated, weight, bias.reshape(1, -1), grad_out),
     )
     far_rows = lax.all_to_all(send, FAR, 0, 0, tiled=True)
+    group = lax.axis_size("d0")
+    part = call(part_kernel, "grad_part", shape((2 * TILE + 8, TILE), F32), (), (aggregated, grad_pre))
+    part = lax.all_gather(part, "d0")
+    part = call(
+        pick_kernel, "grad_pick", shape((2 * TILE // group + 8, TILE), F32), (lax.axis_index("d0").reshape(1),), (part,)
+    )
+    part = lax.all_gather(part, "x")
+    size = 2 * TILE // dst
     near_rows = call(
-        middle_kernel, "middle_sums", shape((near, far * TILE + 2 * rows + 8, TILE), BF16), (), (far_rows,)
+        middle_kernel, "middle_sums", shape((near, far * TILE + 2 * size + 8, TILE), BF16),
+        (lax.axis_index("x").reshape(1),), (far_rows, part),
     )
     near_rows = lax.all_to_all(near_rows, NEAR, 0, 0, tiled=True)
+    share = call(share_kernel, "grad_share", shape((far, 2 * size + 8, TILE), BF16), (), (near_rows,))
+    shared = lax.all_to_all(share, FAR, 0, 0, tiled=True)
     back_send = call(
-        backward_kernel, "backward_tiles", shape((dst, TILE + rows + 8, TILE), BF16),
+        backward_kernel, "backward_tiles", shape((dst, TILE, TILE), BF16),
         (index,), (back_tiles, near_rows),
         [pltpu.VMEM((src, TILE, TILE), BF16), pltpu.VMEM((dst, TILE, TILE), F32)],
     )
-    received = lax.all_to_all(back_send, "dst", 0, 0, tiled=True)
     node_scale = 1.0 / math.sqrt(features.shape[0] * src * dst)
-    extra = jnp.sum(received[:, TILE:, :].astype(F32), axis=0) * node_scale
-    chunk = jnp.concatenate([extra[: rows // 2], extra[rows // 2 : rows]], axis=1).astype(BF16)
-    chunks = lax.all_to_all(jnp.broadcast_to(chunk[None], (far,) + chunk.shape), FAR, 0, 0, tiled=True)
-    weight_grad = chunks.reshape(TILE, 2 * TILE).astype(F32)
-    bias_grad = bias_sum(extra[rows:]).reshape(-1)
-    input_grad = jnp.sum(received[:, :TILE, :].astype(F32), axis=0).astype(BF16)
-    return (hidden, input_grad, weight_grad, bias_grad)
+    back_send, bias_grad = call(
+        lambda *refs: chunk_kernel(*refs, scale=node_scale),
+        "grad_chunk",
+        (shape((dst, TILE + 2 * size, TILE), BF16), shape((1, 2 * TILE), F32)),
+        (),
+        (shared, back_send),
+    )
+    received = lax.all_to_all(back_send, DST, 0, 0, tiled=True)
+    input_grad, weight_grad = call(
+        lambda *refs: final_kernel(*refs, group=group),
+        "final_sums",
+        (shape(features.shape, BF16), shape((TILE, 2 * TILE), F32)),
+        (),
+        (received,),
+    )
+    return (hidden, input_grad, weight_grad, bias_grad.reshape(-1))
 
 
 def solution(mesh):
     src, dst = mesh.devices.shape
-    fine = Mesh(mesh.devices.reshape(2, src // 4, 2, dst), ("ylo", "zq", "z0", "dst"))
-    rows = P(("ylo", "zq", "z0", "dst"), None)
+    fine = Mesh(mesh.devices.reshape(2, src // 4, 2, dst // 4, 4), SRC + DST)
+    rows = P(SRC + DST, None)
     placed = (
         rows,
         P(),
         P(),
-        P(SRC, "dst", None),
-        P(SRC, "dst", None),
-        P(SRC, "dst", None, None),
-        P(SRC, "dst", None, None),
+        P(SRC, DST, None),
+        P(SRC, DST, None),
+        P(SRC, DST, None, None),
+        P(SRC, DST, None, None),
         rows,
     )
     return jax.shard_map(

time: 164 us -> 166 us (1.012)
  starting transfers between devices: 28.5 us -> 39 us
  blocking collectives: 80.9 us -> 74.6 us
  waiting for transfers between devices: 23.5 us -> 20.2 us
  Pallas kernels: 15.5 us -> 17.9 us
  other arithmetic: 2.93 us -> 0.97 us
    all_to_all x2 -> x1, blocking collectives: 49.3 us -> 23.2 us  [body(): received = lax.all_to_all(back_send, DST, 0, 0, tiled=True)]
    all_gather x0 -> x2, blocking collectives: none -> 21.7 us  [the longest x1 11.6 us: body(): part = lax.all_gather(part, 'd0')]
    all_to_all x2 -> x3, starting transfers between devices: 15.5 us -> 26 us  [the longest x1 10.2 us: body(): source_rows = lax.all_to_all(sent, DST, 0, 0, tiled=True)]
    all_to_all x2 -> x3, waiting for transfers between devices: 13.3 us -> 9.99 us  [the longest x1 7.41 us: body(): shared = lax.all_to_all(share, FAR, 0, 0, tiled=True)]
    pallas_call x6 -> x11, Pallas kernels: 15.5 us -> 17.9 us  [call(): pl.pallas_call(kernel, out_shape=outs, in_specs=smem(len(scalars)) + vmem...]
    unnamed x28, local copies, waits for them, and re-layouts: 8.25 us -> 10.4 us
    all_to_all x1, blocking collectives: 16.8 us -> 15 us  [body(): near_rows = lax.all_to_all(near_rows, NEAR, 0, 0, tiled=True)]
  transfers between devices with their start and end apart: 3 -> 4, of which waited for: 3 -> 3; matrix products, arithmetic and copies ran while one was open for 1% -> 0% of each run, Pallas kernels for 6% -> 7%
where the time goes in v7:
time: 166 us
  blocking collectives  74.6 us (45%)
  starting transfers between devices  39 us (23%)
  waiting for transfers between devices  20.2 us (12%)
  Pallas kernels  17.9 us (11%)
  local copies, waits for them, and re-layouts  12.1 us (7%)
    all_to_all x1, blocking collectives, body(): received = lax.all_to_all(back_send, DST, 0, 0, tiled=True)  23.2 us
    pallas_call x11, Pallas kernels, call(): pl.pallas_call(kernel, out_shape=outs, in_specs=smem(len(scalars)) + vmem...  17.9 us
    all_to_all x1, blocking collectives, body(): near_rows = lax.all_to_all(near_rows, NEAR, 0, 0, tiled=True)  15 us
    all_to_all x1, blocking collectives, body(): near_parts = lax.all_to_all(partial, NEAR, 0, 0, tiled=True)  14.8 us
    all_to_all x1, starting transfers between devices, body(): parts = lax.all_to_all(near_sums, FAR, 0, 0, tiled=True)  13 us
    all_gather x1, blocking collectives, body(): part = lax.all_gather(part, 'd0')  11.6 us
    unnamed x28, local copies, waits for them, and re-layouts  10.4 us
    all_to_all x1, starting transfers between devices, body(): source_rows = lax.all_to_all(sent, DST, 0, 0, tiled=True)  10.2 us
  transfers between devices with their start and end apart: 4, of which 3 were waited for; matrix products, arithmetic and copies ran while one was open for 0% of the time, Pallas kernels for 7%

profile of v7, /device:TPU:1, one launch (start us, length us, event | category | flops | bytes accessed | tf_op | source)
XLA Modules:
  0.0 165.5 jit_solution(16678939569031655542)
XLA Ops:
  0.6 0.0 copy-start.12
  0.6 1.7 %broadcast_in_dim.2 = bf16[16,128,128]{2,1,0:T(8,128)(2,1)} broadcast(bf16[128,128]{1,0:T(8,128)(2,1)} %param.8), dimensions={1,2} | broadcast | bytes 557056 | tf_op jit(solution)/shard_map/broadcast_in_dim | solution.py:254
  2.3 10.2 %all-to-all-start = ((bf16[16,128,128]{2,1,0:T(8,128)(2,1)}), bf16[16,128,128]{2,1,0:T(8,128)(2,1)S(1)}, u32[]{:S(2)}, u32[]{:S(2)}) async-start(bf16[16,128,128]{2,1,0:T(8,128)(2,1)} %broadcast_in_dim.2), calls=%async_computation | async-start | bytes 1048576 | tf_op jit(solution)/shard_map/all_to_all | solution.py:255
  12.5 0.0 copy-start.4
  12.5 0.8 copy-done.4
  13.3 0.0 copy-start.6
  13.3 0.7 copy-done.6
  14.0 0.0 copy-start.10
  14.0 0.7 copy-done.10
  14.7 4.5 %build_tiles.1.tile_ref = bf16[128,128,128]{2,1,0:T(8,128)(2,1)S(1)} custom-call(s32[128]{0:T(128)S(1)} %bitcast.20, s32[64,128]{1,0:T(8,128)S(1)} %bitcast.16, bf16[64,128]{1,0:T(8,128)(2,1)S(1)} %bitcast.18), custom_call_target="tpu_custom_call" | custom-call | tf_op jit(solution)/shard_map/build_tiles/pallas_call | solution.py:217
  19.2 0.0 copy-start.2
  19.2 1.9 %copy-done.2 = bf16[128,128,128]{2,1,0:T(8,128)(2,1)} copy-done((bf16[128,128,128]{2,1,0:T(8,128)(2,1)}, bf16[128,128,128]{2,1,0:T(8,128)(2,1)S(1)}, u32[]{:S(2)}) %copy-start.2) | copy-done | bytes 4194328
  21.2 2.6 %all-to-all-done.rows_ref = bf16[16,128,128]{2,1,0:T(8,128)(2,1)S(1)} async-done(((bf16[16,128,128]{2,1,0:T(8,128)(2,1)}), bf16[16,128,128]{2,1,0:T(8,128)(2,1)S(1)}, u32[]{:S(2)}, u32[]{:S(2)}) %all-to-all-start) | async-done | bytes 524320 | tf_op jit(solution)/shard_map/all_to_all | solution.py:255
  23.7 0.0 copy-done.12
  23.7 2.2 %copy-done.3 = bf16[128,128,128]{2,1,0:T(8,128)(2,1)S(1)} copy-done((bf16[128,128,128]{2,1,0:T(8,128)(2,1)S(1)}, bf16[128,128,128]{2,1,0:T(8,128)(2,1)}, u32[]{:S(2)}) %copy-start.3) | copy-done | bytes 4194328
  25.9 2.7 %forward_tiles.1 = bf16[4,8,128,128]{3,2,1,0:T(8,128)(2,1)S(1)} custom-call(s32[128]{0:T(128)S(1)} %bitcast.22, bf16[128,128,128]{2,1,0:T(8,128)(2,1)S(1)} %copy-done.3, bf16[16,128,128]{2,1,0:T(8,128)(2,1)S(1)} %all-to-all-done.rows_ref), custom_call_target="tpu_custom_call" | custom-call | tf_op jit(solution)/shard_map/forward_tiles/pallas_call | solution.py:217
  28.6 0.0 copy-start.8
  28.6 0.0 copy-start.9
  28.6 0.0 copy-start.13
  28.6 14.8 %all_to_all.35 = bf16[4,8,128,128]{3,2,1,0:T(8,128)(2,1)S(1)} all-to-all(bf16[4,8,128,128]{3,2,1,0:T(8,128)(2,1)S(1)} %forward_tiles.1), channel_id=1, replica_groups=mesh['ylo'=2,'zq'=8,'z0'=2,'x'=4,'d0'=4] {'ylo','z0'}, dimensions={0} | all-to-all | bytes 2097152 | tf_op jit(solution)/shard_map/all_to_all | solution.py:261
  43.5 0.9 reduce_sum.24
  44.4 13.0 %all-to-all-start.2 = ((bf16[8,128,128]{2,1,0:T(8,128)(2,1)}), bf16[8,128,128]{2,1,0:T(8,128)(2,1)S(1)}, u32[]{:S(2)}, u32[]{:S(2)}) async-start(bf16[8,128,128]{2,1,0:T(8,128)(2,1)} %reduce_sum.24), calls=%async_computation.2 | async-start | bytes 524288 | tf_op jit(solution)/shard_map/all_to_all | solution.py:265
  57.4 0.0 copy-done.5
  57.4 0.0 copy-done.7
  57.4 0.0 copy-done.11
  57.4 4.6 %build_back.1.tile_ref = bf16[128,128,128]{2,1,0:T(8,128)(2,1)S(1)} custom-call(s32[128]{0:T(128)S(1)} %bitcast.21, s32[64,128]{1,0:T(8,128)S(1)} %bitcast.17, bf16[64,128]{1,0:T(8,128)(2,1)S(1)} %bitcast.19), custom_call_target="tpu_custom_call" | custom-call | tf_op jit(solution)/shard_map/build_back/pallas_call | solution.py:217
  62.0 0.0 copy-start
  62.0 1.9 %copy-done = bf16[128,128,128]{2,1,0:T(8,128)(2,1)} copy-done((bf16[128,128,128]{2,1,0:T(8,128)(2,1)}, bf16[128,128,128]{2,1,0:T(8,128)(2,1)S(1)}, u32[]{:S(2)}) %copy-start) | copy-done | bytes 4194328
  63.9 10.2 %all-to-all-done.2 = bf16[8,128,128]{2,1,0:T(8,128)(2,1)S(1)} async-done(((bf16[8,128,128]{2,1,0:T(8,128)(2,1)}), bf16[8,128,128]{2,1,0:T(8,128)(2,1)S(1)}, u32[]{:S(2)}, u32[]{:S(2)}) %all-to-all-start.2) | async-done | bytes 262176 | tf_op jit(solution)/shard_map/all_to_all | solution.py:265
  74.2 0.0 copy-done.8
  74.2 0.0 copy-done.9
  74.2 0.0 copy-done.13
  74.2 1.0 dense_layer.1
  75.3 5.9 %all-to-all-start.3 = ((bf16[8,128,128]{2,1,0:T(8,128)(2,1)}), bf16[8,128,128]{2,1,0:T(8,128)(2,1)S(1)}, u32[]{:S(2)}, u32[]{:S(2)}) async-start(bf16[8,128,128]{2,1,0:T(8,128)(2,1)} %get-tuple-element.19), calls=%async_computation.3 | async-start | bytes 524288 | tf_op jit(solution)/shard_map/all_to_all | solution.py:275
  81.2 0.2 grad_part.1
  81.4 11.6 %all-gather = f32[1056,128]{1,0:T(8,128)S(1)} all-gather(f32[264,128]{1,0:T(8,128)S(1)} %grad_part.1), channel_id=2, replica_groups=mesh['ylo'=2,'zq'=8,'z0'=2,'x'=4,'d0'=4] {'d0'}, dimensions={0}, use_global_device_ids=true | all-gather | bytes 675840 | tf_op jit(solution)/shard_map/all_gather | solution.py:278
  93.0 10.0 %all-gather.1 = f32[288,128]{1,0:T(8,128)S(1)} all-gather(f32[72,128]{1,0:T(8,128)S(1)} %grad_pick.1), channel_id=3, replica_groups=mesh['ylo'=2,'zq'=8,'z0'=2,'x'=4,'d0'=4] {'x'}, dimensions={0}, use_global_device_ids=true | all-gather | bytes 184320 | tf_op jit(solution)/shard_map/all_gather | solution.py:282
  103.0 0.0 all-to-all-done.3.recv_ref
  103.0 0.1 middle_sums.1
  103.2 15.0 %all_to_all.36.recv_ref = bf16[4,1064,128]{2,1,0:T(8,128)(2,1)S(1)} all-to-all(bf16[4,1064,128]{2,1,0:T(8,128)(2,1)S(1)} %middle_sums.1), channel_id=1, replica_groups=mesh['ylo'=2,'zq'=8,'z0'=2,'x'=4,'d0'=4] {'ylo','z0'}, dimensions={0} | all-to-all | bytes 2179072 | tf_op jit(solution)/shard_map/all_to_all | solution.py:288
  118.2 0.7 grad_share.1
  118.8 9.9 %all-to-all-start.5 = ((bf16[8,40,128]{2,1,0:T(8,128)(2,1)}), bf16[8,40,128]{2,1,0:T(8,128)(2,1)S(1)}, u32[]{:S(2)}, u32[]{:S(2)}) async-start(bf16[8,40,128]{2,1,0:T(8,128)(2,1)} %grad_share.1), calls=%async_computation.5 | async-start | bytes 163840 | tf_op jit(solution)/shard_map/all_to_all | solution.py:290
  128.7 2.2 %copy-done.1 = bf16[128,128,128]{2,1,0:T(8,128)(2,1)S(1)} copy-done((bf16[128,128,128]{2,1,0:T(8,128)(2,1)S(1)}, bf16[128,128,128]{2,1,0:T(8,128)(2,1)}, u32[]{:S(2)}) %copy-start.1) | copy-done | bytes 4194328
  130.9 2.7 %backward_tiles.1.refs_1_ = bf16[16,128,128]{2,1,0:T(8,128)(2,1)S(1)} custom-call(s32[128]{0:T(128)S(1)} %bitcast.23, bf16[128,128,128]{2,1,0:T(8,128)(2,1)S(1)} %copy-done.1, bf16[4,1064,128]{2,1,0:T(8,128)(2,1)S(1)} %all_to_all.36.recv_ref), custom_call_target="tpu_custom_call" | custom-call | tf_op jit(solution)/shard_map/backward_tiles/pallas_call | solution.py:217
  133.6 7.4 %all-to-all-done.5.refs_0_ = bf16[8,40,128]{2,1,0:T(8,128)(2,1)S(1)} async-done(((bf16[8,40,128]{2,1,0:T(8,128)(2,1)}), bf16[8,40,128]{2,1,0:T(8,128)(2,1)S(1)}, u32[]{:S(2)}, u32[]{:S(2)}) %all-to-all-start.5) | async-done | bytes 81952 | tf_op jit(solution)/shard_map/all_to_all | solution.py:290
  141.0 0.6 grad_chunk.1
  141.6 23.2 %all_to_all.37.refs_0_ = bf16[16,160,128]{2,1,0:T(8,128)(2,1)S(1)} all-to-all(bf16[16,160,128]{2,1,0:T(8,128)(2,1)S(1)} %get-tuple-element.22), channel_id=1, replica_groups=mesh['ylo'=2,'zq'=8,'z0'=2,'x'=4,'d0'=4] {'x','d0'}, dimensions={0} | all-to-all | bytes 1310720 | tf_op jit(solution)/shard_map/all_to_all | solution.py:304
  164.8 0.7 final_sums.1
  (7 shorter events, 0.1 us)
Async XLA Ops:
  0.6 23.1 %copy-start.12 = (s32[1,1,128]{2,1,0:T(1,128)S(1)}, s32[1,1,128]{2,1,0:T(1,128)}, u32[]{:S(2)}) copy-start(s32[1,1,128]{2,1,0:T(1,128)} %param.11) | copy-start | bytes 1540
  2.3 21.4 %all-to-all-start = ((bf16[16,128,128]{2,1,0:T(8,128)(2,1)}), bf16[16,128,128]{2,1,0:T(8,128)(2,1)S(1)}, u32[]{:S(2)}, u32[]{:S(2)}) async-start(bf16[16,128,128]{2,1,0:T(8,128)(2,1)} %broadcast_in_dim.2), calls=%async_computation | async-start | bytes 1048576 | tf_op jit(solution)/shard_map/all_to_all | solution.py:255
  12.5 0.8 copy-start.4
  13.3 0.7 copy-start.6
  14.0 0.7 copy-start.10
  19.2 2.0 %copy-start.2 = (bf16[128,128,128]{2,1,0:T(8,128)(2,1)}, bf16[128,128,128]{2,1,0:T(8,128)(2,1)S(1)}, u32[]{:S(2)}) copy-start(bf16[128,128,128]{2,1,0:T(8,128)(2,1)S(1)} %build_tiles.1.tile_ref) | copy-start | bytes 12582916
  23.7 2.2 %copy-start.3 = (bf16[128,128,128]{2,1,0:T(8,128)(2,1)S(1)}, bf16[128,128,128]{2,1,0:T(8,128)(2,1)}, u32[]{:S(2)}) copy-start(bf16[128,128,128]{2,1,0:T(8,128)(2,1)} %copy-done.2) | copy-start | bytes 12582916
  25.9 31.5 %copy-start.5 = (s32[1,1,128,64]{2,3,1,0:T(8,128)S(1)}, s32[1,1,128,64]{2,3,1,0:T(8,128)}, u32[]{:S(2)}) copy-start(s32[1,1,128,64]{2,3,1,0:T(8,128)} %param.13) | copy-start | bytes 98308
  25.9 31.5 %copy-start.7 = (bf16[1,1,128,64]{2,3,1,0:T(8,128)(2,1)S(1)}, bf16[1,1,128,64]{2,3,1,0:T(8,128)(2,1)}, u32[]{:S(2)}) copy-start(bf16[1,1,128,64]{2,3,1,0:T(8,128)(2,1)} %param.14) | copy-start | bytes 49156
  25.9 31.5 %copy-start.11 = (s32[1,1,128]{2,1,0:T(1,128)S(1)}, s32[1,1,128]{2,1,0:T(1,128)}, u32[]{:S(2)}) copy-start(s32[1,1,128]{2,1,0:T(1,128)} %param.12) | copy-start | bytes 1540
  28.6 45.6 %copy-start.8 = (bf16[128,256]{1,0:T(8,128)(2,1)S(1)}, bf16[128,256]{1,0:T(8,128)(2,1)}, u32[]{:S(2)}) copy-start(bf16[128,256]{1,0:T(8,128)(2,1)} %weight_ref.1) | copy-start | bytes 196612
  28.6 45.6 %copy-start.9 = (bf16[128,256]{1,0:T(8,128)(2,1)S(1)}, bf16[128,256]{1,0:T(8,128)(2,1)}, u32[]{:S(2)}) copy-start(bf16[128,256]{1,0:T(8,128)(2,1)} %grad_ref.1) | copy-start | bytes 196612
  28.6 45.6 %copy-start.13 = (f32[256]{0:T(256)S(1)}, f32[256]{0:T(256)}, u32[]{:S(2)}) copy-start(f32[256]{0:T(256)} %param.10) | copy-start | bytes 3076
  44.4 29.8 %all-to-all-start.2 = ((bf16[8,128,128]{2,1,0:T(8,128)(2,1)}), bf16[8,128,128]{2,1,0:T(8,128)(2,1)S(1)}, u32[]{:S(2)}, u32[]{:S(2)}) async-start(bf16[8,128,128]{2,1,0:T(8,128)(2,1)} %reduce_sum.24), calls=%async_computation.2 | async-start | bytes 524288 | tf_op jit(solution)/shard_map/all_to_all | solution.py:265
  62.0 2.0 %copy-start = (bf16[128,128,128]{2,1,0:T(8,128)(2,1)}, bf16[128,128,128]{2,1,0:T(8,128)(2,1)S(1)}, u32[]{:S(2)}) copy-start(bf16[128,128,128]{2,1,0:T(8,128)(2,1)S(1)} %build_back.1.tile_ref) | copy-start | bytes 12582916
  75.3 27.8 %all-to-all-start.3 = ((bf16[8,128,128]{2,1,0:T(8,128)(2,1)}), bf16[8,128,128]{2,1,0:T(8,128)(2,1)S(1)}, u32[]{:S(2)}, u32[]{:S(2)}) async-start(bf16[8,128,128]{2,1,0:T(8,128)(2,1)} %get-tuple-element.19), calls=%async_computation.3 | async-start | bytes 524288 | tf_op jit(solution)/shard_map/all_to_all | solution.py:275
  118.8 22.2 %all-to-all-start.5 = ((bf16[8,40,128]{2,1,0:T(8,128)(2,1)}), bf16[8,40,128]{2,1,0:T(8,128)(2,1)S(1)}, u32[]{:S(2)}, u32[]{:S(2)}) async-start(bf16[8,40,128]{2,1,0:T(8,128)(2,1)} %grad_share.1), calls=%async_computation.5 | async-start | bytes 163840 | tf_op jit(solution)/shard_map/all_to_all | solution.py:290
  128.7 2.2 %copy-start.1 = (bf16[128,128,128]{2,1,0:T(8,128)(2,1)S(1)}, bf16[128,128,128]{2,1,0:T(8,128)(2,1)}, u32[]{:S(2)}) copy-start(bf16[128,128,128]{2,1,0:T(8,128)(2,1)} %copy-done) | copy-start | bytes 12582916

commit v8 on v7

--- a/solution.py
+++ b/solution.py
@@ -18,6 +18,7 @@
 NEAR = ("ylo", "z0")
 FAR = "zq"
 GROUP = 32
+CHUNKS = 4
 
 
 def dot(a, b, dims=NN):
@@ -57,14 +58,23 @@
     lax.fori_loop(0, pairs, one_pair, 0, unroll=4)
 
 
-def spread_tiles(index_ref, tile_ref, rows_ref, sums, split, backward):
+def spread_tiles(index_ref, tile_hbm, rows_ref, sums, tile_ref, sems, split, backward, ready):
     shift = split.bit_length() - 1
+    slots = tile_ref.shape[0]
+    chunk = slots // CHUNKS
+    copies = []
+    for c in range(CHUNKS):
+        part = pl.ds(c * chunk, chunk)
+        copies.append(pltpu.make_async_copy(tile_hbm.at[part], tile_ref.at[part], sems.at[c]))
+    for copy in copies:
+        copy.start()
     sums[...] = jnp.zeros_like(sums)
-
-    def one_step(step, carry):
+    ready()
+    for start in range(0, slots, GROUP):
+        if start % chunk == 0:
+            copies[start // chunk].wait()
         found = []
-        for i in range(GROUP):
-            slot = step * GROUP + i
+        for slot in range(start, start + GROUP):
             index = index_ref[slot]
             target = index >> shift
             source = index & (split - 1)
@@ -74,14 +84,12 @@
                 found.append((target, dot(tile_ref[slot], rows_ref[source])))
         for place, value in found:
             sums[place] = sums[place] + value
-        return carry
-
-    lax.fori_loop(0, tile_ref.shape[0] // GROUP, one_step, 0)
-
-
-def forward_kernel(index_ref, tile_ref, rows_ref, out_ref, sums):
+
+
+def forward_kernel(index_ref, tile_hbm, rows_ref, out_ref, sums, tile_ref, sems):
     near, far = out_ref.shape[:2]
-    spread_tiles(index_ref, tile_ref, rows_ref, sums, rows_ref.shape[0], False)
+    split = rows_ref.shape[0]
+    spread_tiles(index_ref, tile_hbm, rows_ref, sums, tile_ref, sems, split, False, lambda: None)
     for target in range(near * far):
         place = target // (2 * far) * 2 + target % 2
         out_ref[place, target // 2 % far] = sums[target].astype(BF16)
@@ -147,11 +155,8 @@
     return jnp.concatenate([rows[:count] + rows[count : 2 * count], bias_rows], axis=0)
 
 
-def middle_kernel(place_ref, recv_ref, part_ref, out_ref):
-    near = out_ref.shape[0]
+def share_kernel(place_ref, part_ref, out_ref):
     peers = part_ref.shape[0]
-    top = recv_ref.shape[0] * TILE
-    back_rows = recv_ref[...].reshape(top, TILE)
     size = (part_ref.shape[1] - 8) // peers
     start = pl.multiple_of(place_ref[0] * size, 8)
     total = part_ref[0, pl.ds(start, size), :]
@@ -160,14 +165,11 @@
         total = total + part_ref[k, pl.ds(start, size), :]
         last = last + part_ref[k, peers * size :, :]
     extra = split_rows(jnp.concatenate([total, last], axis=0))
-    for k in range(near):
-        out_ref[k, :top] = back_rows
-        out_ref[k, top:] = extra
-
-
-def share_kernel(recv_ref, out_ref):
-    top = recv_ref.shape[1] - out_ref.shape[1]
-    total = jnp.sum(recv_ref[:, top:, :].astype(F32), axis=0)
+    out_ref[...] = jnp.broadcast_to(extra[None], out_ref.shape)
+
+
+def reshare_kernel(recv_ref, out_ref):
+    total = jnp.sum(recv_ref[...].astype(F32), axis=0)
     out_ref[...] = jnp.broadcast_to(split_rows(join_rows(total))[None], out_ref.shape)
 
 
@@ -193,14 +195,19 @@
         weight_grad_ref[start % TILE : start % TILE + size, lane : lane + TILE] = chunk
 
 
-def backward_kernel(index_ref, tile_ref, recv_ref, out_ref, rows, sums):
-    near = recv_ref.shape[0]
-    far = rows.shape[0] // near
+def backward_kernel(index_ref, own_ref, tile_hbm, *rest):
+    near_refs, (out_ref, sums, tile_ref, sems, rows) = rest[:-5], rest[-5:]
+    far = near_refs[0].shape[0]
     pieces = out_ref.shape[0]
-    for target in range(near * far):
-        start = target // 2 % far * TILE
-        rows[target] = recv_ref[target // (2 * far) * 2 + target % 2, start : start + TILE]
-    spread_tiles(index_ref, tile_ref, rows, sums, pieces, True)
+
+    def ready():
+        for k, near_ref in enumerate(near_refs):
+            other = own_ref[0] ^ k
+            base = (other >> 1) * (2 * far) + (other & 1)
+            for q in range(far):
+                rows[base + 2 * q] = near_ref[q]
+
+    spread_tiles(index_ref, tile_hbm, rows, sums, tile_ref, sems, pieces, True, ready)
     out_ref[...] = sums[...].astype(BF16)
 
 
@@ -230,6 +237,22 @@
     return jax.ShapeDtypeStruct(dims, dtype)
 
 
+def spread(kernel, name, out, scalars, tiles, arrays, scratch):
+    return pl.pallas_call(
+        kernel,
+        out_shape=out,
+        in_specs=smem(len(scalars)) + [pl.BlockSpec(memory_space=pltpu.HBM)] + vmem(len(arrays)),
+        out_specs=vmem(1)[0],
+        scratch_shapes=scratch,
+        compiler_params=pltpu.CompilerParams(vmem_limit_bytes=20 << 20),
+        name=name,
+    )(*scalars, pltpu.with_memory_space_constraint(tiles, pltpu.HBM), *arrays)
+
+
+def swap(array, step, axis):
+    return lax.ppermute(array, axis, [(i, i ^ step) for i in range(lax.axis_size(axis))])
+
+
 def body(features, weight, bias, tile_index, edge_count, edge_pos, edge_weight, grad_out):
     near = lax.axis_size(NEAR)
     far = lax.axis_size(FAR)
@@ -241,7 +264,7 @@
     positions = edge_pos.reshape(slots, -1).T
     weights = edge_weight.reshape(slots, -1).T
     edges = positions.shape[0]
-    tile_shape = shape((slots, TILE, TILE), BF16)
+    tile_shape = pltpu.HBM((slots, TILE, TILE), BF16)
     pair_scratch = (pltpu.VMEM((slots // 2, 2 * edges), jnp.int32), pltpu.VMEM((slots // 2, 2 * edges), F32))
 
     def build(positions, backward):
@@ -254,9 +277,10 @@
     sent = jnp.broadcast_to(features[None], (dst,) + features.shape)
     source_rows = lax.all_to_all(sent, DST, 0, 0, tiled=True)
     tiles = build(positions, False)
-    partial = call(
+    tile_scratch = [pltpu.VMEM((slots, TILE, TILE), BF16), pltpu.SemaphoreType.DMA((CHUNKS,))]
+    partial = spread(
         forward_kernel, "forward_tiles", shape((near, far, TILE, TILE), BF16),
-        (index,), (tiles, source_rows), [pltpu.VMEM((src, TILE, TILE), F32)],
+        (index,), tiles, (source_rows,), [pltpu.VMEM((src, TILE, TILE), F32)] + tile_scratch,
     )
     near_parts = lax.all_to_all(partial, NEAR, 0, 0, tiled=True)
     near_sums = jnp.sum(near_parts.astype(F32), axis=0).astype(BF16)
@@ -281,17 +305,17 @@
     )
     part = lax.all_gather(part, "x")
     size = 2 * TILE // dst
-    near_rows = call(
-        middle_kernel, "middle_sums", shape((near, far * TILE + 2 * size + 8, TILE), BF16),
-        (lax.axis_index("x").reshape(1),), (far_rows, part),
-    )
-    near_rows = lax.all_to_all(near_rows, NEAR, 0, 0, tiled=True)
-    share = call(share_kernel, "grad_share", shape((far, 2 * size + 8, TILE), BF16), (), (near_rows,))
+    share = call(
+        share_kernel, "grad_share", shape((far, 2 * size + 8, TILE), BF16), (lax.axis_index("x").reshape(1),), (part,)
+    )
     shared = lax.all_to_all(share, FAR, 0, 0, tiled=True)
-    back_send = call(
+    near_all = [far_rows] + [swap(far_rows, k, NEAR) for k in range(1, near)]
+    share = call(reshare_kernel, "grad_reshare", shape((near, 2 * size + 8, TILE), BF16), (), (shared,))
+    shared = lax.all_to_all(share, NEAR, 0, 0, tiled=True)
+    back_send = spread(
         backward_kernel, "backward_tiles", shape((dst, TILE, TILE), BF16),
-        (index,), (back_tiles, near_rows),
-        [pltpu.VMEM((src, TILE, TILE), BF16), pltpu.VMEM((dst, TILE, TILE), F32)],
+        (index, lax.axis_index(NEAR).reshape(1)), back_tiles, near_all,
+        [pltpu.VMEM((dst, TILE, TILE), F32)] + tile_scratch + [pltpu.VMEM((src, TILE, TILE), BF16)],
     )
     node_scale = 1.0 / math.sqrt(features.shape[0] * src * dst)
     back_send, bias_grad = call(

time: 166 us -> 159 us (0.958)
  blocking collectives: 74.6 us -> 59.8 us
  starting transfers between devices: 39 us -> 51.5 us
  local copies, waits for them, and re-layouts: 12.1 us -> 3.82 us
  Pallas kernels: 17.9 us -> 24.6 us
  waiting for transfers between devices: 20.2 us -> 16.9 us
    all_to_all x1 -> x0, blocking collectives: 15 us -> none  [body(): near_rows = lax.all_to_all(near_rows, NEAR, 0, 0, tiled=True)]
    ppermute x0 -> x3, starting transfers between devices: none -> 8.36 us  [swap(): lax.ppermute(array, axis, [(i, i ^ step) for i in range(lax.axis_size(axi...]
    unnamed x28 -> x20, local copies, waits for them, and re-layouts: 10.4 us -> 2.16 us
    pallas_call x0 -> x2, Pallas kernels: none -> 7.65 us  [spread(): pl.pallas_call(kernel, out_shape=out, in_specs=smem(len(scalars)) + [pl.B...]
    all_to_all x0 -> x1, starting transfers between devices: none -> 3.27 us  [body(): shared = lax.all_to_all(share, NEAR, 0, 0, tiled=True)]
    all_to_all x1, waiting for transfers between devices: 7.41 us -> 4.2 us  [body(): shared = lax.all_to_all(share, FAR, 0, 0, tiled=True)]
    pallas_call x11 -> x9, Pallas kernels: 17.9 us -> 16.9 us  [call(): pl.pallas_call(kernel, out_shape=outs, in_specs=smem(len(scalars)) + vmem...]
  transfers between devices with their start and end apart: 4 -> 8, of which waited for: 3 -> 3; matrix products, arithmetic and copies ran while one was open for 0% -> 0% of each run, Pallas kernels for 7% -> 12%
where the time goes in v8:
time: 159 us; the launch traced here: 158 us
  blocking collectives  59.8 us (38%)
  starting transfers between devices  51.5 us (32%)
  Pallas kernels  24.6 us (15%)
  waiting for transfers between devices  16.9 us (11%)
  local copies, waits for them, and re-layouts  3.82 us (2%)
    all_to_all x1, blocking collectives, body(): received = lax.all_to_all(back_send, DST, 0, 0, tiled=True)  23.3 us
    pallas_call x9, Pallas kernels, call(): pl.pallas_call(kernel, out_shape=outs, in_specs=smem(len(scalars)) + vmem...  16.9 us
    all_to_all x1, blocking collectives, body(): near_parts = lax.all_to_all(partial, NEAR, 0, 0, tiled=True)  14.8 us
    all_to_all x1, starting transfers between devices, body(): parts = lax.all_to_all(near_sums, FAR, 0, 0, tiled=True)  13 us
    all_gather x1, blocking collectives, body(): part = lax.all_gather(part, 'd0')  11.7 us
    all_to_all x1, starting transfers between devices, body(): shared = lax.all_to_all(share, FAR, 0, 0, tiled=True)  10.8 us
    all_to_all x1, starting transfers between devices, body(): source_rows = lax.all_to_all(sent, DST, 0, 0, tiled=True)  10.2 us
    all_to_all x1, waiting for transfers between devices, body(): parts = lax.all_to_all(near_sums, FAR, 0, 0, tiled=True)  10.1 us
  transfers between devices with their start and end apart: 8, of which 3 were waited for; matrix products, arithmetic and copies ran while one was open for 0% of the time, Pallas kernels for 12%

profile of v8, /device:TPU:1, one launch (start us, length us, event | category | flops | bytes accessed | tf_op | source)
XLA Modules:
  0.0 158.5 jit_solution(8157241667318648102)
XLA Ops:
  0.6 0.0 copy-start.8
  0.6 1.7 %broadcast_in_dim.2 = bf16[16,128,128]{2,1,0:T(8,128)(2,1)} broadcast(bf16[128,128]{1,0:T(8,128)(2,1)} %param.8), dimensions={1,2} | broadcast | bytes 557056 | tf_op jit(solution)/shard_map/broadcast_in_dim | solution.py:277
  2.3 10.2 %all-to-all-start = ((bf16[16,128,128]{2,1,0:T(8,128)(2,1)}), bf16[16,128,128]{2,1,0:T(8,128)(2,1)S(1)}, u32[]{:S(2)}, u32[]{:S(2)}) async-start(bf16[16,128,128]{2,1,0:T(8,128)(2,1)} %broadcast_in_dim.2), calls=%async_computation | async-start | bytes 1048576 | tf_op jit(solution)/shard_map/all_to_all | solution.py:278
  12.6 0.8 copy-done
  13.3 0.0 copy-start.2
  13.3 0.7 copy-done.2
  14.0 0.0 copy-start.6
  14.0 0.7 copy-done.6
  14.7 6.5 %build_tiles.1.tile_hbm = bf16[128,128,128]{2,1,0:T(8,128)(2,1)} custom-call(s32[128]{0:T(128)S(1)} %bitcast.21, s32[64,128]{1,0:T(8,128)S(1)} %bitcast.17, bf16[64,128]{1,0:T(8,128)(2,1)S(1)} %bitcast.19), custom_call_target="tpu_custom_call" | custom-call | tf_op jit(solution)/shard_map/build_tiles/pallas_call | solution.py:224
  21.2 2.6 %all-to-all-done.rows_ref = bf16[16,128,128]{2,1,0:T(8,128)(2,1)S(1)} async-done(((bf16[16,128,128]{2,1,0:T(8,128)(2,1)}), bf16[16,128,128]{2,1,0:T(8,128)(2,1)S(1)}, u32[]{:S(2)}, u32[]{:S(2)}) %all-to-all-start) | async-done | bytes 524320 | tf_op jit(solution)/shard_map/all_to_all | solution.py:278
  23.7 0.0 copy-done.8
  23.8 3.8 %forward_tiles.1 = bf16[4,8,128,128]{3,2,1,0:T(8,128)(2,1)S(1)} custom-call(s32[128]{0:T(128)S(1)} %bitcast.23, bf16[128,128,128]{2,1,0:T(8,128)(2,1)} %build_tiles.1.tile_hbm, bf16[16,128,128]{2,1,0:T(8,128)(2,1)S(1)} %all-to-all-done.rows_ref), custom_call_target="tpu_custom_call" | custom-call | tf_op jit(solution)/shard_map/forward_tiles/pallas_call | solution.py:241
  27.6 0.0 copy-start.4
  27.6 0.0 copy-start.5
  27.6 0.0 copy-start.9
  27.6 14.8 %all_to_all.35 = bf16[4,8,128,128]{3,2,1,0:T(8,128)(2,1)S(1)} all-to-all(bf16[4,8,128,128]{3,2,1,0:T(8,128)(2,1)S(1)} %forward_tiles.1), channel_id=1, replica_groups=mesh['ylo'=2,'zq'=8,'z0'=2,'x'=4,'d0'=4] {'ylo','z0'}, dimensions={0} | all-to-all | bytes 2097152 | tf_op jit(solution)/shard_map/all_to_all | solution.py:285
  42.5 0.9 reduce_sum.24
  43.4 13.0 %all-to-all-start.2 = ((bf16[8,128,128]{2,1,0:T(8,128)(2,1)}), bf16[8,128,128]{2,1,0:T(8,128)(2,1)S(1)}, u32[]{:S(2)}, u32[]{:S(2)}) async-start(bf16[8,128,128]{2,1,0:T(8,128)(2,1)} %reduce_sum.24), calls=%async_computation.2 | async-start | bytes 524288 | tf_op jit(solution)/shard_map/all_to_all | solution.py:289
  56.4 0.0 copy-done.1
  56.4 0.0 copy-done.3
  56.4 0.0 copy-done.7
  56.4 6.5 %build_back.1.tile_hbm = bf16[128,128,128]{2,1,0:T(8,128)(2,1)} custom-call(s32[128]{0:T(128)S(1)} %bitcast.22, s32[64,128]{1,0:T(8,128)S(1)} %bitcast.18, bf16[64,128]{1,0:T(8,128)(2,1)S(1)} %bitcast.20), custom_call_target="tpu_custom_call" | custom-call | tf_op jit(solution)/shard_map/build_back/pallas_call | solution.py:224
  62.9 10.1 %all-to-all-done.2 = bf16[8,128,128]{2,1,0:T(8,128)(2,1)S(1)} async-done(((bf16[8,128,128]{2,1,0:T(8,128)(2,1)}), bf16[8,128,128]{2,1,0:T(8,128)(2,1)S(1)}, u32[]{:S(2)}, u32[]{:S(2)}) %all-to-all-start.2) | async-done | bytes 262176 | tf_op jit(solution)/shard_map/all_to_all | solution.py:289
  73.1 0.0 copy-done.4
  73.1 0.0 copy-done.5
  73.1 0.0 copy-done.9
  73.1 1.1 dense_layer.1
  74.2 5.9 %all-to-all-start.5 = ((bf16[8,128,128]{2,1,0:T(8,128)(2,1)}), bf16[8,128,128]{2,1,0:T(8,128)(2,1)S(1)}, u32[]{:S(2)}, u32[]{:S(2)}) async-start(bf16[8,128,128]{2,1,0:T(8,128)(2,1)} %get-tuple-element.21), calls=%async_computation.5 | async-start | bytes 524288 | tf_op jit(solution)/shard_map/all_to_all | solution.py:299
  80.1 0.2 grad_part.1
  80.3 11.7 %all-gather = f32[1056,128]{1,0:T(8,128)S(1)} all-gather(f32[264,128]{1,0:T(8,128)S(1)} %grad_part.1), channel_id=2, replica_groups=mesh['ylo'=2,'zq'=8,'z0'=2,'x'=4,'d0'=4] {'d0'}, dimensions={0}, use_global_device_ids=true | all-gather | bytes 675840 | tf_op jit(solution)/shard_map/all_gather | solution.py:302
  92.0 10.0 %all-gather.1 = f32[288,128]{1,0:T(8,128)S(1)} all-gather(f32[72,128]{1,0:T(8,128)S(1)} %grad_pick.1), channel_id=3, replica_groups=mesh['ylo'=2,'zq'=8,'z0'=2,'x'=4,'d0'=4] {'x'}, dimensions={0}, use_global_device_ids=true | all-gather | bytes 184320 | tf_op jit(solution)/shard_map/all_gather | solution.py:306
  102.0 0.6 grad_share.1
  102.7 0.0 all-to-all-done.5.rest_0_
  102.7 10.8 %all-to-all-start.3 = ((bf16[8,40,128]{2,1,0:T(8,128)(2,1)}), bf16[8,40,128]{2,1,0:T(8,128)(2,1)S(1)}, u32[]{:S(2)}, u32[]{:S(2)}) async-start(bf16[8,40,128]{2,1,0:T(8,128)(2,1)} %grad_share.1), calls=%async_computation.3 | async-start | bytes 163840 | tf_op jit(solution)/shard_map/all_to_all | solution.py:311
  113.4 2.1 %collective-permute-start = (bf16[8,128,128]{2,1,0:T(8,128)(2,1)S(1)}, bf16[8,128,128]{2,1,0:T(8,128)(2,1)S(1)}, u32[]{:S(2)}, u32[]{:S(2)}) collective-permute-start(bf16[8,128,128]{2,1,0:T(8,128)(2,1)S(1)} %all-to-all-done.5.rest_0_), channel_id=1, source_target_pairs={{0,16},{16,0},{256,272},{272,256},{1,17},{17,1},{257,273},{273,257... | collective-permute-start | bytes 786440 | tf_op jit(solution)/shard_map/ppermute | solution.py:253
  115.5 2.3 %collective-permute-start.1 = (bf16[8,128,128]{2,1,0:T(8,128)(2,1)S(1)}, bf16[8,128,128]{2,1,0:T(8,128)(2,1)S(1)}, u32[]{:S(2)}, u32[]{:S(2)}) collective-permute-start(bf16[8,128,128]{2,1,0:T(8,128)(2,1)S(1)} %all-to-all-done.5.rest_0_), channel_id=1, source_target_pairs={{0,256},{16,272},{256,0},{272,16},{1,257},{17,273},{257,1},{273,17... | collective-permute-start | bytes 786440 | tf_op jit(solution)/shard_map/ppermute | solution.py:253
  117.9 4.0 %collective-permute-start.2 = (bf16[8,128,128]{2,1,0:T(8,128)(2,1)S(1)}, bf16[8,128,128]{2,1,0:T(8,128)(2,1)S(1)}, u32[]{:S(2)}, u32[]{:S(2)}) collective-permute-start(bf16[8,128,128]{2,1,0:T(8,128)(2,1)S(1)} %all-to-all-done.5.rest_0_), channel_id=1, source_target_pairs={{0,272},{16,256},{256,16},{272,0},{1,273},{17,257},{257,17},{273,1... | collective-permute-start | bytes 786440 | tf_op jit(solution)/shard_map/ppermute | solution.py:253
  121.8 4.2 %all-to-all-done.3.recv_ref = bf16[8,40,128]{2,1,0:T(8,128)(2,1)S(1)} async-done(((bf16[8,40,128]{2,1,0:T(8,128)(2,1)}), bf16[8,40,128]{2,1,0:T(8,128)(2,1)S(1)}, u32[]{:S(2)}, u32[]{:S(2)}) %all-to-all-start.3) | async-done | bytes 81952 | tf_op jit(solution)/shard_map/all_to_all | solution.py:311
  126.0 0.6 grad_reshare.1
  126.7 3.3 %all-to-all-start.4 = ((bf16[4,40,128]{2,1,0:T(8,128)(2,1)}), bf16[4,40,128]{2,1,0:T(8,128)(2,1)S(1)}, u32[]{:S(2)}, u32[]{:S(2)}) async-start(bf16[4,40,128]{2,1,0:T(8,128)(2,1)} %grad_reshare.1), calls=%async_computation.4 | async-start | bytes 81920 | tf_op jit(solution)/shard_map/all_to_all | solution.py:314
  130.0 0.0 collective-permute-done.rest_1_
  130.0 0.0 collective-permute-done.1.rest_2_
  130.0 0.0 collective-permute-done.2.rest_3_
  130.0 3.8 %backward_tiles.1.refs_1_ = bf16[16,128,128]{2,1,0:T(8,128)(2,1)S(1)} custom-call(s32[128]{0:T(128)S(1)} %bitcast.24, s32[1]{0:T(128)} %bitcast.13.own_ref, bf16[128,128,128]{2,1,0:T(8,128)(2,1)} %build_back.1.tile_hbm, bf16[8,128,128]{2,1,0:T(8,128)(2,1)S(1)} %all-to-all-done.5.rest_0_, bf16[8,128,128]{2,1,0:T(8,128)(2,1)S(1)} %collective-permute-done.rest_1_, ...), custom_call_target="tpu_custom_call" | custom-call | tf_op jit(solution)/shard_map/backward_tiles/pallas_call | solution.py:241
  133.8 0.0 all-to-all-done.4.refs_0_
  133.8 0.6 grad_chunk.1
  134.4 23.3 %all_to_all.36.refs_0_ = bf16[16,160,128]{2,1,0:T(8,128)(2,1)S(1)} all-to-all(bf16[16,160,128]{2,1,0:T(8,128)(2,1)S(1)} %get-tuple-element.22), channel_id=1, replica_groups=mesh['ylo'=2,'zq'=8,'z0'=2,'x'=4,'d0'=4] {'x','d0'}, dimensions={0} | all-to-all | bytes 1310720 | tf_op jit(solution)/shard_map/all_to_all | solution.py:328
  157.7 0.7 final_sums.1
  (6 shorter events, 0.1 us)
Async XLA Ops:
  0.6 23.1 %copy-start.8 = (s32[1,1,128]{2,1,0:T(1,128)S(1)}, s32[1,1,128]{2,1,0:T(1,128)}, u32[]{:S(2)}) copy-start(s32[1,1,128]{2,1,0:T(1,128)} %param.11) | copy-start | bytes 1540
  2.3 21.4 %all-to-all-start = ((bf16[16,128,128]{2,1,0:T(8,128)(2,1)}), bf16[16,128,128]{2,1,0:T(8,128)(2,1)S(1)}, u32[]{:S(2)}, u32[]{:S(2)}) async-start(bf16[16,128,128]{2,1,0:T(8,128)(2,1)} %broadcast_in_dim.2), calls=%async_computation | async-start | bytes 1048576 | tf_op jit(solution)/shard_map/all_to_all | solution.py:278
  12.5 0.8 copy-start
  13.3 0.7 copy-start.2
  14.0 0.7 copy-start.6
  23.7 32.6 %copy-start.1 = (s32[1,1,128,64]{2,3,1,0:T(8,128)S(1)}, s32[1,1,128,64]{2,3,1,0:T(8,128)}, u32[]{:S(2)}) copy-start(s32[1,1,128,64]{2,3,1,0:T(8,128)} %param.13) | copy-start | bytes 98308
  23.7 32.6 %copy-start.3 = (bf16[1,1,128,64]{2,3,1,0:T(8,128)(2,1)S(1)}, bf16[1,1,128,64]{2,3,1,0:T(8,128)(2,1)}, u32[]{:S(2)}) copy-start(bf16[1,1,128,64]{2,3,1,0:T(8,128)(2,1)} %param.14) | copy-start | bytes 49156
  23.7 32.6 %copy-start.7 = (s32[1,1,128]{2,1,0:T(1,128)S(1)}, s32[1,1,128]{2,1,0:T(1,128)}, u32[]{:S(2)}) copy-start(s32[1,1,128]{2,1,0:T(1,128)} %param.12) | copy-start | bytes 1540
  27.6 45.5 %copy-start.4 = (bf16[128,256]{1,0:T(8,128)(2,1)S(1)}, bf16[128,256]{1,0:T(8,128)(2,1)}, u32[]{:S(2)}) copy-start(bf16[128,256]{1,0:T(8,128)(2,1)} %weight_ref.1) | copy-start | bytes 196612
  27.6 45.5 %copy-start.5 = (bf16[128,256]{1,0:T(8,128)(2,1)S(1)}, bf16[128,256]{1,0:T(8,128)(2,1)}, u32[]{:S(2)}) copy-start(bf16[128,256]{1,0:T(8,128)(2,1)} %grad_ref.1) | copy-start | bytes 196612
  27.6 45.5 %copy-start.9 = (f32[256]{0:T(256)S(1)}, f32[256]{0:T(256)}, u32[]{:S(2)}) copy-start(f32[256]{0:T(256)} %param.10) | copy-start | bytes 3076
  43.4 29.7 %all-to-all-start.2 = ((bf16[8,128,128]{2,1,0:T(8,128)(2,1)}), bf16[8,128,128]{2,1,0:T(8,128)(2,1)S(1)}, u32[]{:S(2)}, u32[]{:S(2)}) async-start(bf16[8,128,128]{2,1,0:T(8,128)(2,1)} %reduce_sum.24), calls=%async_computation.2 | async-start | bytes 524288 | tf_op jit(solution)/shard_map/all_to_all | solution.py:289
  74.2 28.5 %all-to-all-start.5 = ((bf16[8,128,128]{2,1,0:T(8,128)(2,1)}), bf16[8,128,128]{2,1,0:T(8,128)(2,1)S(1)}, u32[]{:S(2)}, u32[]{:S(2)}) async-start(bf16[8,128,128]{2,1,0:T(8,128)(2,1)} %get-tuple-element.21), calls=%async_computation.5 | async-start | bytes 524288 | tf_op jit(solution)/shard_map/all_to_all | solution.py:299
  102.7 23.3 %all-to-all-start.3 = ((bf16[8,40,128]{2,1,0:T(8,128)(2,1)}), bf16[8,40,128]{2,1,0:T(8,128)(2,1)S(1)}, u32[]{:S(2)}, u32[]{:S(2)}) async-start(bf16[8,40,128]{2,1,0:T(8,128)(2,1)} %grad_share.1), calls=%async_computation.3 | async-start | bytes 163840 | tf_op jit(solution)/shard_map/all_to_all | solution.py:311
  113.4 16.5 %collective-permute-start = (bf16[8,128,128]{2,1,0:T(8,128)(2,1)S(1)}, bf16[8,128,128]{2,1,0:T(8,128)(2,1)S(1)}, u32[]{:S(2)}, u32[]{:S(2)}) collective-permute-start(bf16[8,128,128]{2,1,0:T(8,128)(2,1)S(1)} %all-to-all-done.5.rest_0_), channel_id=1, source_target_pairs={{0,16},{16,0},{256,272},{272,256},{1,17},{17,1},{257,273},{273,257... | collective-permute-start | bytes 786440 | tf_op jit(solution)/shard_map/ppermute | solution.py:253
  115.5 14.5 %collective-permute-start.1 = (bf16[8,128,128]{2,1,0:T(8,128)(2,1)S(1)}, bf16[8,128,128]{2,1,0:T(8,128)(2,1)S(1)}, u32[]{:S(2)}, u32[]{:S(2)}) collective-permute-start(bf16[8,128,128]{2,1,0:T(8,128)(2,1)S(1)} %all-to-all-done.5.rest_0_), channel_id=1, source_target_pairs={{0,256},{16,272},{256,0},{272,16},{1,257},{17,273},{257,1},{273,17... | collective-permute-start | bytes 786440 | tf_op jit(solution)/shard_map/ppermute | solution.py:253
  117.9 12.1 %collective-permute-start.2 = (bf16[8,128,128]{2,1,0:T(8,128)(2,1)S(1)}, bf16[8,128,128]{2,1,0:T(8,128)(2,1)S(1)}, u32[]{:S(2)}, u32[]{:S(2)}) collective-permute-start(bf16[8,128,128]{2,1,0:T(8,128)(2,1)S(1)} %all-to-all-done.5.rest_0_), channel_id=1, source_target_pairs={{0,272},{16,256},{256,16},{272,0},{1,273},{17,257},{257,17},{273,1... | collective-permute-start | bytes 786440 | tf_op jit(solution)/shard_map/ppermute | solution.py:253
  126.7 7.1 %all-to-all-start.4 = ((bf16[4,40,128]{2,1,0:T(8,128)(2,1)}), bf16[4,40,128]{2,1,0:T(8,128)(2,1)S(1)}, u32[]{:S(2)}, u32[]{:S(2)}) async-start(bf16[4,40,128]{2,1,0:T(8,128)(2,1)} %grad_reshare.1), calls=%async_computation.4 | async-start | bytes 81920 | tf_op jit(solution)/shard_map/all_to_all | solution.py:314

commit v9 on v8

--- a/solution.py
+++ b/solution.py
@@ -123,65 +123,57 @@
 
 def part_kernel(agg_ref, grad_pre_ref, out_ref):
     grad_pre = grad_pre_ref[...]
-    part = dot(agg_ref[...], grad_pre, TN)
+    part = dot(agg_ref[...], grad_pre, TN).astype(BF16)
     out_ref[:TILE] = part[:, :TILE]
     out_ref[TILE : 2 * TILE] = part[:, TILE:]
     bias_part = jnp.sum(grad_pre.astype(F32), axis=0, keepdims=True)
-    bias_rows = [bias_part[:, :TILE], bias_part[:, TILE:], jnp.zeros((6, TILE), F32)]
-    out_ref[2 * TILE :] = jnp.concatenate(bias_rows, axis=0)
+    out_ref[2 * TILE :] = bias_tile(jnp.concatenate([bias_part[:, :TILE], bias_part[:, TILE:]], axis=0))
+
+
+def pick_rows(place, recv_ref, size):
+    peers = recv_ref.shape[0]
+    start = pl.multiple_of(place * size, 8)
+    total = recv_ref[0, pl.ds(start, size), :].astype(F32)
+    last = recv_ref[0, peers * size :, :].astype(F32)
+    for k in range(1, peers):
+        total = total + recv_ref[k, pl.ds(start, size), :].astype(F32)
+        last = last + recv_ref[k, peers * size :, :].astype(F32)
+    return total, last
 
 
 def pick_kernel(place_ref, recv_ref, out_ref):
-    peers = recv_ref.shape[0]
     size = out_ref.shape[0] - 8
-    start = pl.multiple_of(place_ref[0] * size, 8)
-    total = recv_ref[0, pl.ds(start, size), :]
-    last = recv_ref[0, peers * size :, :]
-    for k in range(1, peers):
-        total = total + recv_ref[k, pl.ds(start, size), :]
-        last = last + recv_ref[k, peers * size :, :]
-    out_ref[:size] = total
-    out_ref[size:] = last
-
-
-def split_rows(total):
-    high, low = high_low(total[:-8])
-    return jnp.concatenate([high.astype(BF16), low.astype(BF16), bias_tile(total[-8:])], axis=0)
-
-
-def join_rows(rows):
-    count = (rows.shape[0] - 8) // 2
-    bias_rows = jnp.concatenate([bias_sum(rows[2 * count :]), jnp.zeros((6, TILE), F32)], axis=0)
-    return jnp.concatenate([rows[:count] + rows[count : 2 * count], bias_rows], axis=0)
+    out_ref[:size], out_ref[size:] = pick_rows(place_ref[0], recv_ref, size)
 
 
 def share_kernel(place_ref, part_ref, out_ref):
-    peers = part_ref.shape[0]
-    size = (part_ref.shape[1] - 8) // peers
-    start = pl.multiple_of(place_ref[0] * size, 8)
-    total = part_ref[0, pl.ds(start, size), :]
-    last = part_ref[0, peers * size :, :]
-    for k in range(1, peers):
-        total = total + part_ref[k, pl.ds(start, size), :]
-        last = last + part_ref[k, peers * size :, :]
-    extra = split_rows(jnp.concatenate([total, last], axis=0))
-    out_ref[...] = jnp.broadcast_to(extra[None], out_ref.shape)
+    size = (part_ref.shape[1] - 8) // part_ref.shape[0]
+    total, last = pick_rows(place_ref[0], part_ref, size)
+    rows = jnp.concatenate([total.astype(BF16), bias_tile(bias_sum(last))], axis=0)
+    out_ref[...] = jnp.broadcast_to(rows[None], out_ref.shape)
 
 
 def reshare_kernel(recv_ref, out_ref):
     total = jnp.sum(recv_ref[...].astype(F32), axis=0)
-    out_ref[...] = jnp.broadcast_to(split_rows(join_rows(total))[None], out_ref.shape)
+    size = (out_ref.shape[1] - 8) // 2
+    high, low = high_low(total[:size])
+    rows = [high.astype(BF16), low.astype(BF16), bias_tile(bias_sum(total[size:]))]
+    out_ref[...] = jnp.broadcast_to(jnp.concatenate(rows, axis=0)[None], out_ref.shape)
 
 
 def chunk_kernel(recv_ref, back_ref, out_ref, bias_grad_ref, *, scale):
-    total = join_rows(jnp.sum(recv_ref[...].astype(F32), axis=0)) * scale
-    size = total.shape[0] - 8
-    bias_grad_ref[:, :TILE] = total[size : size + 1]
-    bias_grad_ref[:, TILE:] = total[size + 1 : size + 2]
-    high, low = high_low(total[:size])
-    both = jnp.concatenate([high, low], axis=0).astype(BF16)
+    total = jnp.sum(recv_ref[...].astype(F32), axis=0) * scale
+    size = (total.shape[0] - 8) // 2
+    bias_rows = bias_sum(total[2 * size :])
+    bias_grad_ref[:, :TILE] = bias_rows[0:1]
+    bias_grad_ref[:, TILE:] = bias_rows[1:2]
+    chunk = (total[:size] + total[size : 2 * size]).astype(BF16)
     out_ref[:, :TILE, :] = back_ref[...]
-    out_ref[:, TILE:, :] = jnp.broadcast_to(both[None], (out_ref.shape[0], 2 * size, TILE))
+    out_ref[:, TILE:, :] = jnp.broadcast_to(chunk[None], (out_ref.shape[0], size, TILE))
+
+
+def copies_kernel(rows_ref, out_ref):
+    out_ref[...] = jnp.broadcast_to(rows_ref[...][None], out_ref.shape)
 
 
 def final_kernel(recv_ref, input_ref, weight_grad_ref, *, group):
@@ -190,7 +182,7 @@
     size = 2 * TILE // pieces
     for d in range(pieces):
         start = ((d % group) * (pieces // group) + d // group) * size
-        chunk = recv_ref[d, TILE : TILE + size, :].astype(F32) + recv_ref[d, TILE + size :, :].astype(F32)
+        chunk = recv_ref[d, TILE:, :].astype(F32)
         lane = start // TILE * TILE
         weight_grad_ref[start % TILE : start % TILE + size, lane : lane + TILE] = chunk
 
@@ -274,7 +266,7 @@
             tile_shape, (counts,), (positions, weights), pair_scratch,
         )
 
-    sent = jnp.broadcast_to(features[None], (dst,) + features.shape)
+    sent = call(copies_kernel, "feature_copies", shape((dst,) + features.shape, BF16), (), (features,))
     source_rows = lax.all_to_all(sent, DST, 0, 0, tiled=True)
     tiles = build(positions, False)
     tile_scratch = [pltpu.VMEM((slots, TILE, TILE), BF16), pltpu.SemaphoreType.DMA((CHUNKS,))]
@@ -298,7 +290,7 @@
     )
     far_rows = lax.all_to_all(send, FAR, 0, 0, tiled=True)
     group = lax.axis_size("d0")
-    part = call(part_kernel, "grad_part", shape((2 * TILE + 8, TILE), F32), (), (aggregated, grad_pre))
+    part = call(part_kernel, "grad_part", shape((2 * TILE + 8, TILE), BF16), (), (aggregated, grad_pre))
     part = lax.all_gather(part, "d0")
     part = call(
         pick_kernel, "grad_pick", shape((2 * TILE // group + 8, TILE), F32), (lax.axis_index("d0").reshape(1),), (part,)
@@ -306,7 +298,7 @@
     part = lax.all_gather(part, "x")
     size = 2 * TILE // dst
     share = call(
-        share_kernel, "grad_share", shape((far, 2 * size + 8, TILE), BF16), (lax.axis_index("x").reshape(1),), (part,)
+        share_kernel, "grad_share", shape((far, size + 8, TILE), BF16), (lax.axis_index("x").reshape(1),), (part,)
     )
     shared = lax.all_to_all(share, FAR, 0, 0, tiled=True)
     near_all = [far_rows] + [swap(far_rows, k, NEAR) for k in range(1, near)]
@@ -321,7 +313,7 @@
     back_send, bias_grad = call(
         lambda *refs: chunk_kernel(*refs, scale=node_scale),
         "grad_chunk",
-        (shape((dst, TILE + 2 * size, TILE), BF16), shape((1, 2 * TILE), F32)),
+        (shape((dst, TILE + size, TILE), BF16), shape((1, 2 * TILE), F32)),
         (),
         (shared, back_send),
     )

time: 159 us -> 158 us (level)
    broadcast_in_dim x1 -> x0, local copies, waits for them, and re-layouts: 1.67 us -> none  [body(): sent = jnp.broadcast_to(features[None], (dst,) + features.shape)]
    pallas_call x9 -> x10, Pallas kernels: 16.9 us -> 17.8 us  [call(): pl.pallas_call(kernel, out_shape=outs, in_specs=smem(len(scalars)) + vmem...]
where the time goes in v9:
time: 158 us; the launch traced here: 157 us
  blocking collectives  58.5 us (37%)
  starting transfers between devices  51.5 us (33%)
  Pallas kernels  25.4 us (16%)
  waiting for transfers between devices  16.6 us (11%)
  local copies, waits for them, and re-layouts  2.91 us (2%)
    all_to_all x1, blocking collectives, body(): received = lax.all_to_all(back_send, DST, 0, 0, tiled=True)  22.9 us
    pallas_call x10, Pallas kernels, call(): pl.pallas_call(kernel, out_shape=outs, in_specs=smem(len(scalars)) + vmem...  17.8 us
    all_to_all x1, blocking collectives, body(): near_parts = lax.all_to_all(partial, NEAR, 0, 0, tiled=True)  14.8 us
    all_to_all x1, starting transfers between devices, body(): parts = lax.all_to_all(near_sums, FAR, 0, 0, tiled=True)  13 us
    all_to_all x1, starting transfers between devices, body(): shared = lax.all_to_all(share, FAR, 0, 0, tiled=True)  10.8 us
    all_gather x1, blocking collectives, body(): part = lax.all_gather(part, 'd0')  10.4 us
    all_gather x1, blocking collectives, body(): part = lax.all_gather(part, 'x')  10.4 us
    all_to_all x1, starting transfers between devices, body(): source_rows = lax.all_to_all(sent, DST, 0, 0, tiled=True)  10.2 us
  transfers between devices with their start and end apart: 8, of which 3 were waited for; matrix products, arithmetic and copies ran while one was open for 0% of the time, Pallas kernels for 12%

profile of v9, /device:TPU:1, one launch (start us, length us, event | category | flops | bytes accessed | tf_op | source)
XLA Modules:
  0.0 156.7 jit_solution(972909075729835644)
XLA Ops:
  0.6 0.0 copy-start.6
  0.6 0.7 copy-done.6
  1.4 0.0 copy-start.9
  1.4 0.9 feature_copies.1
  2.3 10.2 %all-to-all-start = ((bf16[16,128,128]{2,1,0:T(8,128)(2,1)}), bf16[16,128,128]{2,1,0:T(8,128)(2,1)S(1)}, u32[]{:S(2)}, u32[]{:S(2)}) async-start(bf16[16,128,128]{2,1,0:T(8,128)(2,1)} %feature_copies.1), calls=%async_computation | async-start | bytes 1048576 | tf_op jit(solution)/shard_map/all_to_all | solution.py:270
  12.5 0.8 copy-done
  13.3 0.7 copy-done.2
  14.0 0.7 copy-done.7
  14.7 6.5 %build_tiles.1.tile_hbm = bf16[128,128,128]{2,1,0:T(8,128)(2,1)} custom-call(s32[128]{0:T(128)S(1)} %bitcast.21, s32[64,128]{1,0:T(8,128)S(1)} %bitcast.17, bf16[64,128]{1,0:T(8,128)(2,1)S(1)} %bitcast.19), custom_call_target="tpu_custom_call" | custom-call | tf_op jit(solution)/shard_map/build_tiles/pallas_call | solution.py:216
  21.1 2.6 %all-to-all-done.rows_ref = bf16[16,128,128]{2,1,0:T(8,128)(2,1)S(1)} async-done(((bf16[16,128,128]{2,1,0:T(8,128)(2,1)}), bf16[16,128,128]{2,1,0:T(8,128)(2,1)S(1)}, u32[]{:S(2)}, u32[]{:S(2)}) %all-to-all-start) | async-done | bytes 524320 | tf_op jit(solution)/shard_map/all_to_all | solution.py:270
  23.7 0.0 copy-done.9
  23.7 3.8 %forward_tiles.1 = bf16[4,8,128,128]{3,2,1,0:T(8,128)(2,1)S(1)} custom-call(s32[128]{0:T(128)S(1)} %bitcast.23, bf16[128,128,128]{2,1,0:T(8,128)(2,1)} %build_tiles.1.tile_hbm, bf16[16,128,128]{2,1,0:T(8,128)(2,1)S(1)} %all-to-all-done.rows_ref), custom_call_target="tpu_custom_call" | custom-call | tf_op jit(solution)/shard_map/forward_tiles/pallas_call | solution.py:233
  27.6 0.0 copy-start.4
  27.6 0.0 copy-start.5
  27.6 0.0 copy-start.10
  27.6 14.8 %all_to_all.35 = bf16[4,8,128,128]{3,2,1,0:T(8,128)(2,1)S(1)} all-to-all(bf16[4,8,128,128]{3,2,1,0:T(8,128)(2,1)S(1)} %forward_tiles.1), channel_id=1, replica_groups=mesh['ylo'=2,'zq'=8,'z0'=2,'x'=4,'d0'=4] {'ylo','z0'}, dimensions={0} | all-to-all | bytes 2097152 | tf_op jit(solution)/shard_map/all_to_all | solution.py:277
  42.4 0.9 reduce_sum.24
  43.4 13.0 %all-to-all-start.2 = ((bf16[8,128,128]{2,1,0:T(8,128)(2,1)}), bf16[8,128,128]{2,1,0:T(8,128)(2,1)S(1)}, u32[]{:S(2)}, u32[]{:S(2)}) async-start(bf16[8,128,128]{2,1,0:T(8,128)(2,1)} %reduce_sum.24), calls=%async_computation.2 | async-start | bytes 524288 | tf_op jit(solution)/shard_map/all_to_all | solution.py:281
  56.4 0.0 copy-done.1
  56.4 0.0 copy-done.3
  56.4 0.0 copy-done.8
  56.4 6.5 %build_back.1.tile_hbm = bf16[128,128,128]{2,1,0:T(8,128)(2,1)} custom-call(s32[128]{0:T(128)S(1)} %bitcast.22, s32[64,128]{1,0:T(8,128)S(1)} %bitcast.18, bf16[64,128]{1,0:T(8,128)(2,1)S(1)} %bitcast.20), custom_call_target="tpu_custom_call" | custom-call | tf_op jit(solution)/shard_map/build_back/pallas_call | solution.py:216
  62.9 10.2 %all-to-all-done.2 = bf16[8,128,128]{2,1,0:T(8,128)(2,1)S(1)} async-done(((bf16[8,128,128]{2,1,0:T(8,128)(2,1)}), bf16[8,128,128]{2,1,0:T(8,128)(2,1)S(1)}, u32[]{:S(2)}, u32[]{:S(2)}) %all-to-all-start.2) | async-done | bytes 262176 | tf_op jit(solution)/shard_map/all_to_all | solution.py:281
  73.2 0.0 copy-done.4
  73.2 0.0 copy-done.5
  73.2 0.0 copy-done.10
  73.2 1.1 dense_layer.1
  74.2 5.9 %all-to-all-start.5 = ((bf16[8,128,128]{2,1,0:T(8,128)(2,1)}), bf16[8,128,128]{2,1,0:T(8,128)(2,1)S(1)}, u32[]{:S(2)}, u32[]{:S(2)}) async-start(bf16[8,128,128]{2,1,0:T(8,128)(2,1)} %get-tuple-element.21), calls=%async_computation.5 | async-start | bytes 524288 | tf_op jit(solution)/shard_map/all_to_all | solution.py:291
  80.2 0.2 grad_part.1
  80.3 10.4 %all-gather = bf16[1056,128]{1,0:T(8,128)(2,1)S(1)} all-gather(bf16[264,128]{1,0:T(8,128)(2,1)S(1)} %grad_part.1), channel_id=2, replica_groups=mesh['ylo'=2,'zq'=8,'z0'=2,'x'=4,'d0'=4] {'d0'}, dimensions={0}, use_global_device_ids=true | all-gather | bytes 337920 | tf_op jit(solution)/shard_map/all_gather | solution.py:294
  90.8 10.4 %all-gather.1 = f32[288,128]{1,0:T(8,128)S(1)} all-gather(f32[72,128]{1,0:T(8,128)S(1)} %grad_pick.1), channel_id=3, replica_groups=mesh['ylo'=2,'zq'=8,'z0'=2,'x'=4,'d0'=4] {'x'}, dimensions={0}, use_global_device_ids=true | all-gather | bytes 184320 | tf_op jit(solution)/shard_map/all_gather | solution.py:298
  101.2 0.6 grad_share.1
  101.8 0.0 all-to-all-done.5.rest_0_
  101.8 10.8 %all-to-all-start.3 = ((bf16[8,24,128]{2,1,0:T(8,128)(2,1)}), bf16[8,24,128]{2,1,0:T(8,128)(2,1)S(1)}, u32[]{:S(2)}, u32[]{:S(2)}) async-start(bf16[8,24,128]{2,1,0:T(8,128)(2,1)} %grad_share.1), calls=%async_computation.3 | async-start | bytes 98304 | tf_op jit(solution)/shard_map/all_to_all | solution.py:303
  112.6 2.3 %collective-permute-start.2 = (bf16[8,128,128]{2,1,0:T(8,128)(2,1)S(1)}, bf16[8,128,128]{2,1,0:T(8,128)(2,1)S(1)}, u32[]{:S(2)}, u32[]{:S(2)}) collective-permute-start(bf16[8,128,128]{2,1,0:T(8,128)(2,1)S(1)} %all-to-all-done.5.rest_0_), channel_id=1, source_target_pairs={{0,272},{16,256},{256,16},{272,0},{1,273},{17,257},{257,17},{273,1... | collective-permute-start | bytes 786440 | tf_op jit(solution)/shard_map/ppermute | solution.py:245
  114.9 2.8 %collective-permute-start.1 = (bf16[8,128,128]{2,1,0:T(8,128)(2,1)S(1)}, bf16[8,128,128]{2,1,0:T(8,128)(2,1)S(1)}, u32[]{:S(2)}, u32[]{:S(2)}) collective-permute-start(bf16[8,128,128]{2,1,0:T(8,128)(2,1)S(1)} %all-to-all-done.5.rest_0_), channel_id=1, source_target_pairs={{0,256},{16,272},{256,0},{272,16},{1,257},{17,273},{257,1},{273,17... | collective-permute-start | bytes 786440 | tf_op jit(solution)/shard_map/ppermute | solution.py:245
  117.7 3.2 %collective-permute-start = (bf16[8,128,128]{2,1,0:T(8,128)(2,1)S(1)}, bf16[8,128,128]{2,1,0:T(8,128)(2,1)S(1)}, u32[]{:S(2)}, u32[]{:S(2)}) collective-permute-start(bf16[8,128,128]{2,1,0:T(8,128)(2,1)S(1)} %all-to-all-done.5.rest_0_), channel_id=1, source_target_pairs={{0,16},{16,0},{256,272},{272,256},{1,17},{17,1},{257,273},{273,257... | collective-permute-start | bytes 786440 | tf_op jit(solution)/shard_map/ppermute | solution.py:245
  120.9 3.8 %all-to-all-done.3.recv_ref = bf16[8,24,128]{2,1,0:T(8,128)(2,1)S(1)} async-done(((bf16[8,24,128]{2,1,0:T(8,128)(2,1)}), bf16[8,24,128]{2,1,0:T(8,128)(2,1)S(1)}, u32[]{:S(2)}, u32[]{:S(2)}) %all-to-all-start.3) | async-done | bytes 49184 | tf_op jit(solution)/shard_map/all_to_all | solution.py:303
  124.7 0.6 grad_reshare.1
  125.3 3.3 %all-to-all-start.4 = ((bf16[4,40,128]{2,1,0:T(8,128)(2,1)}), bf16[4,40,128]{2,1,0:T(8,128)(2,1)S(1)}, u32[]{:S(2)}, u32[]{:S(2)}) async-start(bf16[4,40,128]{2,1,0:T(8,128)(2,1)} %grad_reshare.1), calls=%async_computation.4 | async-start | bytes 81920 | tf_op jit(solution)/shard_map/all_to_all | solution.py:306
  128.6 0.0 collective-permute-done.2.rest_3_
  128.6 0.0 collective-permute-done.1.rest_2_
  128.7 0.0 collective-permute-done.rest_1_
  128.7 3.8 %backward_tiles.1.refs_1_ = bf16[16,128,128]{2,1,0:T(8,128)(2,1)S(1)} custom-call(s32[128]{0:T(128)S(1)} %bitcast.24, s32[1]{0:T(128)} %bitcast.13.own_ref, bf16[128,128,128]{2,1,0:T(8,128)(2,1)} %build_back.1.tile_hbm, bf16[8,128,128]{2,1,0:T(8,128)(2,1)S(1)} %all-to-all-done.5.rest_0_, bf16[8,128,128]{2,1,0:T(8,128)(2,1)S(1)} %collective-permute-done.rest_1_, ...), custom_call_target="tpu_custom_call" | custom-call | tf_op jit(solution)/shard_map/backward_tiles/pallas_call | solution.py:233
  132.5 0.0 all-to-all-done.4.refs_0_
  132.5 0.6 grad_chunk.1
  133.1 22.9 %all_to_all.36.refs_0_ = bf16[16,144,128]{2,1,0:T(8,128)(2,1)S(1)} all-to-all(bf16[16,144,128]{2,1,0:T(8,128)(2,1)S(1)} %get-tuple-element.22), channel_id=1, replica_groups=mesh['ylo'=2,'zq'=8,'z0'=2,'x'=4,'d0'=4] {'x','d0'}, dimensions={0} | all-to-all | bytes 1179648 | tf_op jit(solution)/shard_map/all_to_all | solution.py:320
  156.0 0.7 final_sums.1
  (8 shorter events, 0.1 us)
Async XLA Ops:
  0.6 0.8 copy-start.6
  1.4 22.3 %copy-start.9 = (s32[1,1,128]{2,1,0:T(1,128)S(1)}, s32[1,1,128]{2,1,0:T(1,128)}, u32[]{:S(2)}) copy-start(s32[1,1,128]{2,1,0:T(1,128)} %param.11) | copy-start | bytes 1540
  2.3 21.4 %all-to-all-start = ((bf16[16,128,128]{2,1,0:T(8,128)(2,1)}), bf16[16,128,128]{2,1,0:T(8,128)(2,1)S(1)}, u32[]{:S(2)}, u32[]{:S(2)}) async-start(bf16[16,128,128]{2,1,0:T(8,128)(2,1)} %feature_copies.1), calls=%async_computation | async-start | bytes 1048576 | tf_op jit(solution)/shard_map/all_to_all | solution.py:270
  12.5 0.8 copy-start
  13.3 0.7 copy-start.2
  14.0 0.7 copy-start.7
  23.7 32.6 %copy-start.1 = (s32[1,1,128,64]{2,3,1,0:T(8,128)S(1)}, s32[1,1,128,64]{2,3,1,0:T(8,128)}, u32[]{:S(2)}) copy-start(s32[1,1,128,64]{2,3,1,0:T(8,128)} %param.13) | copy-start | bytes 98308
  23.7 32.6 %copy-start.3 = (bf16[1,1,128,64]{2,3,1,0:T(8,128)(2,1)S(1)}, bf16[1,1,128,64]{2,3,1,0:T(8,128)(2,1)}, u32[]{:S(2)}) copy-start(bf16[1,1,128,64]{2,3,1,0:T(8,128)(2,1)} %param.14) | copy-start | bytes 49156
  23.7 32.7 %copy-start.8 = (s32[1,1,128]{2,1,0:T(1,128)S(1)}, s32[1,1,128]{2,1,0:T(1,128)}, u32[]{:S(2)}) copy-start(s32[1,1,128]{2,1,0:T(1,128)} %param.12) | copy-start | bytes 1540
  27.6 45.6 %copy-start.4 = (bf16[128,256]{1,0:T(8,128)(2,1)S(1)}, bf16[128,256]{1,0:T(8,128)(2,1)}, u32[]{:S(2)}) copy-start(bf16[128,256]{1,0:T(8,128)(2,1)} %weight_ref.1) | copy-start | bytes 196612
  27.6 45.6 %copy-start.5 = (bf16[128,256]{1,0:T(8,128)(2,1)S(1)}, bf16[128,256]{1,0:T(8,128)(2,1)}, u32[]{:S(2)}) copy-start(bf16[128,256]{1,0:T(8,128)(2,1)} %grad_ref.1) | copy-start | bytes 196612
  27.6 45.6 %copy-start.10 = (f32[256]{0:T(256)S(1)}, f32[256]{0:T(256)}, u32[]{:S(2)}) copy-start(f32[256]{0:T(256)} %param.10) | copy-start | bytes 3076
  43.4 29.7 %all-to-all-start.2 = ((bf16[8,128,128]{2,1,0:T(8,128)(2,1)}), bf16[8,128,128]{2,1,0:T(8,128)(2,1)S(1)}, u32[]{:S(2)}, u32[]{:S(2)}) async-start(bf16[8,128,128]{2,1,0:T(8,128)(2,1)} %reduce_sum.24), calls=%async_computation.2 | async-start | bytes 524288 | tf_op jit(solution)/shard_map/all_to_all | solution.py:281
  74.2 27.6 %all-to-all-start.5 = ((bf16[8,128,128]{2,1,0:T(8,128)(2,1)}), bf16[8,128,128]{2,1,0:T(8,128)(2,1)S(1)}, u32[]{:S(2)}, u32[]{:S(2)}) async-start(bf16[8,128,128]{2,1,0:T(8,128)(2,1)} %get-tuple-element.21), calls=%async_computation.5 | async-start | bytes 524288 | tf_op jit(solution)/shard_map/all_to_all | solution.py:291
  101.8 22.9 %all-to-all-start.3 = ((bf16[8,24,128]{2,1,0:T(8,128)(2,1)}), bf16[8,24,128]{2,1,0:T(8,128)(2,1)S(1)}, u32[]{:S(2)}, u32[]{:S(2)}) async-start(bf16[8,24,128]{2,1,0:T(8,128)(2,1)} %grad_share.1), calls=%async_computation.3 | async-start | bytes 98304 | tf_op jit(solution)/shard_map/all_to_all | solution.py:303
  112.6 16.1 %collective-permute-start.2 = (bf16[8,128,128]{2,1,0:T(8,128)(2,1)S(1)}, bf16[8,128,128]{2,1,0:T(8,128)(2,1)S(1)}, u32[]{:S(2)}, u32[]{:S(2)}) collective-permute-start(bf16[8,128,128]{2,1,0:T(8,128)(2,1)S(1)} %all-to-all-done.5.rest_0_), channel_id=1, source_target_pairs={{0,272},{16,256},{256,16},{272,0},{1,273},{17,257},{257,17},{273,1... | collective-permute-start | bytes 786440 | tf_op jit(solution)/shard_map/ppermute | solution.py:245
  114.9 13.8 %collective-permute-start.1 = (bf16[8,128,128]{2,1,0:T(8,128)(2,1)S(1)}, bf16[8,128,128]{2,1,0:T(8,128)(2,1)S(1)}, u32[]{:S(2)}, u32[]{:S(2)}) collective-permute-start(bf16[8,128,128]{2,1,0:T(8,128)(2,1)S(1)} %all-to-all-done.5.rest_0_), channel_id=1, source_target_pairs={{0,256},{16,272},{256,0},{272,16},{1,257},{17,273},{257,1},{273,17... | collective-permute-start | bytes 786440 | tf_op jit(solution)/shard_map/ppermute | solution.py:245
  117.7 10.9 %collective-permute-start = (bf16[8,128,128]{2,1,0:T(8,128)(2,1)S(1)}, bf16[8,128,128]{2,1,0:T(8,128)(2,1)S(1)}, u32[]{:S(2)}, u32[]{:S(2)}) collective-permute-start(bf16[8,128,128]{2,1,0:T(8,128)(2,1)S(1)} %all-to-all-done.5.rest_0_), channel_id=1, source_target_pairs={{0,16},{16,0},{256,272},{272,256},{1,17},{17,1},{257,273},{273,257... | collective-permute-start | bytes 786440 | tf_op jit(solution)/shard_map/ppermute | solution.py:245
  125.3 7.1 %all-to-all-start.4 = ((bf16[4,40,128]{2,1,0:T(8,128)(2,1)}), bf16[4,40,128]{2,1,0:T(8,128)(2,1)S(1)}, u32[]{:S(2)}, u32[]{:S(2)}) async-start(bf16[4,40,128]{2,1,0:T(8,128)(2,1)} %grad_reshare.1), calls=%async_computation.4 | async-start | bytes 81920 | tf_op jit(solution)/shard_map/all_to_all | solution.py:306

commit v10 on v9

--- a/solution.py
+++ b/solution.py
@@ -14,7 +14,7 @@
 NT = (((1,), (1,)), ((), ()))
 TN = (((0,), (0,)), ((), ()))
 SRC = ("ylo", "zq", "z0")
-DST = ("x", "d0")
+DST = ("x1", "x0", "d0")
 NEAR = ("ylo", "z0")
 FAR = "zq"
 GROUP = 32
@@ -172,7 +172,10 @@
     out_ref[:, TILE:, :] = jnp.broadcast_to(chunk[None], (out_ref.shape[0], size, TILE))
 
 
-def copies_kernel(rows_ref, out_ref):
+def copies_kernel(rows_hbm, out_ref, rows_ref, sem):
+    copy = pltpu.make_async_copy(rows_hbm, rows_ref, sem)
+    copy.start()
+    copy.wait()
     out_ref[...] = jnp.broadcast_to(rows_ref[...][None], out_ref.shape)
 
 
@@ -266,7 +269,15 @@
             tile_shape, (counts,), (positions, weights), pair_scratch,
         )
 
-    sent = call(copies_kernel, "feature_copies", shape((dst,) + features.shape, BF16), (), (features,))
+    sent = pl.pallas_call(
+        copies_kernel,
+        out_shape=shape((dst,) + features.shape, BF16),
+        in_specs=[pl.BlockSpec(memory_space=pltpu.HBM)],
+        out_specs=vmem(1)[0],
+        scratch_shapes=[pltpu.VMEM(features.shape, BF16), pltpu.SemaphoreType.DMA(())],
+        compiler_params=pltpu.CompilerParams(vmem_limit_bytes=20 << 20),
+        name="feature_copies",
+    )(pltpu.with_memory_space_constraint(features, pltpu.HBM))
     source_rows = lax.all_to_all(sent, DST, 0, 0, tiled=True)
     tiles = build(positions, False)
     tile_scratch = [pltpu.VMEM((slots, TILE, TILE), BF16), pltpu.SemaphoreType.DMA((CHUNKS,))]
@@ -295,10 +306,14 @@
     part = call(
         pick_kernel, "grad_pick", shape((2 * TILE // group + 8, TILE), F32), (lax.axis_index("d0").reshape(1),), (part,)
     )
-    part = lax.all_gather(part, "x")
+    part = lax.all_gather(part, "x1")
+    part = call(
+        pick_kernel, "grad_half", shape((TILE // group + 8, TILE), F32), (lax.axis_index("x1").reshape(1),), (part,)
+    )
+    part = lax.all_gather(part, "x0")
     size = 2 * TILE // dst
     share = call(
-        share_kernel, "grad_share", shape((far, size + 8, TILE), BF16), (lax.axis_index("x").reshape(1),), (part,)
+        share_kernel, "grad_share", shape((far, size + 8, TILE), BF16), (lax.axis_index("x0").reshape(1),), (part,)
     )
     shared = lax.all_to_all(share, FAR, 0, 0, tiled=True)
     near_all = [far_rows] + [swap(far_rows, k, NEAR) for k in range(1, near)]
@@ -330,7 +345,7 @@
 
 def solution(mesh):
     src, dst = mesh.devices.shape
-    fine = Mesh(mesh.devices.reshape(2, src // 4, 2, dst // 4, 4), SRC + DST)
+    fine = Mesh(mesh.devices.reshape(2, src // 4, 2, 2, dst // 8, 4), SRC + DST)
     rows = P(SRC + DST, None)
     placed = (
         rows,

time: 158 us -> 156 us (0.987)
  blocking collectives: 58.5 us -> 56.8 us
    pallas_call x0 -> x1, Pallas kernels: none -> 1.67 us  [body(): pl.pallas_call(copies_kernel, out_shape=shape((dst,) + features.shape, BF...]
    all_gather x1 -> x2, blocking collectives: 10.4 us -> 8.88 us  [the longest x1 5.28 us: body(): part = lax.all_gather(part, 'x1')]
where the time goes in v10:
time: 156 us; the launch traced here: 155 us
  blocking collectives  56.8 us (36%)
  starting transfers between devices  51.9 us (33%)
  Pallas kernels  26.2 us (17%)
  waiting for transfers between devices  16.5 us (11%)
  local copies, waits for them, and re-layouts  2.16 us (1%)
    all_to_all x1, blocking collectives, body(): received = lax.all_to_all(back_send, DST, 0, 0, tiled=True)  22.7 us
    pallas_call x10, Pallas kernels, call(): pl.pallas_call(kernel, out_shape=outs, in_specs=smem(len(scalars)) + vmem...  16.9 us
    all_to_all x1, blocking collectives, body(): near_parts = lax.all_to_all(partial, NEAR, 0, 0, tiled=True)  14.8 us
    all_to_all x1, starting transfers between devices, body(): parts = lax.all_to_all(near_sums, FAR, 0, 0, tiled=True)  13 us
    all_to_all x1, starting transfers between devices, body(): shared = lax.all_to_all(share, FAR, 0, 0, tiled=True)  11.1 us
    all_gather x1, blocking collectives, body(): part = lax.all_gather(part, 'd0')  10.4 us
    all_to_all x1, starting transfers between devices, body(): source_rows = lax.all_to_all(sent, DST, 0, 0, tiled=True)  10.2 us
    all_to_all x1, waiting for transfers between devices, body(): parts = lax.all_to_all(near_sums, FAR, 0, 0, tiled=True)  10.2 us
  transfers between devices with their start and end apart: 8, of which 3 were waited for; matrix products, arithmetic and copies ran while one was open for 0% of the time, Pallas kernels for 12%

profile of v10, /device:TPU:1, one launch (start us, length us, event | category | flops | bytes accessed | tf_op | source)
XLA Modules:
  0.0 155.3 jit_solution(11046801075482643376)
XLA Ops:
  0.6 0.0 copy-start.8
  0.6 1.7 %feature_copies.1 = bf16[16,128,128]{2,1,0:T(8,128)(2,1)} custom-call(bf16[128,128]{1,0:T(8,128)(2,1)} %rows_hbm.1), custom_call_target="tpu_custom_call" | custom-call | tf_op jit(solution)/shard_map/feature_copies/pallas_call | solution.py:272
  2.3 10.2 %all-to-all-start = ((bf16[16,128,128]{2,1,0:T(8,128)(2,1)}), bf16[16,128,128]{2,1,0:T(8,128)(2,1)S(1)}, u32[]{:S(2)}, u32[]{:S(2)}) async-start(bf16[16,128,128]{2,1,0:T(8,128)(2,1)} %feature_copies.1), calls=%async_computation | async-start | bytes 1048576 | tf_op jit(solution)/shard_map/all_to_all | solution.py:281
  12.6 0.0 copy-start
  12.6 0.8 copy-done
  13.3 0.7 copy-done.2
  14.1 0.7 copy-done.6
  14.7 6.5 %build_tiles.1.tile_hbm = bf16[128,128,128]{2,1,0:T(8,128)(2,1)} custom-call(s32[128]{0:T(128)S(1)} %bitcast.24, s32[64,128]{1,0:T(8,128)S(1)} %bitcast.20, bf16[64,128]{1,0:T(8,128)(2,1)S(1)} %bitcast.22), custom_call_target="tpu_custom_call" | custom-call | tf_op jit(solution)/shard_map/build_tiles/pallas_call | solution.py:219
  21.2 2.6 %all-to-all-done.rows_ref = bf16[16,128,128]{2,1,0:T(8,128)(2,1)S(1)} async-done(((bf16[16,128,128]{2,1,0:T(8,128)(2,1)}), bf16[16,128,128]{2,1,0:T(8,128)(2,1)S(1)}, u32[]{:S(2)}, u32[]{:S(2)}) %all-to-all-start) | async-done | bytes 524320 | tf_op jit(solution)/shard_map/all_to_all | solution.py:281
  23.8 0.0 copy-done.8
  23.8 3.8 %forward_tiles.1 = bf16[4,8,128,128]{3,2,1,0:T(8,128)(2,1)S(1)} custom-call(s32[128]{0:T(128)S(1)} %bitcast.26, bf16[128,128,128]{2,1,0:T(8,128)(2,1)} %build_tiles.1.tile_hbm, bf16[16,128,128]{2,1,0:T(8,128)(2,1)S(1)} %all-to-all-done.rows_ref), custom_call_target="tpu_custom_call" | custom-call | tf_op jit(solution)/shard_map/forward_tiles/pallas_call | solution.py:236
  27.6 0.0 copy-start.4
  27.6 0.0 copy-start.5
  27.6 0.0 copy-start.9
  27.7 14.8 %all_to_all.35 = bf16[4,8,128,128]{3,2,1,0:T(8,128)(2,1)S(1)} all-to-all(bf16[4,8,128,128]{3,2,1,0:T(8,128)(2,1)S(1)} %forward_tiles.1), channel_id=1, replica_groups=mesh['ylo'=2,'zq'=8,'z0'=2,'x1'=2,'x0'=2,'d0'=4] {'ylo','z0'}, dimensions={0} | all-to-all | bytes 2097152 | tf_op jit(solution)/shard_map/all_to_all | solution.py:288
  42.5 0.9 reduce_sum.24
  43.4 13.0 %all-to-all-start.2 = ((bf16[8,128,128]{2,1,0:T(8,128)(2,1)}), bf16[8,128,128]{2,1,0:T(8,128)(2,1)S(1)}, u32[]{:S(2)}, u32[]{:S(2)}) async-start(bf16[8,128,128]{2,1,0:T(8,128)(2,1)} %reduce_sum.24), calls=%async_computation.2 | async-start | bytes 524288 | tf_op jit(solution)/shard_map/all_to_all | solution.py:292
  56.4 0.0 copy-done.1
  56.4 0.0 copy-done.3
  56.4 0.0 copy-done.7
  56.4 6.5 %build_back.1.tile_hbm = bf16[128,128,128]{2,1,0:T(8,128)(2,1)} custom-call(s32[128]{0:T(128)S(1)} %bitcast.25, s32[64,128]{1,0:T(8,128)S(1)} %bitcast.21, bf16[64,128]{1,0:T(8,128)(2,1)S(1)} %bitcast.23), custom_call_target="tpu_custom_call" | custom-call | tf_op jit(solution)/shard_map/build_back/pallas_call | solution.py:219
  63.0 10.2 %all-to-all-done.2 = bf16[8,128,128]{2,1,0:T(8,128)(2,1)S(1)} async-done(((bf16[8,128,128]{2,1,0:T(8,128)(2,1)}), bf16[8,128,128]{2,1,0:T(8,128)(2,1)S(1)}, u32[]{:S(2)}, u32[]{:S(2)}) %all-to-all-start.2) | async-done | bytes 262176 | tf_op jit(solution)/shard_map/all_to_all | solution.py:292
  73.2 0.0 copy-done.4
  73.2 0.0 copy-done.5
  73.2 0.0 copy-done.9
  73.2 1.1 dense_layer.1
  74.3 5.9 %all-to-all-start.5 = ((bf16[8,128,128]{2,1,0:T(8,128)(2,1)}), bf16[8,128,128]{2,1,0:T(8,128)(2,1)S(1)}, u32[]{:S(2)}, u32[]{:S(2)}) async-start(bf16[8,128,128]{2,1,0:T(8,128)(2,1)} %get-tuple-element.21), calls=%async_computation.5 | async-start | bytes 524288 | tf_op jit(solution)/shard_map/all_to_all | solution.py:302
  80.2 0.2 grad_part.1
  80.4 10.4 %all-gather = bf16[1056,128]{1,0:T(8,128)(2,1)S(1)} all-gather(bf16[264,128]{1,0:T(8,128)(2,1)S(1)} %grad_part.1), channel_id=2, replica_groups=mesh['ylo'=2,'zq'=8,'z0'=2,'x1'=2,'x0'=2,'d0'=4] {'d0'}, dimensions={0}, use_global_device_ids=true | all-gather | bytes 337920 | tf_op jit(solution)/shard_map/all_gather | solution.py:305
  90.8 5.3 %all-gather.1 = f32[144,128]{1,0:T(8,128)S(1)} all-gather(f32[72,128]{1,0:T(8,128)S(1)} %grad_pick.1), channel_id=3, replica_groups=mesh['ylo'=2,'zq'=8,'z0'=2,'x1'=2,'x0'=2,'d0'=4] {'x1'}, dimensions={0}, use_global_device_ids=true | all-gather | bytes 110592 | tf_op jit(solution)/shard_map/all_gather | solution.py:309
  96.1 3.6 %all-gather.2 = f32[80,128]{1,0:T(8,128)S(1)} all-gather(f32[40,128]{1,0:T(8,128)S(1)} %grad_half.1), channel_id=4, replica_groups=mesh['ylo'=2,'zq'=8,'z0'=2,'x1'=2,'x0'=2,'d0'=4] {'x0'}, dimensions={0}, use_global_device_ids=true | all-gather | bytes 61440 | tf_op jit(solution)/shard_map/all_gather | solution.py:313
  99.7 0.6 grad_share.1
  100.3 0.0 all-to-all-done.5.rest_0_
  100.3 11.1 %all-to-all-start.3 = ((bf16[8,24,128]{2,1,0:T(8,128)(2,1)}), bf16[8,24,128]{2,1,0:T(8,128)(2,1)S(1)}, u32[]{:S(2)}, u32[]{:S(2)}) async-start(bf16[8,24,128]{2,1,0:T(8,128)(2,1)} %grad_share.1), calls=%async_computation.3 | async-start | bytes 98304 | tf_op jit(solution)/shard_map/all_to_all | solution.py:318
  111.5 2.3 %collective-permute-start.2 = (bf16[8,128,128]{2,1,0:T(8,128)(2,1)S(1)}, bf16[8,128,128]{2,1,0:T(8,128)(2,1)S(1)}, u32[]{:S(2)}, u32[]{:S(2)}) collective-permute-start(bf16[8,128,128]{2,1,0:T(8,128)(2,1)S(1)} %all-to-all-done.5.rest_0_), channel_id=1, source_target_pairs={{0,272},{16,256},{256,16},{272,0},{1,273},{17,257},{257,17},{273,1... | collective-permute-start | bytes 786440 | tf_op jit(solution)/shard_map/ppermute | solution.py:248
  113.8 2.9 %collective-permute-start.1 = (bf16[8,128,128]{2,1,0:T(8,128)(2,1)S(1)}, bf16[8,128,128]{2,1,0:T(8,128)(2,1)S(1)}, u32[]{:S(2)}, u32[]{:S(2)}) collective-permute-start(bf16[8,128,128]{2,1,0:T(8,128)(2,1)S(1)} %all-to-all-done.5.rest_0_), channel_id=1, source_target_pairs={{0,256},{16,272},{256,0},{272,16},{1,257},{17,273},{257,1},{273,17... | collective-permute-start | bytes 786440 | tf_op jit(solution)/shard_map/ppermute | solution.py:248
  116.6 3.2 %collective-permute-start = (bf16[8,128,128]{2,1,0:T(8,128)(2,1)S(1)}, bf16[8,128,128]{2,1,0:T(8,128)(2,1)S(1)}, u32[]{:S(2)}, u32[]{:S(2)}) collective-permute-start(bf16[8,128,128]{2,1,0:T(8,128)(2,1)S(1)} %all-to-all-done.5.rest_0_), channel_id=1, source_target_pairs={{0,16},{16,0},{256,272},{272,256},{1,17},{17,1},{257,273},{273,257... | collective-permute-start | bytes 786440 | tf_op jit(solution)/shard_map/ppermute | solution.py:248
  119.9 3.7 %all-to-all-done.3.recv_ref = bf16[8,24,128]{2,1,0:T(8,128)(2,1)S(1)} async-done(((bf16[8,24,128]{2,1,0:T(8,128)(2,1)}), bf16[8,24,128]{2,1,0:T(8,128)(2,1)S(1)}, u32[]{:S(2)}, u32[]{:S(2)}) %all-to-all-start.3) | async-done | bytes 49184 | tf_op jit(solution)/shard_map/all_to_all | solution.py:318
  123.5 0.6 grad_reshare.1
  124.2 3.3 %all-to-all-start.4 = ((bf16[4,40,128]{2,1,0:T(8,128)(2,1)}), bf16[4,40,128]{2,1,0:T(8,128)(2,1)S(1)}, u32[]{:S(2)}, u32[]{:S(2)}) async-start(bf16[4,40,128]{2,1,0:T(8,128)(2,1)} %grad_reshare.1), calls=%async_computation.4 | async-start | bytes 81920 | tf_op jit(solution)/shard_map/all_to_all | solution.py:321
  127.4 0.0 collective-permute-done.2.rest_3_
  127.5 0.0 collective-permute-done.1.rest_2_
  127.5 0.0 collective-permute-done.rest_1_
  127.5 3.8 %backward_tiles.1.refs_1_ = bf16[16,128,128]{2,1,0:T(8,128)(2,1)S(1)} custom-call(s32[128]{0:T(128)S(1)} %bitcast.27, s32[1]{0:T(128)} %bitcast.15.own_ref, bf16[128,128,128]{2,1,0:T(8,128)(2,1)} %build_back.1.tile_hbm, bf16[8,128,128]{2,1,0:T(8,128)(2,1)S(1)} %all-to-all-done.5.rest_0_, bf16[8,128,128]{2,1,0:T(8,128)(2,1)S(1)} %collective-permute-done.rest_1_, ...), custom_call_target="tpu_custom_call" | custom-call | tf_op jit(solution)/shard_map/backward_tiles/pallas_call | solution.py:236
  131.3 0.0 all-to-all-done.4.refs_0_
  131.3 0.6 grad_chunk.1
  131.9 22.7 %all_to_all.36.refs_0_ = bf16[16,144,128]{2,1,0:T(8,128)(2,1)S(1)} all-to-all(bf16[16,144,128]{2,1,0:T(8,128)(2,1)S(1)} %get-tuple-element.22), channel_id=1, replica_groups=mesh['ylo'=2,'zq'=8,'z0'=2,'x1'=2,'x0'=2,'d0'=4] {'x1','x0','d0'}, dimensions={0} | all-to-all | bytes 1179648 | tf_op jit(solution)/shard_map/all_to_all | solution.py:335
  154.6 0.7 final_sums.1
  (8 shorter events, 0.1 us)
Async XLA Ops:
  0.6 23.1 %copy-start.8 = (s32[1,1,128]{2,1,0:T(1,128)S(1)}, s32[1,1,128]{2,1,0:T(1,128)}, u32[]{:S(2)}) copy-start(s32[1,1,128]{2,1,0:T(1,128)} %param.11) | copy-start | bytes 1540
  2.3 21.4 %all-to-all-start = ((bf16[16,128,128]{2,1,0:T(8,128)(2,1)}), bf16[16,128,128]{2,1,0:T(8,128)(2,1)S(1)}, u32[]{:S(2)}, u32[]{:S(2)}) async-start(bf16[16,128,128]{2,1,0:T(8,128)(2,1)} %feature_copies.1), calls=%async_computation | async-start | bytes 1048576 | tf_op jit(solution)/shard_map/all_to_all | solution.py:281
  12.6 0.8 copy-start
  13.3 0.7 copy-start.2
  14.0 0.7 copy-start.6
  23.8 32.6 %copy-start.1 = (s32[1,1,128,64]{2,3,1,0:T(8,128)S(1)}, s32[1,1,128,64]{2,3,1,0:T(8,128)}, u32[]{:S(2)}) copy-start(s32[1,1,128,64]{2,3,1,0:T(8,128)} %param.13) | copy-start | bytes 98308
  23.8 32.7 %copy-start.3 = (bf16[1,1,128,64]{2,3,1,0:T(8,128)(2,1)S(1)}, bf16[1,1,128,64]{2,3,1,0:T(8,128)(2,1)}, u32[]{:S(2)}) copy-start(bf16[1,1,128,64]{2,3,1,0:T(8,128)(2,1)} %param.14) | copy-start | bytes 49156
  23.8 32.7 %copy-start.7 = (s32[1,1,128]{2,1,0:T(1,128)S(1)}, s32[1,1,128]{2,1,0:T(1,128)}, u32[]{:S(2)}) copy-start(s32[1,1,128]{2,1,0:T(1,128)} %param.12) | copy-start | bytes 1540
  27.6 45.6 %copy-start.4 = (bf16[128,256]{1,0:T(8,128)(2,1)S(1)}, bf16[128,256]{1,0:T(8,128)(2,1)}, u32[]{:S(2)}) copy-start(bf16[128,256]{1,0:T(8,128)(2,1)} %weight_ref.1) | copy-start | bytes 196612
  27.6 45.6 %copy-start.5 = (bf16[128,256]{1,0:T(8,128)(2,1)S(1)}, bf16[128,256]{1,0:T(8,128)(2,1)}, u32[]{:S(2)}) copy-start(bf16[128,256]{1,0:T(8,128)(2,1)} %grad_ref.1) | copy-start | bytes 196612
  27.6 45.6 %copy-start.9 = (f32[256]{0:T(256)S(1)}, f32[256]{0:T(256)}, u32[]{:S(2)}) copy-start(f32[256]{0:T(256)} %param.10) | copy-start | bytes 3076
  43.4 29.7 %all-to-all-start.2 = ((bf16[8,128,128]{2,1,0:T(8,128)(2,1)}), bf16[8,128,128]{2,1,0:T(8,128)(2,1)S(1)}, u32[]{:S(2)}, u32[]{:S(2)}) async-start(bf16[8,128,128]{2,1,0:T(8,128)(2,1)} %reduce_sum.24), calls=%async_computation.2 | async-start | bytes 524288 | tf_op jit(solution)/shard_map/all_to_all | solution.py:292
  74.3 26.0 %all-to-all-start.5 = ((bf16[8,128,128]{2,1,0:T(8,128)(2,1)}), bf16[8,128,128]{2,1,0:T(8,128)(2,1)S(1)}, u32[]{:S(2)}, u32[]{:S(2)}) async-start(bf16[8,128,128]{2,1,0:T(8,128)(2,1)} %get-tuple-element.21), calls=%async_computation.5 | async-start | bytes 524288 | tf_op jit(solution)/shard_map/all_to_all | solution.py:302
  100.3 23.2 %all-to-all-start.3 = ((bf16[8,24,128]{2,1,0:T(8,128)(2,1)}), bf16[8,24,128]{2,1,0:T(8,128)(2,1)S(1)}, u32[]{:S(2)}, u32[]{:S(2)}) async-start(bf16[8,24,128]{2,1,0:T(8,128)(2,1)} %grad_share.1), calls=%async_computation.3 | async-start | bytes 98304 | tf_op jit(solution)/shard_map/all_to_all | solution.py:318
  111.5 16.0 %collective-permute-start.2 = (bf16[8,128,128]{2,1,0:T(8,128)(2,1)S(1)}, bf16[8,128,128]{2,1,0:T(8,128)(2,1)S(1)}, u32[]{:S(2)}, u32[]{:S(2)}) collective-permute-start(bf16[8,128,128]{2,1,0:T(8,128)(2,1)S(1)} %all-to-all-done.5.rest_0_), channel_id=1, source_target_pairs={{0,272},{16,256},{256,16},{272,0},{1,273},{17,257},{257,17},{273,1... | collective-permute-start | bytes 786440 | tf_op jit(solution)/shard_map/ppermute | solution.py:248
  113.8 13.7 %collective-permute-start.1 = (bf16[8,128,128]{2,1,0:T(8,128)(2,1)S(1)}, bf16[8,128,128]{2,1,0:T(8,128)(2,1)S(1)}, u32[]{:S(2)}, u32[]{:S(2)}) collective-permute-start(bf16[8,128,128]{2,1,0:T(8,128)(2,1)S(1)} %all-to-all-done.5.rest_0_), channel_id=1, source_target_pairs={{0,256},{16,272},{256,0},{272,16},{1,257},{17,273},{257,1},{273,17... | collective-permute-start | bytes 786440 | tf_op jit(solution)/shard_map/ppermute | solution.py:248
  116.6 10.8 %collective-permute-start = (bf16[8,128,128]{2,1,0:T(8,128)(2,1)S(1)}, bf16[8,128,128]{2,1,0:T(8,128)(2,1)S(1)}, u32[]{:S(2)}, u32[]{:S(2)}) collective-permute-start(bf16[8,128,128]{2,1,0:T(8,128)(2,1)S(1)} %all-to-all-done.5.rest_0_), channel_id=1, source_target_pairs={{0,16},{16,0},{256,272},{272,256},{1,17},{17,1},{257,273},{273,257... | collective-permute-start | bytes 786440 | tf_op jit(solution)/shard_map/ppermute | solution.py:248
  124.2 7.1 %all-to-all-start.4 = ((bf16[4,40,128]{2,1,0:T(8,128)(2,1)}), bf16[4,40,128]{2,1,0:T(8,128)(2,1)S(1)}, u32[]{:S(2)}, u32[]{:S(2)}) async-start(bf16[4,40,128]{2,1,0:T(8,128)(2,1)} %grad_reshare.1), calls=%async_computation.4 | async-start | bytes 81920 | tf_op jit(solution)/shard_map/all_to_all | solution.py:321

commit v11 on v10

--- a/solution.py
+++ b/solution.py
@@ -18,7 +18,6 @@
 NEAR = ("ylo", "z0")
 FAR = "zq"
 GROUP = 32
-CHUNKS = 4
 
 
 def dot(a, b, dims=NN):
@@ -58,21 +57,20 @@
     lax.fori_loop(0, pairs, one_pair, 0, unroll=4)
 
 
-def spread_tiles(index_ref, tile_hbm, rows_ref, sums, tile_ref, sems, split, backward, ready):
+def spread_tiles(index_ref, count_ref, tile_hbm, rows_ref, sums, tile_ref, sems, split, backward, ready):
     shift = split.bit_length() - 1
-    slots = tile_ref.shape[0]
-    chunk = slots // CHUNKS
+    starts = range(0, tile_ref.shape[0], GROUP)
     copies = []
-    for c in range(CHUNKS):
-        part = pl.ds(c * chunk, chunk)
-        copies.append(pltpu.make_async_copy(tile_hbm.at[part], tile_ref.at[part], sems.at[c]))
-    for copy in copies:
-        copy.start()
+    for start in starts:
+        part = pl.ds(start, GROUP)
+        copies.append(pltpu.make_async_copy(tile_hbm.at[part], tile_ref.at[part], sems.at[start // GROUP]))
+    for start in starts:
+        pl.when(count_ref[start] > 0)(copies[start // GROUP].start)
     sums[...] = jnp.zeros_like(sums)
     ready()
-    for start in range(0, slots, GROUP):
-        if start % chunk == 0:
-            copies[start // chunk].wait()
+
+    def one_group(start):
+        copies[start // GROUP].wait()
         found = []
         for slot in range(start, start + GROUP):
             index = index_ref[slot]
@@ -85,11 +83,14 @@
         for place, value in found:
             sums[place] = sums[place] + value
 
-
-def forward_kernel(index_ref, tile_hbm, rows_ref, out_ref, sums, tile_ref, sems):
+    for start in starts:
+        pl.when(count_ref[start] > 0)(lambda start=start: one_group(start))
+
+
+def forward_kernel(index_ref, count_ref, tile_hbm, rows_ref, out_ref, sums, tile_ref, sems):
     near, far = out_ref.shape[:2]
     split = rows_ref.shape[0]
-    spread_tiles(index_ref, tile_hbm, rows_ref, sums, tile_ref, sems, split, False, lambda: None)
+    spread_tiles(index_ref, count_ref, tile_hbm, rows_ref, sums, tile_ref, sems, split, False, lambda: None)
     for target in range(near * far):
         place = target // (2 * far) * 2 + target % 2
         out_ref[place, target // 2 % far] = sums[target].astype(BF16)
@@ -190,7 +191,7 @@
         weight_grad_ref[start % TILE : start % TILE + size, lane : lane + TILE] = chunk
 
 
-def backward_kernel(index_ref, own_ref, tile_hbm, *rest):
+def backward_kernel(index_ref, count_ref, own_ref, tile_hbm, *rest):
     near_refs, (out_ref, sums, tile_ref, sems, rows) = rest[:-5], rest[-5:]
     far = near_refs[0].shape[0]
     pieces = out_ref.shape[0]
@@ -202,7 +203,7 @@
             for q in range(far):
                 rows[base + 2 * q] = near_ref[q]
 
-    spread_tiles(index_ref, tile_hbm, rows, sums, tile_ref, sems, pieces, True, ready)
+    spread_tiles(index_ref, count_ref, tile_hbm, rows, sums, tile_ref, sems, pieces, True, ready)
     out_ref[...] = sums[...].astype(BF16)
 
 
@@ -280,10 +281,10 @@
     )(pltpu.with_memory_space_constraint(features, pltpu.HBM))
     source_rows = lax.all_to_all(sent, DST, 0, 0, tiled=True)
     tiles = build(positions, False)
-    tile_scratch = [pltpu.VMEM((slots, TILE, TILE), BF16), pltpu.SemaphoreType.DMA((CHUNKS,))]
+    tile_scratch = [pltpu.VMEM((slots, TILE, TILE), BF16), pltpu.SemaphoreType.DMA((slots // GROUP,))]
     partial = spread(
         forward_kernel, "forward_tiles", shape((near, far, TILE, TILE), BF16),
-        (index,), tiles, (source_rows,), [pltpu.VMEM((src, TILE, TILE), F32)] + tile_scratch,
+        (index, counts), tiles, (source_rows,), [pltpu.VMEM((src, TILE, TILE), F32)] + tile_scratch,
     )
     near_parts = lax.all_to_all(partial, NEAR, 0, 0, tiled=True)
     near_sums = jnp.sum(near_parts.astype(F32), axis=0).astype(BF16)
@@ -321,7 +322,7 @@
     shared = lax.all_to_all(share, NEAR, 0, 0, tiled=True)
     back_send = spread(
         backward_kernel, "backward_tiles", shape((dst, TILE, TILE), BF16),
-        (index, lax.axis_index(NEAR).reshape(1)), back_tiles, near_all,
+        (index, counts, lax.axis_index(NEAR).reshape(1)), back_tiles, near_all,
         [pltpu.VMEM((dst, TILE, TILE), F32)] + tile_scratch + [pltpu.VMEM((src, TILE, TILE), BF16)],
     )
     node_scale = 1.0 / math.sqrt(features.shape[0] * src * dst)

time: 156 us -> 156 us (level)
  Pallas kernels: 26.2 us -> 23.3 us
  blocking collectives: 56.8 us -> 58.7 us
  waiting for transfers between devices: 16.5 us -> 18.3 us
    pallas_call x2, Pallas kernels: 7.64 us -> 4.77 us  [spread(): pl.pallas_call(kernel, out_shape=out, in_specs=smem(len(scalars)) + [pl.B...]
  transfers between devices with their start and end apart: 8 -> 8, of which waited for: 3 -> 4; matrix products, arithmetic and copies ran while one was open for 0% -> 0% of each run, Pallas kernels for 12% -> 11%
where the time goes in v11:
time: 156 us
  blocking collectives  58.7 us (38%)
  starting transfers between devices  51.6 us (33%)
  Pallas kernels  23.3 us (15%)
  waiting for transfers between devices  18.3 us (12%)
  local copies, waits for them, and re-layouts  2.16 us (1%)
    all_to_all x1, blocking collectives, body(): received = lax.all_to_all(back_send, DST, 0, 0, tiled=True)  24.2 us
    pallas_call x10, Pallas kernels, call(): pl.pallas_call(kernel, out_shape=outs, in_specs=smem(len(scalars)) + vmem...  16.9 us
    all_to_all x1, blocking collectives, body(): near_parts = lax.all_to_all(partial, NEAR, 0, 0, tiled=True)  14.6 us
    all_to_all x1, starting transfers between devices, body(): parts = lax.all_to_all(near_sums, FAR, 0, 0, tiled=True)  14 us
    all_to_all x1, starting transfers between devices, body(): shared = lax.all_to_all(share, FAR, 0, 0, tiled=True)  11.1 us
    all_gather x1, blocking collectives, body(): part = lax.all_gather(part, 'd0')  11 us
    all_to_all x1, waiting for transfers between devices, body(): parts = lax.all_to_all(near_sums, FAR, 0, 0, tiled=True)  10.8 us
    all_to_all x1, starting transfers between devices, body(): source_rows = lax.all_to_all(sent, DST, 0, 0, tiled=True)  10.2 us
  transfers between devices with their start and end apart: 8, of which 4 were waited for; matrix products, arithmetic and copies ran while one was open for 0% of the time, Pallas kernels for 11%

profile of v11, /device:TPU:1, one launch (start us, length us, event | category | flops | bytes accessed | tf_op | source)
XLA Modules:
  0.0 155.9 jit_solution(6127108235161012746)
XLA Ops:
  0.6 0.0 copy-start.7
  0.6 0.0 copy-start.8
  0.7 1.7 %feature_copies.1 = bf16[16,128,128]{2,1,0:T(8,128)(2,1)} custom-call(bf16[128,128]{1,0:T(8,128)(2,1)} %rows_hbm.1), custom_call_target="tpu_custom_call" | custom-call | tf_op jit(solution)/shard_map/feature_copies/pallas_call | solution.py:273
  2.3 10.2 %all-to-all-start = ((bf16[16,128,128]{2,1,0:T(8,128)(2,1)}), bf16[16,128,128]{2,1,0:T(8,128)(2,1)S(1)}, u32[]{:S(2)}, u32[]{:S(2)}) async-start(bf16[16,128,128]{2,1,0:T(8,128)(2,1)} %feature_copies.1), calls=%async_computation | async-start | bytes 1048576 | tf_op jit(solution)/shard_map/all_to_all | solution.py:282
  12.6 0.8 copy-done
  13.4 0.7 copy-done.2
  14.1 0.7 copy-done.6
  14.7 6.5 %build_tiles.1.tile_hbm = bf16[128,128,128]{2,1,0:T(8,128)(2,1)} custom-call(s32[128]{0:T(128)S(1)} %bitcast.24, s32[64,128]{1,0:T(8,128)S(1)} %bitcast.20, bf16[64,128]{1,0:T(8,128)(2,1)S(1)} %bitcast.22), custom_call_target="tpu_custom_call" | custom-call | tf_op jit(solution)/shard_map/build_tiles/pallas_call | solution.py:220
  21.2 2.6 %all-to-all-done.rows_ref = bf16[16,128,128]{2,1,0:T(8,128)(2,1)S(1)} async-done(((bf16[16,128,128]{2,1,0:T(8,128)(2,1)}), bf16[16,128,128]{2,1,0:T(8,128)(2,1)S(1)}, u32[]{:S(2)}, u32[]{:S(2)}) %all-to-all-start) | async-done | bytes 524320 | tf_op jit(solution)/shard_map/all_to_all | solution.py:282
  23.8 0.0 copy-done.7
  23.8 0.0 copy-done.8
  23.8 2.4 %forward_tiles.1 = bf16[4,8,128,128]{3,2,1,0:T(8,128)(2,1)S(1)} custom-call(s32[128]{0:T(128)S(1)} %bitcast.28, s32[128]{0:T(128)S(1)} %bitcast.25, bf16[128,128,128]{2,1,0:T(8,128)(2,1)} %build_tiles.1.tile_hbm, bf16[16,128,128]{2,1,0:T(8,128)(2,1)S(1)} %all-to-all-done.rows_ref), custom_call_target="tpu_custom_call" | custom-call | tf_op jit(solution)/shard_map/forward_tiles/pallas_call | solution.py:237
  26.2 0.0 copy-start.4
  26.2 0.0 copy-start.5
  26.2 0.0 copy-start.9
  26.3 14.6 %all_to_all.35 = bf16[4,8,128,128]{3,2,1,0:T(8,128)(2,1)S(1)} all-to-all(bf16[4,8,128,128]{3,2,1,0:T(8,128)(2,1)S(1)} %forward_tiles.1), channel_id=1, replica_groups=mesh['ylo'=2,'zq'=8,'z0'=2,'x1'=2,'x0'=2,'d0'=4] {'ylo','z0'}, dimensions={0} | all-to-all | bytes 2097152 | tf_op jit(solution)/shard_map/all_to_all | solution.py:289
  40.8 0.9 reduce_sum.24
  41.8 14.0 %all-to-all-start.2 = ((bf16[8,128,128]{2,1,0:T(8,128)(2,1)}), bf16[8,128,128]{2,1,0:T(8,128)(2,1)S(1)}, u32[]{:S(2)}, u32[]{:S(2)}) async-start(bf16[8,128,128]{2,1,0:T(8,128)(2,1)} %reduce_sum.24), calls=%async_computation.2 | async-start | bytes 524288 | tf_op jit(solution)/shard_map/all_to_all | solution.py:293
  55.8 0.0 copy-done.1
  55.8 0.0 copy-done.3
  55.8 6.5 %build_back.1.tile_hbm = bf16[128,128,128]{2,1,0:T(8,128)(2,1)} custom-call(s32[128]{0:T(128)S(1)} %bitcast.26, s32[64,128]{1,0:T(8,128)S(1)} %bitcast.21, bf16[64,128]{1,0:T(8,128)(2,1)S(1)} %bitcast.23), custom_call_target="tpu_custom_call" | custom-call | tf_op jit(solution)/shard_map/build_back/pallas_call | solution.py:220
  62.4 10.8 %all-to-all-done.2 = bf16[8,128,128]{2,1,0:T(8,128)(2,1)S(1)} async-done(((bf16[8,128,128]{2,1,0:T(8,128)(2,1)}), bf16[8,128,128]{2,1,0:T(8,128)(2,1)S(1)}, u32[]{:S(2)}, u32[]{:S(2)}) %all-to-all-start.2) | async-done | bytes 262176 | tf_op jit(solution)/shard_map/all_to_all | solution.py:293
  73.2 0.0 copy-done.4
  73.2 0.0 copy-done.5
  73.3 0.0 copy-done.9
  73.3 1.1 dense_layer.1
  74.3 4.7 %all-to-all-start.5 = ((bf16[8,128,128]{2,1,0:T(8,128)(2,1)}), bf16[8,128,128]{2,1,0:T(8,128)(2,1)S(1)}, u32[]{:S(2)}, u32[]{:S(2)}) async-start(bf16[8,128,128]{2,1,0:T(8,128)(2,1)} %get-tuple-element.21), calls=%async_computation.5 | async-start | bytes 524288 | tf_op jit(solution)/shard_map/all_to_all | solution.py:303
  79.0 0.2 grad_part.1
  79.2 11.0 %all-gather = bf16[1056,128]{1,0:T(8,128)(2,1)S(1)} all-gather(bf16[264,128]{1,0:T(8,128)(2,1)S(1)} %grad_part.1), channel_id=2, replica_groups=mesh['ylo'=2,'zq'=8,'z0'=2,'x1'=2,'x0'=2,'d0'=4] {'d0'}, dimensions={0}, use_global_device_ids=true | all-gather | bytes 337920 | tf_op jit(solution)/shard_map/all_gather | solution.py:306
  90.2 5.3 %all-gather.1 = f32[144,128]{1,0:T(8,128)S(1)} all-gather(f32[72,128]{1,0:T(8,128)S(1)} %grad_pick.1), channel_id=3, replica_groups=mesh['ylo'=2,'zq'=8,'z0'=2,'x1'=2,'x0'=2,'d0'=4] {'x1'}, dimensions={0}, use_global_device_ids=true | all-gather | bytes 110592 | tf_op jit(solution)/shard_map/all_gather | solution.py:310
  95.5 3.6 %all-gather.2 = f32[80,128]{1,0:T(8,128)S(1)} all-gather(f32[40,128]{1,0:T(8,128)S(1)} %grad_half.1), channel_id=4, replica_groups=mesh['ylo'=2,'zq'=8,'z0'=2,'x1'=2,'x0'=2,'d0'=4] {'x0'}, dimensions={0}, use_global_device_ids=true | all-gather | bytes 61440 | tf_op jit(solution)/shard_map/all_gather | solution.py:314
  99.1 0.6 grad_share.1
  99.7 0.0 all-to-all-done.5.rest_0_
  99.7 11.1 %all-to-all-start.3 = ((bf16[8,24,128]{2,1,0:T(8,128)(2,1)}), bf16[8,24,128]{2,1,0:T(8,128)(2,1)S(1)}, u32[]{:S(2)}, u32[]{:S(2)}) async-start(bf16[8,24,128]{2,1,0:T(8,128)(2,1)} %grad_share.1), calls=%async_computation.3 | async-start | bytes 98304 | tf_op jit(solution)/shard_map/all_to_all | solution.py:319
  110.8 2.8 %collective-permute-start.2 = (bf16[8,128,128]{2,1,0:T(8,128)(2,1)S(1)}, bf16[8,128,128]{2,1,0:T(8,128)(2,1)S(1)}, u32[]{:S(2)}, u32[]{:S(2)}) collective-permute-start(bf16[8,128,128]{2,1,0:T(8,128)(2,1)S(1)} %all-to-all-done.5.rest_0_), channel_id=1, source_target_pairs={{0,272},{16,256},{256,16},{272,0},{1,273},{17,257},{257,17},{273,1... | collective-permute-start | bytes 786440 | tf_op jit(solution)/shard_map/ppermute | solution.py:249
  113.6 2.4 %collective-permute-start.1 = (bf16[8,128,128]{2,1,0:T(8,128)(2,1)S(1)}, bf16[8,128,128]{2,1,0:T(8,128)(2,1)S(1)}, u32[]{:S(2)}, u32[]{:S(2)}) collective-permute-start(bf16[8,128,128]{2,1,0:T(8,128)(2,1)S(1)} %all-to-all-done.5.rest_0_), channel_id=1, source_target_pairs={{0,256},{16,272},{256,0},{272,16},{1,257},{17,273},{257,1},{273,17... | collective-permute-start | bytes 786440 | tf_op jit(solution)/shard_map/ppermute | solution.py:249
  116.0 3.2 %collective-permute-start = (bf16[8,128,128]{2,1,0:T(8,128)(2,1)S(1)}, bf16[8,128,128]{2,1,0:T(8,128)(2,1)S(1)}, u32[]{:S(2)}, u32[]{:S(2)}) collective-permute-start(bf16[8,128,128]{2,1,0:T(8,128)(2,1)S(1)} %all-to-all-done.5.rest_0_), channel_id=1, source_target_pairs={{0,16},{16,0},{256,272},{272,256},{1,17},{17,1},{257,273},{273,257... | collective-permute-start | bytes 786440 | tf_op jit(solution)/shard_map/ppermute | solution.py:249
  119.2 3.7 %all-to-all-done.3.recv_ref = bf16[8,24,128]{2,1,0:T(8,128)(2,1)S(1)} async-done(((bf16[8,24,128]{2,1,0:T(8,128)(2,1)}), bf16[8,24,128]{2,1,0:T(8,128)(2,1)S(1)}, u32[]{:S(2)}, u32[]{:S(2)}) %all-to-all-start.3) | async-done | bytes 49184 | tf_op jit(solution)/shard_map/all_to_all | solution.py:319
  122.8 0.6 grad_reshare.1
  123.5 3.3 %all-to-all-start.4 = ((bf16[4,40,128]{2,1,0:T(8,128)(2,1)}), bf16[4,40,128]{2,1,0:T(8,128)(2,1)S(1)}, u32[]{:S(2)}, u32[]{:S(2)}) async-start(bf16[4,40,128]{2,1,0:T(8,128)(2,1)} %grad_reshare.1), calls=%async_computation.4 | async-start | bytes 81920 | tf_op jit(solution)/shard_map/all_to_all | solution.py:322
  126.8 0.0 collective-permute-done.2.rest_3_
  126.8 0.0 collective-permute-done.1.rest_2_
  126.8 0.0 collective-permute-done.rest_1_
  126.8 2.4 %backward_tiles.1.refs_1_ = bf16[16,128,128]{2,1,0:T(8,128)(2,1)S(1)} custom-call(s32[128]{0:T(128)S(1)} %bitcast.29, s32[128]{0:T(128)S(1)} %bitcast.27, s32[1]{0:T(128)} %bitcast.15.own_ref, bf16[128,128,128]{2,1,0:T(8,128)(2,1)} %build_back.1.tile_hbm, bf16[8,128,128]{2,1,0:T(8,128)(2,1)S(1)} %all-to-all-done.5.rest_0_, ...), custom_call_target="tpu_custom_call" | custom-call | tf_op jit(solution)/shard_map/backward_tiles/pallas_call | solution.py:237
  129.2 1.2 all-to-all-done.4.refs_0_
  130.4 0.6 grad_chunk.1
  131.0 24.2 %all_to_all.36.refs_0_ = bf16[16,144,128]{2,1,0:T(8,128)(2,1)S(1)} all-to-all(bf16[16,144,128]{2,1,0:T(8,128)(2,1)S(1)} %get-tuple-element.22), channel_id=1, replica_groups=mesh['ylo'=2,'zq'=8,'z0'=2,'x1'=2,'x0'=2,'d0'=4] {'x1','x0','d0'}, dimensions={0} | all-to-all | bytes 1179648 | tf_op jit(solution)/shard_map/all_to_all | solution.py:336
  155.2 0.7 final_sums.1
  (8 shorter events, 0.1 us)
Async XLA Ops:
  0.6 23.2 %copy-start.7 = (s32[1,1,128]{2,1,0:T(1,128)S(1)}, s32[1,1,128]{2,1,0:T(1,128)}, u32[]{:S(2)}) copy-start(s32[1,1,128]{2,1,0:T(1,128)} %param.12) | copy-start | bytes 1540
  0.6 23.1 %copy-start.8 = (s32[1,1,128]{2,1,0:T(1,128)S(1)}, s32[1,1,128]{2,1,0:T(1,128)}, u32[]{:S(2)}) copy-start(s32[1,1,128]{2,1,0:T(1,128)} %param.11) | copy-start | bytes 1540
  2.3 21.4 %all-to-all-start = ((bf16[16,128,128]{2,1,0:T(8,128)(2,1)}), bf16[16,128,128]{2,1,0:T(8,128)(2,1)S(1)}, u32[]{:S(2)}, u32[]{:S(2)}) async-start(bf16[16,128,128]{2,1,0:T(8,128)(2,1)} %feature_copies.1), calls=%async_computation | async-start | bytes 1048576 | tf_op jit(solution)/shard_map/all_to_all | solution.py:282
  12.6 0.8 copy-start
  13.3 0.7 copy-start.2
  14.1 0.7 copy-start.6
  23.8 32.0 %copy-start.1 = (s32[1,1,128,64]{2,3,1,0:T(8,128)S(1)}, s32[1,1,128,64]{2,3,1,0:T(8,128)}, u32[]{:S(2)}) copy-start(s32[1,1,128,64]{2,3,1,0:T(8,128)} %param.13) | copy-start | bytes 98308
  23.8 32.0 %copy-start.3 = (bf16[1,1,128,64]{2,3,1,0:T(8,128)(2,1)S(1)}, bf16[1,1,128,64]{2,3,1,0:T(8,128)(2,1)}, u32[]{:S(2)}) copy-start(bf16[1,1,128,64]{2,3,1,0:T(8,128)(2,1)} %param.14) | copy-start | bytes 49156
  26.2 47.0 %copy-start.4 = (bf16[128,256]{1,0:T(8,128)(2,1)S(1)}, bf16[128,256]{1,0:T(8,128)(2,1)}, u32[]{:S(2)}) copy-start(bf16[128,256]{1,0:T(8,128)(2,1)} %weight_ref.1) | copy-start | bytes 196612
  26.2 47.0 %copy-start.5 = (bf16[128,256]{1,0:T(8,128)(2,1)S(1)}, bf16[128,256]{1,0:T(8,128)(2,1)}, u32[]{:S(2)}) copy-start(bf16[128,256]{1,0:T(8,128)(2,1)} %grad_ref.1) | copy-start | bytes 196612
  26.2 47.0 %copy-start.9 = (f32[256]{0:T(256)S(1)}, f32[256]{0:T(256)}, u32[]{:S(2)}) copy-start(f32[256]{0:T(256)} %param.10) | copy-start | bytes 3076
  41.8 31.4 %all-to-all-start.2 = ((bf16[8,128,128]{2,1,0:T(8,128)(2,1)}), bf16[8,128,128]{2,1,0:T(8,128)(2,1)S(1)}, u32[]{:S(2)}, u32[]{:S(2)}) async-start(bf16[8,128,128]{2,1,0:T(8,128)(2,1)} %reduce_sum.24), calls=%async_computation.2 | async-start | bytes 524288 | tf_op jit(solution)/shard_map/all_to_all | solution.py:293
  74.3 25.4 %all-to-all-start.5 = ((bf16[8,128,128]{2,1,0:T(8,128)(2,1)}), bf16[8,128,128]{2,1,0:T(8,128)(2,1)S(1)}, u32[]{:S(2)}, u32[]{:S(2)}) async-start(bf16[8,128,128]{2,1,0:T(8,128)(2,1)} %get-tuple-element.21), calls=%async_computation.5 | async-start | bytes 524288 | tf_op jit(solution)/shard_map/all_to_all | solution.py:303
  99.7 23.1 %all-to-all-start.3 = ((bf16[8,24,128]{2,1,0:T(8,128)(2,1)}), bf16[8,24,128]{2,1,0:T(8,128)(2,1)S(1)}, u32[]{:S(2)}, u32[]{:S(2)}) async-start(bf16[8,24,128]{2,1,0:T(8,128)(2,1)} %grad_share.1), calls=%async_computation.3 | async-start | bytes 98304 | tf_op jit(solution)/shard_map/all_to_all | solution.py:319
  110.8 16.0 %collective-permute-start.2 = (bf16[8,128,128]{2,1,0:T(8,128)(2,1)S(1)}, bf16[8,128,128]{2,1,0:T(8,128)(2,1)S(1)}, u32[]{:S(2)}, u32[]{:S(2)}) collective-permute-start(bf16[8,128,128]{2,1,0:T(8,128)(2,1)S(1)} %all-to-all-done.5.rest_0_), channel_id=1, source_target_pairs={{0,272},{16,256},{256,16},{272,0},{1,273},{17,257},{257,17},{273,1... | collective-permute-start | bytes 786440 | tf_op jit(solution)/shard_map/ppermute | solution.py:249
  113.6 13.2 %collective-permute-start.1 = (bf16[8,128,128]{2,1,0:T(8,128)(2,1)S(1)}, bf16[8,128,128]{2,1,0:T(8,128)(2,1)S(1)}, u32[]{:S(2)}, u32[]{:S(2)}) collective-permute-start(bf16[8,128,128]{2,1,0:T(8,128)(2,1)S(1)} %all-to-all-done.5.rest_0_), channel_id=1, source_target_pairs={{0,256},{16,272},{256,0},{272,16},{1,257},{17,273},{257,1},{273,17... | collective-permute-start | bytes 786440 | tf_op jit(solution)/shard_map/ppermute | solution.py:249
  116.0 10.8 %collective-permute-start = (bf16[8,128,128]{2,1,0:T(8,128)(2,1)S(1)}, bf16[8,128,128]{2,1,0:T(8,128)(2,1)S(1)}, u32[]{:S(2)}, u32[]{:S(2)}) collective-permute-start(bf16[8,128,128]{2,1,0:T(8,128)(2,1)S(1)} %all-to-all-done.5.rest_0_), channel_id=1, source_target_pairs={{0,16},{16,0},{256,272},{272,256},{1,17},{17,1},{257,273},{273,257... | collective-permute-start | bytes 786440 | tf_op jit(solution)/shard_map/ppermute | solution.py:249
  123.5 6.9 %all-to-all-start.4 = ((bf16[4,40,128]{2,1,0:T(8,128)(2,1)}), bf16[4,40,128]{2,1,0:T(8,128)(2,1)S(1)}, u32[]{:S(2)}, u32[]{:S(2)}) async-start(bf16[4,40,128]{2,1,0:T(8,128)(2,1)} %grad_reshare.1), calls=%async_computation.4 | async-start | bytes 81920 | tf_op jit(solution)/shard_map/all_to_all | solution.py:322

commit v12 on v11

--- a/solution.py
+++ b/solution.py
@@ -173,10 +173,7 @@
     out_ref[:, TILE:, :] = jnp.broadcast_to(chunk[None], (out_ref.shape[0], size, TILE))
 
 
-def copies_kernel(rows_hbm, out_ref, rows_ref, sem):
-    copy = pltpu.make_async_copy(rows_hbm, rows_ref, sem)
-    copy.start()
-    copy.wait()
+def copies_kernel(rows_ref, out_ref):
     out_ref[...] = jnp.broadcast_to(rows_ref[...][None], out_ref.shape)
 
 
@@ -270,15 +267,7 @@
             tile_shape, (counts,), (positions, weights), pair_scratch,
         )
 
-    sent = pl.pallas_call(
-        copies_kernel,
-        out_shape=shape((dst,) + features.shape, BF16),
-        in_specs=[pl.BlockSpec(memory_space=pltpu.HBM)],
-        out_specs=vmem(1)[0],
-        scratch_shapes=[pltpu.VMEM(features.shape, BF16), pltpu.SemaphoreType.DMA(())],
-        compiler_params=pltpu.CompilerParams(vmem_limit_bytes=20 << 20),
-        name="feature_copies",
-    )(pltpu.with_memory_space_constraint(features, pltpu.HBM))
+    sent = call(copies_kernel, "feature_copies", shape((dst,) + features.shape, BF16), (), (features,))
     source_rows = lax.all_to_all(sent, DST, 0, 0, tiled=True)
     tiles = build(positions, False)
     tile_scratch = [pltpu.VMEM((slots, TILE, TILE), BF16), pltpu.SemaphoreType.DMA((slots // GROUP,))]

time: 156 us -> 156 us (level)
  waiting for transfers between devices: 18.3 us -> 16.6 us
    all_to_all x1, starting transfers between devices: 14 us -> 11.9 us  [body(): parts = lax.all_to_all(near_sums, FAR, 0, 0, tiled=True)]
    pallas_call x2, Pallas kernels: 4.77 us -> 6.69 us  [spread(): pl.pallas_call(kernel, out_shape=out, in_specs=smem(len(scalars)) + [pl.B...]
    pallas_call x1 -> x0, Pallas kernels: 1.68 us -> none  [body(): pl.pallas_call(copies_kernel, out_shape=shape((dst,) + features.shape, BF...]
    pallas_call x10 -> x11, Pallas kernels: 16.9 us -> 17.8 us  [call(): pl.pallas_call(kernel, out_shape=outs, in_specs=smem(len(scalars)) + vmem...]
where the time goes in v12:
time: 156 us
  blocking collectives  59.7 us (38%)
  starting transfers between devices  50.1 us (32%)
  Pallas kernels  24.5 us (16%)
  waiting for transfers between devices  16.6 us (11%)
  local copies, waits for them, and re-layouts  2.91 us (2%)
    all_to_all x1, blocking collectives, body(): received = lax.all_to_all(back_send, DST, 0, 0, tiled=True)  23.5 us
    pallas_call x11, Pallas kernels, call(): pl.pallas_call(kernel, out_shape=outs, in_specs=smem(len(scalars)) + vmem...  17.8 us
    all_to_all x1, blocking collectives, body(): near_parts = lax.all_to_all(partial, NEAR, 0, 0, tiled=True)  16.1 us
    all_to_all x1, starting transfers between devices, body(): parts = lax.all_to_all(near_sums, FAR, 0, 0, tiled=True)  11.9 us
    all_gather x1, blocking collectives, body(): part = lax.all_gather(part, 'd0')  11.3 us
    all_to_all x1, starting transfers between devices, body(): shared = lax.all_to_all(share, FAR, 0, 0, tiled=True)  11.1 us
    all_to_all x1, starting transfers between devices, body(): source_rows = lax.all_to_all(sent, DST, 0, 0, tiled=True)  10.2 us
    all_to_all x1, waiting for transfers between devices, body(): parts = lax.all_to_all(near_sums, FAR, 0, 0, tiled=True)  10.1 us
  transfers between devices with their start and end apart: 8, of which 4 were waited for; matrix products, arithmetic and copies ran while one was open for 0% of the time, Pallas kernels for 11%

profile of v12, /device:TPU:1, one launch (start us, length us, event | category | flops | bytes accessed | tf_op | source)
XLA Modules:
  0.0 155.5 jit_solution(9815976554677433998)
XLA Ops:
  0.6 0.0 copy-start.6
  0.6 0.7 copy-done.6
  1.4 0.9 feature_copies.1
  2.3 10.2 %all-to-all-start = ((bf16[16,128,128]{2,1,0:T(8,128)(2,1)}), bf16[16,128,128]{2,1,0:T(8,128)(2,1)S(1)}, u32[]{:S(2)}, u32[]{:S(2)}) async-start(bf16[16,128,128]{2,1,0:T(8,128)(2,1)} %feature_copies.1), calls=%async_computation | async-start | bytes 1048576 | tf_op jit(solution)/shard_map/all_to_all | solution.py:271
  12.5 0.8 copy-done
  13.3 0.7 copy-done.2
  14.0 0.7 copy-done.7
  14.7 6.5 %build_tiles.1.tile_hbm = bf16[128,128,128]{2,1,0:T(8,128)(2,1)} custom-call(s32[128]{0:T(128)S(1)} %bitcast.24, s32[64,128]{1,0:T(8,128)S(1)} %bitcast.20, bf16[64,128]{1,0:T(8,128)(2,1)S(1)} %bitcast.22), custom_call_target="tpu_custom_call" | custom-call | tf_op jit(solution)/shard_map/build_tiles/pallas_call | solution.py:217
  21.2 2.6 %all-to-all-done.rows_ref = bf16[16,128,128]{2,1,0:T(8,128)(2,1)S(1)} async-done(((bf16[16,128,128]{2,1,0:T(8,128)(2,1)}), bf16[16,128,128]{2,1,0:T(8,128)(2,1)S(1)}, u32[]{:S(2)}, u32[]{:S(2)}) %all-to-all-start) | async-done | bytes 524320 | tf_op jit(solution)/shard_map/all_to_all | solution.py:271
  23.7 0.0 copy-done.8
  23.7 0.0 copy-done.9
  23.7 3.4 %forward_tiles.1 = bf16[4,8,128,128]{3,2,1,0:T(8,128)(2,1)S(1)} custom-call(s32[128]{0:T(128)S(1)} %bitcast.28, s32[128]{0:T(128)S(1)} %bitcast.25, bf16[128,128,128]{2,1,0:T(8,128)(2,1)} %build_tiles.1.tile_hbm, bf16[16,128,128]{2,1,0:T(8,128)(2,1)S(1)} %all-to-all-done.rows_ref), custom_call_target="tpu_custom_call" | custom-call | tf_op jit(solution)/shard_map/forward_tiles/pallas_call | solution.py:234
  27.1 0.0 copy-start.4
  27.1 0.0 copy-start.5
  27.1 0.0 copy-start.10
  27.2 16.1 %all_to_all.35 = bf16[4,8,128,128]{3,2,1,0:T(8,128)(2,1)S(1)} all-to-all(bf16[4,8,128,128]{3,2,1,0:T(8,128)(2,1)S(1)} %forward_tiles.1), channel_id=1, replica_groups=mesh['ylo'=2,'zq'=8,'z0'=2,'x1'=2,'x0'=2,'d0'=4] {'ylo','z0'}, dimensions={0} | all-to-all | bytes 2097152 | tf_op jit(solution)/shard_map/all_to_all | solution.py:278
  43.2 0.9 reduce_sum.24
  44.2 11.9 %all-to-all-start.2 = ((bf16[8,128,128]{2,1,0:T(8,128)(2,1)}), bf16[8,128,128]{2,1,0:T(8,128)(2,1)S(1)}, u32[]{:S(2)}, u32[]{:S(2)}) async-start(bf16[8,128,128]{2,1,0:T(8,128)(2,1)} %reduce_sum.24), calls=%async_computation.2 | async-start | bytes 524288 | tf_op jit(solution)/shard_map/all_to_all | solution.py:282
  56.1 0.0 copy-done.1
  56.1 0.0 copy-done.3
  56.1 6.5 %build_back.1.tile_hbm = bf16[128,128,128]{2,1,0:T(8,128)(2,1)} custom-call(s32[128]{0:T(128)S(1)} %bitcast.26, s32[64,128]{1,0:T(8,128)S(1)} %bitcast.21, bf16[64,128]{1,0:T(8,128)(2,1)S(1)} %bitcast.23), custom_call_target="tpu_custom_call" | custom-call | tf_op jit(solution)/shard_map/build_back/pallas_call | solution.py:217
  62.6 10.1 %all-to-all-done.2 = bf16[8,128,128]{2,1,0:T(8,128)(2,1)S(1)} async-done(((bf16[8,128,128]{2,1,0:T(8,128)(2,1)}), bf16[8,128,128]{2,1,0:T(8,128)(2,1)S(1)}, u32[]{:S(2)}, u32[]{:S(2)}) %all-to-all-start.2) | async-done | bytes 262176 | tf_op jit(solution)/shard_map/all_to_all | solution.py:282
  72.8 0.0 copy-done.4
  72.8 0.0 copy-done.5
  72.8 0.0 copy-done.10
  72.8 1.1 dense_layer.1
  73.9 5.2 %all-to-all-start.5 = ((bf16[8,128,128]{2,1,0:T(8,128)(2,1)}), bf16[8,128,128]{2,1,0:T(8,128)(2,1)S(1)}, u32[]{:S(2)}, u32[]{:S(2)}) async-start(bf16[8,128,128]{2,1,0:T(8,128)(2,1)} %get-tuple-element.21), calls=%async_computation.5 | async-start | bytes 524288 | tf_op jit(solution)/shard_map/all_to_all | solution.py:292
  79.1 0.2 grad_part.1
  79.3 11.3 %all-gather = bf16[1056,128]{1,0:T(8,128)(2,1)S(1)} all-gather(bf16[264,128]{1,0:T(8,128)(2,1)S(1)} %grad_part.1), channel_id=2, replica_groups=mesh['ylo'=2,'zq'=8,'z0'=2,'x1'=2,'x0'=2,'d0'=4] {'d0'}, dimensions={0}, use_global_device_ids=true | all-gather | bytes 337920 | tf_op jit(solution)/shard_map/all_gather | solution.py:295
  90.6 5.3 %all-gather.1 = f32[144,128]{1,0:T(8,128)S(1)} all-gather(f32[72,128]{1,0:T(8,128)S(1)} %grad_pick.1), channel_id=3, replica_groups=mesh['ylo'=2,'zq'=8,'z0'=2,'x1'=2,'x0'=2,'d0'=4] {'x1'}, dimensions={0}, use_global_device_ids=true | all-gather | bytes 110592 | tf_op jit(solution)/shard_map/all_gather | solution.py:299
  95.9 3.6 %all-gather.2 = f32[80,128]{1,0:T(8,128)S(1)} all-gather(f32[40,128]{1,0:T(8,128)S(1)} %grad_half.1), channel_id=4, replica_groups=mesh['ylo'=2,'zq'=8,'z0'=2,'x1'=2,'x0'=2,'d0'=4] {'x0'}, dimensions={0}, use_global_device_ids=true | all-gather | bytes 61440 | tf_op jit(solution)/shard_map/all_gather | solution.py:303
  99.5 0.6 grad_share.1
  100.1 0.0 all-to-all-done.5.rest_0_
  100.1 11.1 %all-to-all-start.3 = ((bf16[8,24,128]{2,1,0:T(8,128)(2,1)}), bf16[8,24,128]{2,1,0:T(8,128)(2,1)S(1)}, u32[]{:S(2)}, u32[]{:S(2)}) async-start(bf16[8,24,128]{2,1,0:T(8,128)(2,1)} %grad_share.1), calls=%async_computation.3 | async-start | bytes 98304 | tf_op jit(solution)/shard_map/all_to_all | solution.py:308
  111.2 2.4 %collective-permute-start.2 = (bf16[8,128,128]{2,1,0:T(8,128)(2,1)S(1)}, bf16[8,128,128]{2,1,0:T(8,128)(2,1)S(1)}, u32[]{:S(2)}, u32[]{:S(2)}) collective-permute-start(bf16[8,128,128]{2,1,0:T(8,128)(2,1)S(1)} %all-to-all-done.5.rest_0_), channel_id=1, source_target_pairs={{0,272},{16,256},{256,16},{272,0},{1,273},{17,257},{257,17},{273,1... | collective-permute-start | bytes 786440 | tf_op jit(solution)/shard_map/ppermute | solution.py:246
  113.5 2.8 %collective-permute-start.1 = (bf16[8,128,128]{2,1,0:T(8,128)(2,1)S(1)}, bf16[8,128,128]{2,1,0:T(8,128)(2,1)S(1)}, u32[]{:S(2)}, u32[]{:S(2)}) collective-permute-start(bf16[8,128,128]{2,1,0:T(8,128)(2,1)S(1)} %all-to-all-done.5.rest_0_), channel_id=1, source_target_pairs={{0,256},{16,272},{256,0},{272,16},{1,257},{17,273},{257,1},{273,17... | collective-permute-start | bytes 786440 | tf_op jit(solution)/shard_map/ppermute | solution.py:246
  116.3 3.2 %collective-permute-start = (bf16[8,128,128]{2,1,0:T(8,128)(2,1)S(1)}, bf16[8,128,128]{2,1,0:T(8,128)(2,1)S(1)}, u32[]{:S(2)}, u32[]{:S(2)}) collective-permute-start(bf16[8,128,128]{2,1,0:T(8,128)(2,1)S(1)} %all-to-all-done.5.rest_0_), channel_id=1, source_target_pairs={{0,16},{16,0},{256,272},{272,256},{1,17},{17,1},{257,273},{273,257... | collective-permute-start | bytes 786440 | tf_op jit(solution)/shard_map/ppermute | solution.py:246
  119.5 3.7 %all-to-all-done.3.recv_ref = bf16[8,24,128]{2,1,0:T(8,128)(2,1)S(1)} async-done(((bf16[8,24,128]{2,1,0:T(8,128)(2,1)}), bf16[8,24,128]{2,1,0:T(8,128)(2,1)S(1)}, u32[]{:S(2)}, u32[]{:S(2)}) %all-to-all-start.3) | async-done | bytes 49184 | tf_op jit(solution)/shard_map/all_to_all | solution.py:308
  123.2 0.6 grad_reshare.1
  123.9 3.3 %all-to-all-start.4 = ((bf16[4,40,128]{2,1,0:T(8,128)(2,1)}), bf16[4,40,128]{2,1,0:T(8,128)(2,1)S(1)}, u32[]{:S(2)}, u32[]{:S(2)}) async-start(bf16[4,40,128]{2,1,0:T(8,128)(2,1)} %grad_reshare.1), calls=%async_computation.4 | async-start | bytes 81920 | tf_op jit(solution)/shard_map/all_to_all | solution.py:311
  127.1 0.0 collective-permute-done.2.rest_3_
  127.2 0.0 collective-permute-done.1.rest_2_
  127.2 0.0 collective-permute-done.rest_1_
  127.2 3.3 %backward_tiles.1.refs_1_ = bf16[16,128,128]{2,1,0:T(8,128)(2,1)S(1)} custom-call(s32[128]{0:T(128)S(1)} %bitcast.29, s32[128]{0:T(128)S(1)} %bitcast.27, s32[1]{0:T(128)} %bitcast.15.own_ref, bf16[128,128,128]{2,1,0:T(8,128)(2,1)} %build_back.1.tile_hbm, bf16[8,128,128]{2,1,0:T(8,128)(2,1)S(1)} %all-to-all-done.5.rest_0_, ...), custom_call_target="tpu_custom_call" | custom-call | tf_op jit(solution)/shard_map/backward_tiles/pallas_call | solution.py:234
  130.5 0.2 all-to-all-done.4.refs_0_
  130.7 0.6 grad_chunk.1
  131.3 23.5 %all_to_all.36.refs_0_ = bf16[16,144,128]{2,1,0:T(8,128)(2,1)S(1)} all-to-all(bf16[16,144,128]{2,1,0:T(8,128)(2,1)S(1)} %get-tuple-element.22), channel_id=1, replica_groups=mesh['ylo'=2,'zq'=8,'z0'=2,'x1'=2,'x0'=2,'d0'=4] {'x1','x0','d0'}, dimensions={0} | all-to-all | bytes 1179648 | tf_op jit(solution)/shard_map/all_to_all | solution.py:325
  154.8 0.7 final_sums.1
  (10 shorter events, 0.1 us)
Async XLA Ops:
  0.6 0.8 copy-start.6
  1.4 22.3 %copy-start.8 = (s32[1,1,128]{2,1,0:T(1,128)S(1)}, s32[1,1,128]{2,1,0:T(1,128)}, u32[]{:S(2)}) copy-start(s32[1,1,128]{2,1,0:T(1,128)} %param.12) | copy-start | bytes 1540
  1.4 22.3 %copy-start.9 = (s32[1,1,128]{2,1,0:T(1,128)S(1)}, s32[1,1,128]{2,1,0:T(1,128)}, u32[]{:S(2)}) copy-start(s32[1,1,128]{2,1,0:T(1,128)} %param.11) | copy-start | bytes 1540
  2.3 21.4 %all-to-all-start = ((bf16[16,128,128]{2,1,0:T(8,128)(2,1)}), bf16[16,128,128]{2,1,0:T(8,128)(2,1)S(1)}, u32[]{:S(2)}, u32[]{:S(2)}) async-start(bf16[16,128,128]{2,1,0:T(8,128)(2,1)} %feature_copies.1), calls=%async_computation | async-start | bytes 1048576 | tf_op jit(solution)/shard_map/all_to_all | solution.py:271
  12.5 0.8 copy-start
  13.3 0.7 copy-start.2
  14.0 0.7 copy-start.7
  23.7 32.4 %copy-start.1 = (s32[1,1,128,64]{2,3,1,0:T(8,128)S(1)}, s32[1,1,128,64]{2,3,1,0:T(8,128)}, u32[]{:S(2)}) copy-start(s32[1,1,128,64]{2,3,1,0:T(8,128)} %param.13) | copy-start | bytes 98308
  23.7 32.4 %copy-start.3 = (bf16[1,1,128,64]{2,3,1,0:T(8,128)(2,1)S(1)}, bf16[1,1,128,64]{2,3,1,0:T(8,128)(2,1)}, u32[]{:S(2)}) copy-start(bf16[1,1,128,64]{2,3,1,0:T(8,128)(2,1)} %param.14) | copy-start | bytes 49156
  27.1 45.7 %copy-start.4 = (bf16[128,256]{1,0:T(8,128)(2,1)S(1)}, bf16[128,256]{1,0:T(8,128)(2,1)}, u32[]{:S(2)}) copy-start(bf16[128,256]{1,0:T(8,128)(2,1)} %weight_ref.1) | copy-start | bytes 196612
  27.1 45.7 %copy-start.5 = (bf16[128,256]{1,0:T(8,128)(2,1)S(1)}, bf16[128,256]{1,0:T(8,128)(2,1)}, u32[]{:S(2)}) copy-start(bf16[128,256]{1,0:T(8,128)(2,1)} %grad_ref.1) | copy-start | bytes 196612
  27.1 45.7 %copy-start.10 = (f32[256]{0:T(256)S(1)}, f32[256]{0:T(256)}, u32[]{:S(2)}) copy-start(f32[256]{0:T(256)} %param.10) | copy-start | bytes 3076
  44.2 28.6 %all-to-all-start.2 = ((bf16[8,128,128]{2,1,0:T(8,128)(2,1)}), bf16[8,128,128]{2,1,0:T(8,128)(2,1)S(1)}, u32[]{:S(2)}, u32[]{:S(2)}) async-start(bf16[8,128,128]{2,1,0:T(8,128)(2,1)} %reduce_sum.24), calls=%async_computation.2 | async-start | bytes 524288 | tf_op jit(solution)/shard_map/all_to_all | solution.py:282
  73.9 26.3 %all-to-all-start.5 = ((bf16[8,128,128]{2,1,0:T(8,128)(2,1)}), bf16[8,128,128]{2,1,0:T(8,128)(2,1)S(1)}, u32[]{:S(2)}, u32[]{:S(2)}) async-start(bf16[8,128,128]{2,1,0:T(8,128)(2,1)} %get-tuple-element.21), calls=%async_computation.5 | async-start | bytes 524288 | tf_op jit(solution)/shard_map/all_to_all | solution.py:292
  100.1 23.1 %all-to-all-start.3 = ((bf16[8,24,128]{2,1,0:T(8,128)(2,1)}), bf16[8,24,128]{2,1,0:T(8,128)(2,1)S(1)}, u32[]{:S(2)}, u32[]{:S(2)}) async-start(bf16[8,24,128]{2,1,0:T(8,128)(2,1)} %grad_share.1), calls=%async_computation.3 | async-start | bytes 98304 | tf_op jit(solution)/shard_map/all_to_all | solution.py:308
  111.2 16.0 %collective-permute-start.2 = (bf16[8,128,128]{2,1,0:T(8,128)(2,1)S(1)}, bf16[8,128,128]{2,1,0:T(8,128)(2,1)S(1)}, u32[]{:S(2)}, u32[]{:S(2)}) collective-permute-start(bf16[8,128,128]{2,1,0:T(8,128)(2,1)S(1)} %all-to-all-done.5.rest_0_), channel_id=1, source_target_pairs={{0,272},{16,256},{256,16},{272,0},{1,273},{17,257},{257,17},{273,1... | collective-permute-start | bytes 786440 | tf_op jit(solution)/shard_map/ppermute | solution.py:246
  113.5 13.6 %collective-permute-start.1 = (bf16[8,128,128]{2,1,0:T(8,128)(2,1)S(1)}, bf16[8,128,128]{2,1,0:T(8,128)(2,1)S(1)}, u32[]{:S(2)}, u32[]{:S(2)}) collective-permute-start(bf16[8,128,128]{2,1,0:T(8,128)(2,1)S(1)} %all-to-all-done.5.rest_0_), channel_id=1, source_target_pairs={{0,256},{16,272},{256,0},{272,16},{1,257},{17,273},{257,1},{273,17... | collective-permute-start | bytes 786440 | tf_op jit(solution)/shard_map/ppermute | solution.py:246
  116.3 10.8 %collective-permute-start = (bf16[8,128,128]{2,1,0:T(8,128)(2,1)S(1)}, bf16[8,128,128]{2,1,0:T(8,128)(2,1)S(1)}, u32[]{:S(2)}, u32[]{:S(2)}) collective-permute-start(bf16[8,128,128]{2,1,0:T(8,128)(2,1)S(1)} %all-to-all-done.5.rest_0_), channel_id=1, source_target_pairs={{0,16},{16,0},{256,272},{272,256},{1,17},{17,1},{257,273},{273,257... | collective-permute-start | bytes 786440 | tf_op jit(solution)/shard_map/ppermute | solution.py:246
  123.9 6.9 %all-to-all-start.4 = ((bf16[4,40,128]{2,1,0:T(8,128)(2,1)}), bf16[4,40,128]{2,1,0:T(8,128)(2,1)S(1)}, u32[]{:S(2)}, u32[]{:S(2)}) async-start(bf16[4,40,128]{2,1,0:T(8,128)(2,1)} %grad_reshare.1), calls=%async_computation.4 | async-start | bytes 81920 | tf_op jit(solution)/shard_map/all_to_all | solution.py:311
